TPU v7x, 32 devices: a whole 2x2x4 slice. The times are simulated.
32 devices in a mesh: batch: 2 (over core), ctx: 4 (over z), tensor: 4 (over y, x).
Axes of the slice: x: 2, y: 2, z: 4, core: 2. Of those that a mesh axis runs over, the one named last changes fastest.
Arguments:
- hidden_in: bfloat16 [2, 2, 512, 2048], P(None, 'batch', 'ctx'), may hold values from -6 to 6
- segment_ids: int32 [2, 2, 512], P(None, 'batch', 'ctx'), may hold values from 0 to 3, never falling along the last dimension, each value on 1 to 256 neighbouring positions
- expert_ids: int32 [2, 2, 512, 8], P(None, 'batch', 'ctx'), may hold values from 0 to 31, as said below
- capacity: int32 [32], replicated, may hold values from 128 to 320, as said below
- norm_attn: float32 [2048], replicated, may hold values from 0.25 to 1.75
- norm_ffn: float32 [2048], replicated, may hold values from 0.25 to 1.75
- norm_query: float32 [128], replicated, may hold values from 0.25 to 1.75
- norm_key: float32 [128], replicated, may hold values from 0.25 to 1.75
- w_query: bfloat16 [2048, 4096], P(('batch', 'ctx'), 'tensor'), may hold values from -0.125 to 0.125
- w_key: bfloat16 [2048, 512], P(('batch', 'ctx'), 'tensor'), may hold values from -0.125 to 0.125
- w_value: bfloat16 [2048, 512], P(('batch', 'ctx'), 'tensor'), may hold values from -0.125 to 0.125
- w_out: bfloat16 [2048, 4096], P(('batch', 'ctx'), 'tensor'), may hold values from -0.75 to 0.75
- w_router: bfloat16 [2048, 32], P(('batch', 'ctx')), may hold values from -0.0625 to 0.0625
- w_gate: bfloat16 [32, 768, 2048], P(('batch', 'ctx'), 'tensor'), may hold values from -0.125 to 0.125
- w_up: bfloat16 [32, 768, 2048], P(('batch', 'ctx'), 'tensor'), may hold values from -0.125 to 0.125
- w_down: bfloat16 [32, 768, 2048], P(('batch', 'ctx'), 'tensor'), may hold values from -1.25 to 1.25
- grad_out: bfloat16 [2, 2, 512, 2048], P(None, 'batch', 'ctx'), may hold values from -6 to 6
Outputs:
- hidden_out: float32 [2, 2, 512, 2048], P(None, 'batch', 'ctx')
- grad_in: float32 [2, 2, 512, 2048], P(None, 'batch', 'ctx')
- grad_norm_attn: float32 [2048], P(('batch', 'ctx'))
- grad_norm_ffn: float32 [2048], P(('batch', 'ctx'))
- grad_norm_query: float32 [128], P(('batch', 'ctx'))
- grad_norm_key: float32 [128], P(('batch', 'ctx'))
- grad_query: float32 [2048, 4096], P(('batch', 'ctx'), 'tensor')
- grad_key: float32 [2048, 512], P(('batch', 'ctx'), 'tensor')
- grad_value: float32 [2048, 512], P(('batch', 'ctx'), 'tensor')
- grad_out_proj: float32 [2048, 4096], P(('batch', 'ctx'), 'tensor')
- grad_router: float32 [2048, 32], P(('batch', 'ctx'))
- grad_gate: float32 [32, 768, 2048], P(('batch', 'ctx'), 'tensor')
- grad_up: float32 [32, 768, 2048], P(('batch', 'ctx'), 'tensor')
- grad_down: float32 [32, 768, 2048], P(('batch', 'ctx'), 'tensor')
Inputs may be any that keep to these rules, and one draw needn't show every extreme that they name: `expert_ids`: each row names 8 different experts; among the 128 rows of one device of one micro-batch a quarter of the experts are named exactly 64 times, a quarter exactly 64 / 2 times and the rest exactly 64 / 4 times. `segment_ids`: ids never fall along a sequence; a document holds at most 256 tokens. `capacity`: the most pairs of one micro-batch that an expert keeps.
All inputs are finite; a program needn't handle non-finite values.
Results may differ from a plain program's by a relative error of at most 0.028.
Values may be sent and summed in bfloat16 or wider, within the bound.
No kernel may reach another device: no remote copies, remote signals or barrier semaphores. Data moves between devices by JAX's collectives and lax.ppermute only.
A program may use at most 320 MiB of HBM per device.

v0:
```python
import jax
import jax.numpy as jnp
from jax import lax
from jax.sharding import PartitionSpec as P

B, C, T = "batch", "ctx", "tensor"
BC = (B, C)
ALL = (B, C, T)
f32 = jnp.float32
bf16 = jnp.bfloat16
EPS = 1e-06


def dot(a, b, ca, cb):
    return lax.dot_general(a, b, (((ca,), (cb,)), ((), ())), preferred_element_type=f32)


def nn(a, b):
    return dot(a, b, 1, 0)


def nt(a, b):
    return dot(a, b, 1, 1)


def tn(a, b):
    return dot(a, b, 0, 0)


def bdot(a, b, ca, cb):
    return lax.dot_general(a, b, (((ca,), (cb,)), ((0,), (0,))), preferred_element_type=f32)


def pad_cols(v, width):
    return jnp.pad(v, ((0, 0), (0, width - v.shape[1])))


def inv_rms(v):
    return lax.rsqrt(jnp.mean(v * v, axis=-1, keepdims=True) + EPS)


def turn(v):
    half = v.shape[-1] // 2
    return jnp.concatenate([-v[..., half:], v[..., :half]], axis=-1)


def angles(positions, width):
    half = width // 2
    frequency = jnp.power(1000000.0, -(2.0 * jnp.arange(half, dtype=f32)) / width)
    phases = positions.astype(f32)[:, None] * frequency[None, :]
    phases = jnp.concatenate([phases, phases], axis=-1)
    return jnp.cos(phases), jnp.sin(phases)


def norm_back(v, r, gain, grad):
    scaled = gain * grad
    grad_v = r * scaled - v * (r * r * r) * jnp.mean(v * scaled, axis=-1, keepdims=True)
    return grad_v, grad * v * r


def heads_forward(raw, gain, cosine, sine):
    v = raw * inv_rms(raw) * gain
    return (v * cosine + turn(v) * sine).astype(bf16)


def heads_back(raw, gain, cosine, sine, grad):
    grad = grad * cosine - turn(grad) * sine
    return norm_back(raw, inv_rms(raw), gain, grad)


def gather_t(v):
    count = lax.axis_size(T)
    return lax.all_to_all(jnp.concatenate([v] * count, axis=0), T, 0, 0, tiled=True)


def sum_t(v):
    count = lax.axis_size(T)
    got = lax.all_to_all(v.astype(bf16), T, 0, 0, tiled=True)
    got = got.reshape(count, v.shape[0] // count, v.shape[1])
    return jnp.sum(got.astype(f32), axis=0)


def sum_all(v):
    width = v.shape[1]
    halves = v.reshape(2, -1, width)
    me = lax.axis_index(B)
    other = lax.ppermute(lax.dynamic_index_in_dim(halves, 1 - me, 0, False), B, [(0, 1), (1, 0)])
    own = lax.dynamic_index_in_dim(halves, me, 0, False)
    chip = (own.astype(f32) + other.astype(f32)).astype(bf16)
    plane = sum_t(chip).astype(bf16)
    count = lax.axis_size(C)
    got = lax.all_to_all(plane, C, 0, 0, tiled=True)
    got = got.reshape(count, plane.shape[0] // count, width)
    return jnp.sum(got.astype(f32), axis=0)


def to_features(v):
    return lax.all_to_all(v, BC, 1, 0, tiled=True)


def body(
    hidden_in,
    segment_ids,
    expert_ids,
    capacity,
    norm_attn,
    norm_ffn,
    norm_query,
    norm_key,
    w_query,
    w_key,
    w_value,
    w_out,
    w_router,
    w_gate,
    w_up,
    w_down,
    grad_out,
):
    micro, _, span, width = hidden_in.shape
    rows = micro * span
    hd = norm_query.shape[0]
    topk = expert_ids.shape[3]
    experts = w_router.shape[1]
    mine = w_gate.shape[0]
    nb, nc, nt_ = lax.axis_size(B), lax.axis_size(C), lax.axis_size(T)
    sources = nb * nc
    cut = rows // nt_
    b, c, t = lax.axis_index(B), lax.axis_index(C), lax.axis_index(T)
    place = b * nc + c
    seq = span * nc
    back = (seq // 2 - 1 + span - 1) // span
    heads = w_query.shape[1] // hd
    q_cols = heads * hd
    scale = hd ** (-0.5)
    routed = -(-experts // 128) * 128

    x = hidden_in.reshape(rows, width)
    dy = grad_out.reshape(rows, width)

    w_qkv = lax.all_gather(
        jnp.concatenate([w_query, w_key, w_value], axis=1), BC, axis=0, tiled=True
    )
    w_or = lax.all_gather(
        jnp.concatenate([w_out, pad_cols(w_router, routed)], axis=1), BC, axis=0, tiled=True
    )
    out_w = w_or[:, :q_cols]
    router_w = w_or[:, q_cols : q_cols + experts]

    ids_own = expert_ids.reshape(rows, topk).T
    info = jnp.concatenate([ids_own, segment_ids.reshape(1, rows)], axis=0)
    info = jnp.pad(info, ((0, -(-(topk + 1) // 8) * 8 - topk - 1), (0, 0)))
    tall = info.shape[0]
    info = lax.all_to_all(jnp.concatenate([info] * sources, axis=0), BC, 0, 0, tiled=True)
    info = info.reshape(sources, tall, rows)
    ids_all = info[:, :topk]
    seg_all = info[:, topk].reshape(nb, nc, micro, span)
    local = place * mine + jnp.arange(mine)
    hot = jnp.sum((ids_all[:, :, None, :] == local[None, None, :, None]).astype(f32), axis=1)
    hot = hot.reshape(sources, mine, micro, span)
    upper = (jnp.arange(span)[:, None] < jnp.arange(span)[None, :]).astype(bf16)
    within = nn(hot.astype(bf16).reshape(-1, span), upper).reshape(hot.shape)
    totals = jnp.sum(hot, axis=-1)
    earlier = jnp.arange(sources)[:, None] < jnp.arange(sources)[None, :]
    before = jnp.sum(jnp.where(earlier[:, :, None, None], totals[:, None], 0.0), axis=0)
    rank = within + before[..., None]
    room = lax.dynamic_slice(capacity, (place * mine,), (mine,)).astype(f32)
    kept = jnp.where(rank < room[None, :, None, None], hot, 0.0)
    kept = kept.reshape(nb, nc, mine, nt_, cut).transpose(0, 3, 1, 4, 2).reshape(-1, mine)
    ids_rows = ids_all.reshape(nb, nc, topk, nt_, cut).transpose(0, 3, 1, 4, 2).reshape(-1, topk)
    names = jnp.arange(experts)
    chosen_all = jnp.sum((ids_rows[:, :, None] == names).astype(f32), axis=1)
    ids_slice = lax.dynamic_slice(expert_ids.reshape(rows, topk), (t * cut, 0), (cut, topk))
    chosen = jnp.sum((ids_slice[:, :, None] == names).astype(f32), axis=1)

    xf = x.astype(f32)
    act1 = (xf * inv_rms(xf) * norm_attn).astype(bf16)
    act1_cols = to_features(act1)
    dy_slice = lax.dynamic_slice(dy, (t * cut, 0), (cut, width))
    dy_all = lax.all_gather(dy_slice, (B, T, C), axis=0, tiled=True)
    qkv = nn(act1, w_qkv)
    positions = c * span + jnp.arange(span)
    cosine, sine = angles(positions, hd)
    cosine = jnp.concatenate([cosine] * micro, axis=0)
    sine = jnp.concatenate([sine] * micro, axis=0)
    q_raw = qkv[:, :q_cols].reshape(rows, heads, hd)
    k_raw = qkv[:, q_cols : q_cols + hd]
    q = heads_forward(q_raw, norm_query, cosine[:, None], sine[:, None])
    k = heads_forward(k_raw, norm_key, cosine, sine)
    kv = jnp.concatenate([k, qkv[:, q_cols + hd :].astype(bf16)], axis=1)
    blocks = [
        lax.ppermute(kv, C, [(i, i + s) for i in range(nc - s)]) for s in range(back, 0, -1)
    ]
    window = jnp.stack(blocks + [kv]).reshape(back + 1, micro, span, 2 * hd)
    window = window.transpose(1, 0, 2, 3).reshape(micro, (back + 1) * span, 2 * hd)
    keys, values = window[..., :hd], window[..., hd:]
    seg_seq = lax.dynamic_index_in_dim(seg_all, b, 0, False)
    seg_seq = jnp.pad(seg_seq, ((back, 0), (0, 0), (0, 0)), constant_values=-1)
    seg_win = lax.dynamic_slice(seg_seq, (c, 0, 0), (back + 1, micro, span))
    seg_win = seg_win.transpose(1, 0, 2).reshape(micro, -1)
    seg_own = segment_ids.reshape(micro, span)
    allowed = (seg_own[:, :, None] == seg_win[:, None, :]) & (
        jnp.arange((back + 1) * span)[None, None, :] <= back * span + jnp.arange(span)[None, :, None]
    )
    qg = q.reshape(micro, span, heads, hd).transpose(0, 2, 1, 3)
    qg = qg.reshape(micro, heads * span, hd)
    scores = bdot(qg, keys, 2, 2).reshape(micro, heads, span, -1) * scale
    scores = jnp.where(allowed[:, None], scores, -1e30)
    top = jnp.max(scores, axis=-1, keepdims=True)
    weight = jnp.exp(scores - top)
    total = jnp.sum(weight, axis=-1, keepdims=True)
    probs = weight / total
    log_total = top + jnp.log(total)
    probs_low = probs.astype(bf16).reshape(micro, heads * span, -1)
    mixed = bdot(probs_low, values, 2, 1).astype(bf16).reshape(micro, heads, span, hd)
    mixed = mixed.transpose(0, 2, 1, 3).reshape(rows, q_cols)
    branch = sum_t(nt(mixed, out_w))
    x_slice = lax.dynamic_slice(x, (t * cut, 0), (cut, width)).astype(f32)
    middle = x_slice + branch
    r2 = inv_rms(middle)
    act2 = (middle * r2 * norm_ffn).astype(bf16)
    act2_all = lax.all_gather(act2, (B, T, C), axis=0, tiled=True)
    mixed_later, act2_all = lax.optimization_barrier((mixed, act2_all))
    mixed_all = lax.all_gather(mixed_later, BC, axis=0, tiled=True)

    logits_all = nn(act2_all, router_w)
    shifted = jnp.exp(logits_all - jnp.max(logits_all, axis=-1, keepdims=True)) * chosen_all
    gates_all = shifted / jnp.sum(shifted, axis=-1, keepdims=True)
    gates = lax.dynamic_slice(gates_all, (0, place * mine), (gates_all.shape[0], mine)) * kept
    hidden = mine * w_gate.shape[1]
    gate_w = w_gate.reshape(hidden, width)
    up_w = w_up.reshape(hidden, width)
    down_w = w_down.reshape(hidden, width)
    owner = jnp.arange(hidden)[None, :] // w_gate.shape[1]

    def spread(v):
        wide = jnp.where(owner == 0, v[:, 0:1], 0.0)
        for e in range(1, mine):
            wide = jnp.where(owner == e, v[:, e : e + 1], wide)
        return wide

    dy_down = nt(dy_all, down_w)
    gate_pre = nt(act2_all, gate_w)
    up_pre = nt(act2_all, up_w)
    sig = jax.nn.sigmoid(gate_pre)
    silu = gate_pre * sig
    gates_wide = spread(gates)
    hid = silu * up_pre
    hid_gated = (gates_wide * hid).astype(bf16)
    agree = hid * dy_down
    d_gates = jnp.stack(
        [jnp.sum(jnp.where(owner == e, agree, 0.0), axis=1) for e in range(mine)], axis=1
    )
    d_gates = jnp.where(kept > 0.0, d_gates, 0.0)
    d_hid = gates_wide * dy_down
    d_gate = (d_hid * up_pre * sig * (1.0 + gate_pre * (1.0 - sig))).astype(bf16)
    d_up = (d_hid * silu).astype(bf16)
    d_in = (nn(d_gate, gate_w) + nn(d_up, up_w)).astype(bf16)
    d_gates_wide = lax.dynamic_update_slice(
        jnp.zeros((d_in.shape[0], routed), bf16), d_gates.astype(bf16), (0, place * mine)
    )
    d_in_sum = sum_all(jnp.concatenate([d_in, d_gates_wide], axis=1))
    out_part = nn(hid_gated, down_w).astype(bf16)
    grad_down = tn(hid_gated, dy_all).reshape(w_down.shape)
    grad_gate = tn(d_gate, act2_all).reshape(w_gate.shape)
    grad_up = tn(d_up, act2_all).reshape(w_up.shape)

    d_gates_slice = d_in_sum[:, width : width + experts]
    logits = nn(act2, router_w)
    probs_r = jax.nn.softmax(logits, axis=-1)
    picked = probs_r * chosen
    picked_sum = jnp.sum(picked, axis=-1, keepdims=True)
    gates_slice = picked / picked_sum
    lean = jnp.sum(d_gates_slice * gates_slice, axis=-1, keepdims=True)
    c_grad = chosen * (d_gates_slice - lean) / picked_sum
    d_logits = probs_r * (c_grad - jnp.sum(probs_r * c_grad, axis=-1, keepdims=True))
    d_logits = d_logits.astype(bf16)
    d_act2 = d_in_sum[:, :width] + nt(d_logits, router_w)
    d_norm, gain_rows = norm_back(middle, r2, norm_ffn, d_act2)
    gain_ffn = jnp.sum(gain_rows, axis=0)
    dy_f = dy_slice.astype(f32)
    d_middle = dy_f + d_norm
    packed = jnp.concatenate([d_middle.astype(bf16), pad_cols(d_logits, routed)], axis=1)
    packed = gather_t(packed)
    d_branch = packed[:, :width]
    d_logits_rows = packed[:, width:]

    d_mixed = nn(d_branch, out_w).astype(bf16)
    d_branch_cols = to_features(d_branch)
    grad_out_w = tn(d_branch_cols, mixed_all)
    dmg = d_mixed.reshape(micro, span, heads, hd).transpose(0, 2, 1, 3)
    dmg = dmg.reshape(micro, heads * span, hd)
    again = bdot(qg, keys, 2, 2).reshape(micro, heads, span, -1) * scale
    probs2 = jnp.where(allowed[:, None], jnp.exp(again - log_total), 0.0)
    d_probs = bdot(dmg, values, 2, 2).reshape(probs2.shape)
    row_dot = jnp.sum(probs2 * d_probs, axis=-1, keepdims=True)
    d_scores = (probs2 * (d_probs - row_dot)).astype(bf16).reshape(micro, heads * span, -1)
    d_q = bdot(d_scores, keys, 2, 1) * scale
    d_keys = bdot(d_scores, qg, 1, 1) * scale
    d_values = bdot(probs2.astype(bf16).reshape(d_scores.shape), dmg, 1, 1)
    d_kv = jnp.concatenate([d_keys, d_values], axis=-1).reshape(micro, back + 1, span, 2 * hd)
    d_kv_own = d_kv[:, back].reshape(rows, 2 * hd)
    for s in range(1, back + 1):
        piece = d_kv[:, back - s].reshape(rows, 2 * hd).astype(bf16)
        d_kv_own = d_kv_own + lax.ppermute(piece, C, [(i + s, i) for i in range(nc - s)]).astype(f32)
    d_q = d_q.reshape(micro, heads, span, hd).transpose(0, 2, 1, 3).reshape(rows, heads, hd)
    d_q_raw, gain_q_rows = heads_back(q_raw, norm_query, cosine[:, None], sine[:, None], d_q)
    d_k_raw, gain_k_rows = heads_back(k_raw, norm_key, cosine, sine, d_kv_own[:, :hd])
    gain_q = jnp.sum(gain_q_rows, axis=(0, 1))
    gain_k = jnp.sum(gain_k_rows, axis=0)
    d_qkv = jnp.concatenate([d_q_raw.reshape(rows, q_cols), d_k_raw, d_kv_own[:, hd:]], axis=1)
    d_qkv = d_qkv.astype(bf16)
    late = lax.all_gather(jnp.concatenate([d_qkv, d_logits_rows], axis=1), BC, axis=0, tiled=True)
    d_act1 = sum_t(nt(d_qkv, w_qkv))
    d_norm1, gain1_rows = norm_back(x_slice, inv_rms(x_slice), norm_attn, d_act1)
    gain_attn = jnp.sum(gain1_rows, axis=0)
    grad_in = gather_t((d_norm + d_norm1).astype(bf16)).astype(f32) + dy.astype(f32)

    grad_qkv = tn(act1_cols, late[:, : d_qkv.shape[1]])
    d_logits_all = late[:, d_qkv.shape[1] : d_qkv.shape[1] + experts]
    d_logits_all = d_logits_all.reshape(nb, nc, nt_, cut, experts).transpose(0, 2, 1, 3, 4)
    d_logits_all = d_logits_all.reshape(-1, experts)
    own_cols = width // sources
    act2_cols = lax.dynamic_slice(act2_all, (0, place * own_cols), (act2_all.shape[0], own_cols))
    grad_router = tn(act2_cols, d_logits_all)

    pieces = [v.reshape(sources, -1) for v in (gain_attn, gain_ffn, gain_q, gain_k)]
    sizes = [v.shape[1] for v in pieces]
    flat = jnp.concatenate(pieces, axis=1)
    lanes = -(-flat.shape[1] // 128) * 128
    flat = jnp.broadcast_to(pad_cols(flat, lanes)[:, None], (sources, nt_, lanes))
    flat = lax.all_to_all(flat.reshape(-1, lanes), ALL, 0, 0, tiled=True)
    flat = jnp.sum(flat, axis=0)
    gains, start = [], 0
    for size in sizes:
        gains.append(flat[start : start + size])
        start += size

    hidden_out = gather_t((branch + sum_all(out_part)).astype(bf16)).astype(f32) + xf
    shape = hidden_in.shape
    return (
        hidden_out.reshape(shape),
        grad_in.reshape(shape),
        gains[0],
        gains[1],
        gains[2],
        gains[3],
        grad_qkv[:, :q_cols],
        grad_qkv[:, q_cols : q_cols + hd],
        grad_qkv[:, q_cols + hd :],
        grad_out_w,
        grad_router,
        grad_gate,
        grad_up,
        grad_down,
    )


def solution(mesh):
    rows = P(None, B, C, None)
    ids = P(None, B, C)
    whole = P()
    matrix = P(BC, T)
    router = P(BC, None)
    expert = P(BC, T, None)
    vector = P(BC)
    in_specs = (rows, ids, rows) + (whole,) * 5 + (matrix,) * 4 + (router,) + (expert,) * 3 + (rows,)
    out_specs = (rows, rows) + (vector,) * 4 + (matrix,) * 4 + (router,) + (expert,) * 3
    return jax.shard_map(body, mesh=mesh, in_specs=in_specs, out_specs=out_specs, check_vma=False)
```

profile of v0, /device:TPU:0, one launch (start us, length us, event | category | flops | bytes accessed | tf_op | source)
XLA Modules:
  0.0 746.4 jit_solution(8929601338880756963)
XLA Ops:
  18.9 6.3 all-to-all-start
  27.4 9.4 %all-to-all-done = s32[8,16,256]{2,1,0:T(8,128)S(1)} async-done(((s32[8,16,256]{2,1,0:T(8,128)}), s32[8,16,256]{2,1,0:T(8,128)S(1)}, u32[]{:S(2)}, u32[]{:S(2)}) %all-to-all-start) | async-done | bytes 131104 | tf_op jit(solution)/shard_map/all_to_all | solution.py:154
  41.6 30.1 %all-gather.7.cloned.1.call-done = bf16[2048,1280]{1,0:T(8,128)(2,1)} async-done(((bf16[256,1280]{1,0:T(8,128)(2,1)}), bf16[2048,1280]{1,0:T(8,128)(2,1)}) %all-gather.7.cloned.1.call-update) | async-done | bytes 5242896 | tf_op jit(solution)/shard_map/all_gather | solution.py:141
  71.8 4.4 fusion.30
  79.0 3.9 collective-permute-start
  96.3 28.0 %all-gather.9.cloned.1.call-done = bf16[2048,1152]{1,0:T(8,128)(2,1)} async-done(((bf16[256,1152]{1,0:T(8,128)(2,1)}), bf16[2048,1152]{1,0:T(8,128)(2,1)}) %all-gather.9.cloned.1.call-update) | async-done | bytes 4718608 | tf_op jit(solution)/shard_map/all_gather | solution.py:144
  127.9 19.5 %all_to_all.137 = bf16[4,64,2048]{2,1,0:T(8,128)(2,1)S(1)} all-to-all(bf16[4,64,2048]{2,1,0:T(8,128)(2,1)S(1)} %bitcast.304), channel_id=1, replica_groups=mesh['batch'=2,'ctx'=4,'tensor'=4] {'tensor'}, dimensions={0} | all-to-all | bytes 2097152 | tf_op jit(solution)/shard_map/all_to_all | solution.py:78
  178.6 35.4 %all-gather.13.cloned.1.call-done = bf16[2048,2048]{1,0:T(8,128)(2,1)} async-done(((bf16[64,2048]{1,0:T(8,128)(2,1)}), bf16[2048,2048]{1,0:T(8,128)(2,1)}) %all-gather.13.cloned.1.call-update) | async-done | bytes 8388624 | tf_op jit(solution)/shard_map/all_gather | solution.py:180
  214.0 11.7 %fusion.104 = f32[2048,768]{0,1:T(8,128)} fusion(bf16[2048,2048]{1,0:T(8,128)(2,1)} %all-gather.13.cloned.1.call-done, bf16[768,2048]{1,0:T(8,128)(2,1)} %bitcast.328), kind=kOutput, calls=%fused_computation.255 | convolution fusion | flops 6442450944 | bytes 17825792 | tf_op jit(solution)/shard_map/dot_general | solution.py:15
  225.8 67.2 %all-gather.11.cloned.1.call-done = bf16[2048,2048]{1,0:T(8,128)(2,1)} async-done(((bf16[64,2048]{1,0:T(8,128)(2,1)}), bf16[2048,2048]{1,0:T(8,128)(2,1)}) %all-gather.11.cloned.1.call-update) | async-done | bytes 8388624 | tf_op jit(solution)/shard_map/all_gather | solution.py:222
  292.9 11.9 %fusion.103 = f32[2048,768]{0,1:T(8,128)} fusion(bf16[2048,2048]{1,0:T(8,128)(2,1)} %all-gather.11.cloned.1.call-done, bf16[768,2048]{1,0:T(8,128)(2,1)} %bitcast.326), kind=kOutput, calls=%fused_computation.254 | convolution fusion | flops 6442450944 | bytes 17825792 | tf_op jit(solution)/shard_map/dot_general | solution.py:15
  304.8 3.7 fusion.101
  308.7 16.6 %multiply_convert_fusion.1 = (bf16[2048,768]{0,1:T(8,128)(2,1)}, f32[2048,768]{0,1:T(8,128)}, bf16[2048,768]{0,1:T(8,128)(2,1)}, bf16[2048,768]{0,1:T(8,128)(2,1)}) fusion(f32[2048,768]{0,1:T(8,128)} %fusion.103, f32[2048,768]{0,1:T(8,128)} %fusion.104, f32[2048]{0:T(1024)S(1)} %bitcast.321, f32[2048]{0:T(1024)S(1)} %bitcast.322, f32[2048]{0:T(1024)S(1)} %bitcast.323, ...), kind=kOutput, calls=%fused_computation.12 | convolution fusion | flops 6477053952 | bytes 39881728 | tf_op jit(solution)/shard_map/dot_general | solution.py:15
  325.3 5.3 select_reduce_fusion.3
  330.6 10.4 %fusion.105 = f32[2048,2048]{0,1:T(8,128)} fusion(bf16[2048,768]{0,1:T(8,128)(2,1)S(1)} %copy-done.82, bf16[768,2048]{1,0:T(8,128)(2,1)S(1)} %bitcast.253), kind=kOutput, calls=%fused_computation.256 | convolution fusion | flops 6442450944 | bytes 23068672 | tf_op jit(solution)/shard_map/dot_general | solution.py:15
  341.0 11.8 %add_convert_fusion = bf16[2048,2048]{0,1:T(8,128)(2,1)S(1)} fusion(f32[2048,2048]{0,1:T(8,128)} %fusion.105, bf16[2048,768]{0,1:T(8,128)(2,1)} %get-tuple-element.37, bf16[768,2048]{1,0:T(8,128)(2,1)} %bitcast.327), kind=kOutput, calls=%fused_computation | convolution fusion | flops 6450839552 | bytes 31457280 | tf_op jit(solution)/shard_map/dot_general | solution.py:15
  352.9 4.2 pad_maximum_fusion
  357.1 12.1 %copy.193 = bf16[2048,2176]{1,0:T(8,128)(2,1)} copy(bf16[2048,2176]{0,1:T(8,128)(2,1)} %pad_maximum_fusion) | data formatting | bytes 17825792 | tf_op jit(solution)/shard_map/reshape | solution.py:85
  372.5 11.1 %convolution_convert_fusion = bf16[2048,2048]{1,0:T(8,128)(2,1)} fusion(bf16[2048,768]{0,1:T(8,128)(2,1)} %get-tuple-element.38, bf16[768,2048]{1,0:T(8,128)(2,1)S(1)} %bitcast.329), kind=kOutput, calls=%fused_computation.6 | convolution fusion | flops 6446645248 | bytes 14680064 | tf_op jit(solution)/shard_map/dot_general | solution.py:15
  387.0 4.9 all-to-all-start.5
  391.9 4.8 dynamic-slice_bitcast_fusion.1
  397.0 45.9 %all-to-all-done.5 = bf16[4,256,2176]{2,1,0:T(8,128)(2,1)} async-done(((bf16[4,256,2176]{2,1,0:T(8,128)(2,1)}), bf16[4,256,2176]{2,1,0:T(8,128)(2,1)}, u32[]{:S(2)}, u32[]{:S(2)}) %all-to-all-start.5) | async-done | bytes 4456480 | tf_op jit(solution)/shard_map/all_to_all | solution.py:78
  442.8 4.2 reduce_sum.362
  450.6 7.8 %fusion.1 = bf16[1024,2048]{1,0:T(8,128)(2,1)} fusion(bf16[1024,2048]{1,0:T(8,128)(2,1)} %collective-permute-done.2, bf16[2,1024,2048]{2,1,0:T(8,128)(2,1)} %bitcast.272, s32[]{:T(128)S(6)} %select_n.115), kind=kLoop, calls=%fused_computation.5 | loop fusion | flops 8388608 | bytes 12582916 | tf_op jit(solution)/shard_map/convert_element_type | solution.py:89
  458.4 19.2 %all-to-all-done.6 = bf16[4,64,2176]{2,1,0:T(8,128)(2,1)S(1)} async-done(((bf16[4,64,2176]{2,1,0:T(8,128)(2,1)}), bf16[4,64,2176]{2,1,0:T(8,128)(2,1)S(1)}, u32[]{:S(2)}, u32[]{:S(2)}) %all-to-all-start.6) | async-done | bytes 1114144 | tf_op jit(solution)/shard_map/all_to_all | solution.py:92
  477.6 5.0 all-to-all-start.2
  491.4 38.1 %all-to-all-done.2 = bf16[4,256,2048]{2,1,0:T(8,128)(2,1)} async-done(((bf16[4,256,2048]{2,1,0:T(8,128)(2,1)}), bf16[4,256,2048]{2,1,0:T(8,128)(2,1)}, u32[]{:S(2)}, u32[]{:S(2)}) %all-to-all-start.2) | async-done | bytes 4194336 | tf_op jit(solution)/shard_map/all_to_all | solution.py:78
  529.5 3.7 all-to-all-start.7
  538.1 4.2 reduce_sum.356
  542.4 4.5 all-to-all-done.7
  546.9 4.2 all-to-all-start.3
  575.8 7.2 collective-permute-done.5
  584.6 11.7 %fusion.107 = f32[768,2048]{1,0:T(8,128)} fusion(bf16[2048,768]{0,1:T(8,128)(2,1)} %get-tuple-element.35, bf16[2048,2048]{1,0:T(8,128)(2,1)} %all-gather.11.cloned.1.call-done), kind=kOutput, calls=%fused_computation.258 | convolution fusion | flops 6442450944 | bytes 17825792 | tf_op jit(solution)/shard_map/dot_general | solution.py:15
  597.8 5.1 convolution_convert_fusion.1
  602.9 4.4 all-to-all-start.8
  608.7 10.7 %all-to-all-done.8 = bf16[4,64,2048]{2,1,0:T(8,128)(2,1)} async-done(((bf16[4,64,2048]{2,1,0:T(8,128)(2,1)}), bf16[4,64,2048]{2,1,0:T(8,128)(2,1)}, u32[]{:S(2)}, u32[]{:S(2)}) %all-to-all-start.8) | async-done | bytes 1048608 | tf_op jit(solution)/shard_map/all_to_all | solution.py:78
  619.4 4.2 all-to-all-start.4
  626.5 10.3 %all-to-all-done.4 = bf16[4,64,2048]{2,1,0:T(8,128)(2,1)} async-done(((bf16[4,64,2048]{2,1,0:T(8,128)(2,1)}), bf16[4,64,2048]{2,1,0:T(8,128)(2,1)}, u32[]{:S(2)}, u32[]{:S(2)}) %all-to-all-start.4) | async-done | bytes 1048608 | tf_op jit(solution)/shard_map/all_to_all | solution.py:73
  636.8 4.6 all-to-all-start.10
  642.5 6.4 all-to-all-done.10
  648.9 4.5 all-to-all-start.9
  653.4 11.8 %fusion.108 = f32[768,2048]{1,0:T(8,128)} fusion(bf16[2048,768]{0,1:T(8,128)(2,1)} %get-tuple-element.37, bf16[2048,2048]{1,0:T(8,128)(2,1)} %all-gather.11.cloned.1.call-done), kind=kOutput, calls=%fused_computation.259 | convolution fusion | flops 6442450944 | bytes 17825792 | tf_op jit(solution)/shard_map/dot_general | solution.py:15
  670.7 11.7 %fusion.109 = f32[768,2048]{1,0:T(8,128)} fusion(bf16[2048,768]{0,1:T(8,128)(2,1)} %get-tuple-element.38, bf16[2048,2048]{1,0:T(8,128)(2,1)} %all-gather.13.cloned.1.call-done), kind=kOutput, calls=%fused_computation.260 | convolution fusion | flops 6442450944 | bytes 17825792 | tf_op jit(solution)/shard_map/dot_general | solution.py:15
  682.4 14.3 %all-to-all-done.12 = bf16[256,8,256]{2,0,1:T(8,128)(2,1)S(1)} async-done(((bf16[256,8,256]{2,0,1:T(8,128)(2,1)}), bf16[256,8,256]{2,0,1:T(8,128)(2,1)S(1)}, u32[]{:S(2)}, u32[]{:S(2)}) %all-to-all-start.12) | async-done | bytes 1048608 | tf_op jit(solution)/shard_map/all_to_all | solution.py:98
  696.7 4.2 all-to-all-start.11
  708.0 4.4 fusion.106
  712.5 14.6 %all-to-all-done.11 = bf16[256,8,256]{2,0,1:T(8,128)(2,1)} async-done(((bf16[256,8,256]{2,0,1:T(8,128)(2,1)}), bf16[256,8,256]{2,0,1:T(8,128)(2,1)}, u32[]{:S(2)}, u32[]{:S(2)}) %all-to-all-start.11) | async-done | bytes 1048608 | tf_op jit(solution)/shard_map/all_to_all | solution.py:98
  727.1 4.5 fusion.4
  (368 shorter events, 146.1 us)
Async XLA Ops:
  7.2 301.5 %copy-start = (bf16[4,192,2048]{2,1,0:T(8,128)(2,1)S(1)}, bf16[4,192,2048]{2,1,0:T(8,128)(2,1)}, u32[]{:S(2)}) copy-start(bf16[4,192,2048]{2,1,0:T(8,128)(2,1)} %param.30) | copy-start | bytes 9437188
  7.2 64.5 %all-gather.7.cloned.1.call-start = ((), (), s32[]{:S(2)}) async-start(), calls=%async_computation.13 | async-start | bytes 5898240 | tf_op jit(solution)/shard_map/all_gather | solution.py:141
  9.4 114.9 %all-gather.9.cloned.1.call-start = ((), (), s32[]{:S(2)}) async-start(), calls=%async_computation.14 | async-start | bytes 5308416 | tf_op jit(solution)/shard_map/all_gather | solution.py:144
  12.2 59.5 %copy-start.46 = (f32[2048]{0:T(1024)S(1)}, f32[2048]{0:T(1024)}, u32[]{:S(2)}) copy-start(f32[2048]{0:T(1024)} %param.21) | copy-start | bytes 24580
  12.3 201.8 %all-gather.13.cloned.1.call-start = ((), (), s32[]{:S(2)}) async-start(), calls=%async_computation.16 | async-start | bytes 8650752 | tf_op jit(solution)/shard_map/all_gather | solution.py:180
  18.9 17.9 %all-to-all-start = ((s32[8,16,256]{2,1,0:T(8,128)}), s32[8,16,256]{2,1,0:T(8,128)S(1)}, u32[]{:S(2)}, u32[]{:S(2)}) async-start(s32[8,16,256]{2,1,0:T(8,128)} %bitcast.4), calls=%async_computation | async-start | bytes 262144 | tf_op jit(solution)/shard_map/all_to_all | solution.py:154
  25.2 267.7 %all-gather.11.cloned.1.call-start = ((), (), s32[]{:S(2)}) async-start(), calls=%async_computation.15 | async-start | bytes 8650752 | tf_op jit(solution)/shard_map/all_gather | solution.py:222
  25.7 51.6 %copy-start.38 = (f32[128,128]{1,0:T(8,128)}, f32[128,128]{1,0:T(8,128)S(1)}, u32[]{:S(2)}) copy-start(f32[128,128]{1,0:T(8,128)S(1)} %get-tuple-element.59) | copy-start | bytes 196612
  25.7 51.6 %copy-start.40 = (f32[128,128]{1,0:T(8,128)}, f32[128,128]{1,0:T(8,128)S(1)}, u32[]{:S(2)}) copy-start(f32[128,128]{1,0:T(8,128)S(1)} %get-tuple-element.60) | copy-start | bytes 196612
  27.3 48.9 %copy-start.67 = (f32[256]{0:T(256)}, f32[256]{0:T(256)S(1)}, u32[]{:S(2)}) copy-start(f32[256]{0:T(256)S(1)} %rsqrt_bitcast_fusion) | copy-start | bytes 3076
  36.8 39.4 %copy-start.43 = (s32[8,16,256]{2,1,0:T(8,128)}, s32[8,16,256]{2,1,0:T(8,128)S(1)}, u32[]{:S(2)}) copy-start(s32[8,16,256]{2,1,0:T(8,128)S(1)} %all-to-all-done) | copy-start | bytes 393220
  77.5 13.2 %collective-permute-start.1 = (bf16[256,256]{1,0:T(8,128)(2,1)S(1)}, bf16[256,256]{1,0:T(8,128)(2,1)S(1)}, u32[]{:S(2)}, u32[]{:S(2)}) collective-permute-start(bf16[256,256]{1,0:T(8,128)(2,1)S(1)} %pad_maximum_fusion.8), channel_id=1, source_target_pairs={{0,4},{4,8},{8,12},{1,5},{5,9},{9,13},{2,6},{6,10},{10,14},{3,7},{... | collective-permute-start | bytes 393224 | tf_op jit(solution)/shard_map/ppermute | solution.py:192
  79.0 11.8 %collective-permute-start = (bf16[256,256]{1,0:T(8,128)(2,1)S(1)}, bf16[256,256]{1,0:T(8,128)(2,1)S(1)}, u32[]{:S(2)}, u32[]{:S(2)}) collective-permute-start(bf16[256,256]{1,0:T(8,128)(2,1)S(1)} %pad_maximum_fusion.8), channel_id=1, source_target_pairs={{0,8},{4,12},{1,9},{5,13},{2,10},{6,14},{3,11},{7,15},{16,24},{20,... | collective-permute-start | bytes 393224 | tf_op jit(solution)/shard_map/ppermute | solution.py:192
  127.9 23.3 %copy-start.45 = (f32[2048]{0:T(1024)S(1)}, f32[2048]{0:T(1024)}, u32[]{:S(2)}) copy-start(f32[2048]{0:T(1024)} %param.22) | copy-start | bytes 24580
  292.9 11.9 %copy-start.6 = (bf16[2048,2048]{1,0:T(8,128)(2,1)S(1)}, bf16[2048,2048]{1,0:T(8,128)(2,1)}, u32[]{:S(2)}) copy-start(bf16[2048,2048]{1,0:T(8,128)(2,1)} %all-gather.11.cloned.1.call-done) | copy-start | bytes 25165828
  369.2 14.4 %slice-start = ((s8[8912896]{0:T(1024)(128)(4,1)}), s8[4194304]{0:T(1024)(128)(4,1)S(1)}, s32[]{:S(2)}) async-start(s8[8912896]{0:T(1024)(128)(4,1)} %bitcast.255), calls=%async_computation.19 | async-start | bytes 8388608
  372.0 11.6 %collective-permute-start.3 = (bf16[1024,2176]{1,0:T(8,128)(2,1)S(1)}, bf16[1024,2176]{1,0:T(8,128)(2,1)S(1)}, u32[]{:S(2)}, u32[]{:S(2)}) collective-permute-start(bf16[1024,2176]{1,0:T(8,128)(2,1)S(1)} %dynamic-slice_bitcast_fusion), channel_id=1, source_target_pairs={{0,16},{16,0},{1,17},{17,1},{2,18},{18,2},{3,19},{19,3},{4,20},{20... | collective-permute-start | bytes 13369352 | tf_op jit(solution)/shard_map/ppermute | solution.py:87
  387.0 55.8 %all-to-all-start.5 = ((bf16[4,256,2176]{2,1,0:T(8,128)(2,1)}), bf16[4,256,2176]{2,1,0:T(8,128)(2,1)}, u32[]{:S(2)}, u32[]{:S(2)}) async-start(bf16[4,256,2176]{2,1,0:T(8,128)(2,1)} %bitcast.264), calls=%async_computation.5 | async-start | bytes 8912896 | tf_op jit(solution)/shard_map/all_to_all | solution.py:78
  396.7 53.9 %collective-permute-start.2 = (bf16[1024,2048]{1,0:T(8,128)(2,1)}, bf16[1024,2048]{1,0:T(8,128)(2,1)}, u32[]{:S(2)}, u32[]{:S(2)}) collective-permute-start(bf16[1024,2048]{1,0:T(8,128)(2,1)} %dynamic-slice_bitcast_fusion.1), channel_id=1, source_target_pairs={{0,16},{16,0},{1,17},{17,1},{2,18},{18,2},{3,19},{19,3},{4,20},{20... | collective-permute-start | bytes 12582920 | tf_op jit(solution)/shard_map/ppermute | solution.py:87
  447.0 30.5 %all-to-all-start.6 = ((bf16[4,64,2176]{2,1,0:T(8,128)(2,1)}), bf16[4,64,2176]{2,1,0:T(8,128)(2,1)S(1)}, u32[]{:S(2)}, u32[]{:S(2)}) async-start(bf16[4,64,2176]{2,1,0:T(8,128)(2,1)} %bitcast.52), calls=%async_computation.6 | async-start | bytes 2228224 | tf_op jit(solution)/shard_map/all_to_all | solution.py:92
  477.6 51.9 %all-to-all-start.2 = ((bf16[4,256,2048]{2,1,0:T(8,128)(2,1)}), bf16[4,256,2048]{2,1,0:T(8,128)(2,1)}, u32[]{:S(2)}, u32[]{:S(2)}) async-start(bf16[4,256,2048]{2,1,0:T(8,128)(2,1)} %bitcast.265), calls=%async_computation.2 | async-start | bytes 8388608 | tf_op jit(solution)/shard_map/all_to_all | solution.py:78
  482.6 225.4 %all-gather.17.cloned.1.call-start = ((), (), s32[]{:S(2)}) async-start(), calls=%async_computation.18 | async-start | bytes 4718592 | tf_op jit(solution)/shard_map/all_gather | solution.py:224
  486.8 46.4 %copy-start.68 = (f32[256]{0:T(256)S(1)}, f32[256]{0:T(256)}, u32[]{:S(2)}) copy-start(f32[256]{0:T(256)} %copy-done.67) | copy-start | bytes 3076
  489.0 46.2 %copy-start.21 = (f32[64,2048]{1,0:T(8,128)}, f32[64,2048]{1,0:T(8,128)S(1)}, u32[]{:S(2)}) copy-start(f32[64,2048]{1,0:T(8,128)S(1)} %get-tuple-element.81) | copy-start | bytes 1572868
  489.0 40.5 %copy-start.76 = (f32[64]{0:T(128)}, f32[64]{0:T(128)S(1)}, u32[]{:S(2)}) copy-start(f32[64]{0:T(128)S(1)} %broadcast_multiply_fusion.4) | copy-start | bytes 772
  529.5 17.4 %all-to-all-start.7 = ((bf16[4,64,2176]{2,1,0:T(8,128)(2,1)}), bf16[4,64,2176]{2,1,0:T(8,128)(2,1)S(1)}, u32[]{:S(2)}, u32[]{:S(2)}) async-start(bf16[4,64,2176]{2,1,0:T(8,128)(2,1)} %bitcast.54), calls=%async_computation.7 | async-start | bytes 2228224 | tf_op jit(solution)/shard_map/all_to_all | solution.py:73
  546.9 49.4 %all-to-all-start.3 = ((bf16[4,64,2048]{2,1,0:T(8,128)(2,1)}), bf16[4,64,2048]{2,1,0:T(8,128)(2,1)}, u32[]{:S(2)}, u32[]{:S(2)}) async-start(bf16[4,64,2048]{2,1,0:T(8,128)(2,1)} %bitcast.40), calls=%async_computation.3 | async-start | bytes 2097152 | tf_op jit(solution)/shard_map/all_to_all | solution.py:92
  551.2 175.9 %all-gather.15.cloned.1.call-start = ((), (), s32[]{:S(2)}) async-start(), calls=%async_computation.17 | async-start | bytes 6488064 | tf_op jit(solution)/shard_map/all_gather | solution.py:313
  565.8 17.2 %collective-permute-start.5 = (bf16[256,256]{1,0:T(8,128)(2,1)S(1)}, bf16[256,256]{1,0:T(8,128)(2,1)S(1)}, u32[]{:S(2)}, u32[]{:S(2)}) collective-permute-start(bf16[256,256]{1,0:T(8,128)(2,1)S(1)} %bitcast.310), channel_id=1, source_target_pairs={{8,0},{12,4},{9,1},{13,5},{10,2},{14,6},{11,3},{15,7},{24,16},{28,... | collective-permute-start | bytes 393224 | tf_op jit(solution)/shard_map/ppermute | solution.py:305
  567.2 15.8 %collective-permute-start.4 = (bf16[256,256]{1,0:T(8,128)(2,1)S(1)}, bf16[256,256]{1,0:T(8,128)(2,1)S(1)}, u32[]{:S(2)}, u32[]{:S(2)}) collective-permute-start(bf16[256,256]{1,0:T(8,128)(2,1)S(1)} %bitcast.309), channel_id=1, source_target_pairs={{4,0},{8,4},{12,8},{5,1},{9,5},{13,9},{6,2},{10,6},{14,10},{7,3},{... | collective-permute-start | bytes 393224 | tf_op jit(solution)/shard_map/ppermute | solution.py:305
  584.6 13.2 %copy-start.33 = (bf16[256,1024]{1,0:T(8,128)(2,1)S(1)}, bf16[256,1024]{1,0:T(8,128)(2,1)}, u32[]{:S(2)}) copy-start(bf16[256,1024]{1,0:T(8,128)(2,1)} %copy-done.32) | copy-start | bytes 1572868
  602.9 16.5 %all-to-all-start.8 = ((bf16[4,64,2048]{2,1,0:T(8,128)(2,1)}), bf16[4,64,2048]{2,1,0:T(8,128)(2,1)}, u32[]{:S(2)}, u32[]{:S(2)}) async-start(bf16[4,64,2048]{2,1,0:T(8,128)(2,1)} %bitcast.65), calls=%async_computation.8 | async-start | bytes 2097152 | tf_op jit(solution)/shard_map/all_to_all | solution.py:78
  607.3 17.9 %copy-start.10 = (bf16[2,1,128,2048]{3,2,1,0:T(8,128)(2,1)S(1)}, bf16[2,1,128,2048]{3,2,1,0:T(8,128)(2,1)}, u32[]{:S(2)}) copy-start(bf16[2,1,128,2048]{3,2,1,0:T(8,128)(2,1)} %param.17) | copy-start | bytes 3145732
  607.3 17.8 %copy-start.48 = (f32[2048]{0:T(1024)S(1)}, f32[2048]{0:T(1024)}, u32[]{:S(2)}) copy-start(f32[2048]{0:T(1024)} %param.21) | copy-start | bytes 24580
  607.3 17.8 %copy-start.78 = (f32[64]{0:T(128)S(1)}, f32[64]{0:T(128)}, u32[]{:S(2)}) copy-start(f32[64]{0:T(128)} %get-tuple-element.72) | copy-start | bytes 772
  607.4 18.8 %copy-start.15 = (f32[64,2048]{1,0:T(8,128)S(1)}, f32[64,2048]{1,0:T(8,128)}, u32[]{:S(2)}) copy-start(f32[64,2048]{1,0:T(8,128)} %copy-done.13) | copy-start | bytes 1572868
  607.4 18.8 %copy-start.22 = (f32[64,2048]{1,0:T(8,128)S(1)}, f32[64,2048]{1,0:T(8,128)}, u32[]{:S(2)}) copy-start(f32[64,2048]{1,0:T(8,128)} %copy-done.21) | copy-start | bytes 1572868
  607.4 18.8 %copy-start.65 = (f32[64]{0:T(128)S(1)}, f32[64]{0:T(128)}, u32[]{:S(2)}) copy-start(f32[64]{0:T(128)} %copy-done.63) | copy-start | bytes 772
  607.4 18.8 %copy-start.75 = (f32[64]{0:T(128)S(1)}, f32[64]{0:T(128)}, u32[]{:S(2)}) copy-start(f32[64]{0:T(128)} %get-tuple-element.73) | copy-start | bytes 772
  607.4 18.8 %copy-start.77 = (f32[64]{0:T(128)S(1)}, f32[64]{0:T(128)}, u32[]{:S(2)}) copy-start(f32[64]{0:T(128)} %copy-done.76) | copy-start | bytes 772
  607.4 18.8 %copy-start.80 = (f32[64]{0:T(128)S(1)}, f32[64]{0:T(128)}, u32[]{:S(2)}) copy-start(f32[64]{0:T(128)} %get-tuple-element.71) | copy-start | bytes 772
  619.4 17.4 %all-to-all-start.4 = ((bf16[4,64,2048]{2,1,0:T(8,128)(2,1)}), bf16[4,64,2048]{2,1,0:T(8,128)(2,1)}, u32[]{:S(2)}, u32[]{:S(2)}) async-start(bf16[4,64,2048]{2,1,0:T(8,128)(2,1)} %bitcast.282), calls=%async_computation.4 | async-start | bytes 2097152 | tf_op jit(solution)/shard_map/all_to_all | solution.py:73
  636.8 12.1 %all-to-all-start.10 = ((f32[32,1,640]{2,1,0:T(1,128)}), f32[32,1,640]{2,1,0:T(1,128)S(1)}, u32[]{:S(2)}, u32[]{:S(2)}) async-start(f32[32,1,640]{2,1,0:T(1,128)} %all_to_all.115), calls=%async_computation.10 | async-start | bytes 163840 | tf_op jit(solution)/shard_map/all_to_all | solution.py:332
  648.9 18.2 %all-to-all-start.9 = ((bf16[4,64,2048]{2,1,0:T(8,128)(2,1)}), bf16[4,64,2048]{2,1,0:T(8,128)(2,1)}, u32[]{:S(2)}, u32[]{:S(2)}) async-start(bf16[4,64,2048]{2,1,0:T(8,128)(2,1)} %bitcast.66), calls=%async_computation.9 | async-start | bytes 2097152 | tf_op jit(solution)/shard_map/all_to_all | solution.py:73
  667.1 29.6 %all-to-all-start.12 = ((bf16[256,8,256]{2,0,1:T(8,128)(2,1)}), bf16[256,8,256]{2,0,1:T(8,128)(2,1)S(1)}, u32[]{:S(2)}, u32[]{:S(2)}) async-start(bf16[256,8,256]{2,0,1:T(8,128)(2,1)} %bitcast.247), calls=%async_computation.12 | async-start | bytes 2097152 | tf_op jit(solution)/shard_map/all_to_all | solution.py:98
  682.4 22.7 %copy-start.25 = (bf16[2,1,128,2048]{3,2,1,0:T(8,128)(2,1)S(1)}, bf16[2,1,128,2048]{3,2,1,0:T(8,128)(2,1)}, u32[]{:S(2)}) copy-start(bf16[2,1,128,2048]{3,2,1,0:T(8,128)(2,1)} %param.33) | copy-start | bytes 3145732
  696.7 30.4 %all-to-all-start.11 = ((bf16[256,8,256]{2,0,1:T(8,128)(2,1)}), bf16[256,8,256]{2,0,1:T(8,128)(2,1)}, u32[]{:S(2)}, u32[]{:S(2)}) async-start(bf16[256,8,256]{2,0,1:T(8,128)(2,1)} %copy.181), calls=%async_computation.11 | async-start | bytes 2097152 | tf_op jit(solution)/shard_map/all_to_all | solution.py:98
  727.1 12.1 %copy-start.1 = (bf16[4,192,2048]{2,1,0:T(8,128)(2,1)S(1)}, bf16[4,192,2048]{2,1,0:T(8,128)(2,1)}, u32[]{:S(2)}) copy-start(bf16[4,192,2048]{2,1,0:T(8,128)(2,1)} %param.30) | copy-start | bytes 9437188
  (62 other events, 277.9 us)
Sparse Core Ops, SparseCore 0:
  10.2 61.4 all-gather.6
  73.9 50.3 all-gather.8
  127.9 86.1 all-gather.12
  216.9 76.0 all-gather.10
  485.9 46.6 all-gather.16
  584.7 58.4 all-gather.14
where the time goes:
time: 758 us; the launch traced here: 746 us
  waiting for transfers between devices  342 us (45%)
  matrix products  153 us (20%)
  local copies, waits for them, and re-layouts  77.4 us (10%)
  other arithmetic  76.2 us (10%)
  starting transfers between devices  62.2 us (8%)
  blocking collectives  19.5 us (3%)
  between operations  16.2 us (2%)
    dot_general x20, matrix products, dot(): lax.dot_general(a, b, (((ca,), (cb,)), ((), ())), preferred_element_type=...  144 us
    all_to_all x3, waiting for transfers between devices, sum_t(): got = lax.all_to_all(v.astype(bf16), T, 0, 0, tiled=True)  94.6 us
    all_gather x1, waiting for transfers between devices, body(): act2_all = lax.all_gather(act2, (B, T, C), axis=0, tiled=True)  67.2 us
    all_gather x1, waiting for transfers between devices, body(): dy_all = lax.all_gather(dy_slice, (B, T, C), axis=0, tiled=True)  35.4 us
    all_gather x1, waiting for transfers between devices, body(): lax.all_gather(jnp.concatenate([w_query, w_key, w_value], axis=1), BC, ax...  30.1 us
    all_to_all x2, waiting for transfers between devices, to_features(): return lax.all_to_all(v, BC, 1, 0, tiled=True)  29 us
    all_gather x1, waiting for transfers between devices, body(): lax.all_gather(jnp.concatenate([w_out, pad_cols(w_router, routed)], axis=...  28 us
    all_to_all x1, blocking collectives, sum_t(): got = lax.all_to_all(v.astype(bf16), T, 0, 0, tiled=True)  19.5 us
  transfers between devices with their start and end apart: 24, of which 16 were waited for; matrix products, arithmetic and copies ran while one was open for 28% of the time, Pallas kernels for 0%

commit v1 on v0

v1 whole, which is shorter than its diff:
```python
import functools

import jax
import jax.numpy as jnp
from jax import lax
from jax.experimental import pallas as pl
from jax.experimental.pallas import tpu as pltpu
from jax.sharding import PartitionSpec as P

B, C, T = "batch", "ctx", "tensor"
BC = (B, C)
ALL = (B, C, T)
f32 = jnp.float32
bf16 = jnp.bfloat16
EPS = 1e-06


def dot(a, b, ca, cb):
    return lax.dot_general(a, b, (((ca,), (cb,)), ((), ())), preferred_element_type=f32)


def nn(a, b):
    return dot(a, b, 1, 0)


def nt(a, b):
    return dot(a, b, 1, 1)


def tn(a, b):
    return dot(a, b, 0, 0)


def bdot(a, b, ca, cb):
    return lax.dot_general(a, b, (((ca,), (cb,)), ((0,), (0,))), preferred_element_type=f32)


def after(*values):
    return lax.optimization_barrier(values)


def pad_cols(v, width):
    return jnp.pad(v, ((0, 0), (0, width - v.shape[1])))


def inv_rms(v):
    return lax.rsqrt(jnp.mean(v * v, axis=-1, keepdims=True) + EPS)


def turn(v):
    half = v.shape[-1] // 2
    return jnp.concatenate([-v[..., half:], v[..., :half]], axis=-1)


def angles(positions, width):
    half = width // 2
    frequency = jnp.power(1000000.0, -(2.0 * jnp.arange(half, dtype=f32)) / width)
    phases = positions.astype(f32)[:, None] * frequency[None, :]
    phases = jnp.concatenate([phases, phases], axis=-1)
    return jnp.cos(phases), jnp.sin(phases)


def norm_back(v, r, gain, grad):
    scaled = gain * grad
    grad_v = r * scaled - v * (r * r * r) * jnp.mean(v * scaled, axis=-1, keepdims=True)
    return grad_v, grad * v * r


def heads_forward(raw, gain, cosine, sine):
    v = raw * inv_rms(raw) * gain
    return (v * cosine + turn(v) * sine).astype(bf16)


def heads_back(raw, gain, cosine, sine, grad):
    grad = grad * cosine - turn(grad) * sine
    return norm_back(raw, inv_rms(raw), gain, grad)


def gather_t(v):
    count = lax.axis_size(T)
    return lax.all_to_all(jnp.concatenate([v] * count, axis=0), T, 0, 0, tiled=True)


def sum_t(v):
    count = lax.axis_size(T)
    got = lax.all_to_all(v.astype(bf16), T, 0, 0, tiled=True)
    got = got.reshape(count, v.shape[0] // count, v.shape[1])
    return jnp.sum(got.astype(f32), axis=0)


def swap(v):
    return lax.ppermute(v, B, [(0, 1), (1, 0)])


def across(v, k):
    return lax.ppermute(v, T, [(i, i ^ k) for i in range(lax.axis_size(T))])


def add_low(*parts):
    total = parts[0].astype(f32)
    for part in parts[1:]:
        total = total + part.astype(f32)
    return total.astype(bf16)


def gather_c(v):
    count = lax.axis_size(C)
    return lax.all_to_all(jnp.concatenate([v] * count, axis=0), C, 0, 0, tiled=True)


def spread_plane(own):
    half = own.shape[0] // 2
    from_x, from_y = across(own, 1), across(own, 2)
    low, high = across(from_x[:half], 2), across(from_y[half:], 1)
    return [own, from_x, from_y, jnp.concatenate([low, high], axis=0)]


def sum_plane(own, ring, corner, held=()):
    diagonal = add_low(corner[0][0], swap(corner[1])[0])
    half = diagonal.shape[0] // 2
    from_x, from_y = across(diagonal[:half], 1), across(diagonal[half:], 2)
    ring_far = swap(ring[1])
    own_far = swap(own[1])
    from_x, from_y, *held = after(from_x, from_y, *held)
    east = add_low(ring[0][0], ring_far[0])
    north = add_low(ring[0][1], ring_far[1])
    east = jnp.concatenate([east[:half], add_low(east[half:], from_y)], axis=0)
    north = jnp.concatenate([add_low(north[:half], from_x), north[half:]], axis=0)
    return add_low(own[0][0], own_far[0], across(east, 1), across(north, 2)), held


def to_features(v):
    return lax.all_to_all(v, BC, 1, 0, tiled=True)


def send_c(plane):
    count = lax.axis_size(C)
    got = lax.all_to_all(plane, C, 0, 0, tiled=True)
    return got.reshape(count, plane.shape[0] // count, plane.shape[1])


SLAB = 256


def sum_c_permute(plane):
    count = lax.axis_size(C)
    cut = plane.shape[0] // count
    c = lax.axis_index(C)
    block = lambda k: lax.dynamic_slice(plane, (((c + k) % count) * cut, 0), (cut, plane.shape[1]))
    total = block(0).astype(f32)
    for k in range(1, count):
        got = lax.ppermute(block(k), C, [(i, (i + k) % count) for i in range(count)])
        total = total + got.astype(f32)
    return total


def expert_kernel(count, first, where_ref, *refs):
    acts, dys, marks = refs[:count], refs[count : count + 2], refs[count + 2 : 2 * count + 2]
    router_ref, place_ref = refs[2 * count + 2 : 2 * count + 4]
    weights_hbm = refs[2 * count + 4 : 2 * count + 7]
    tail = refs[-20:]
    act_all, dy_all, hid_all, dg_all, du_all, near, far = tail[:7]
    act_b, dy_b, hid_b, dg_b, du_b, din_b, mark_b = tail[7:14]
    gate_w, up_w, down_w = tail[14:17]
    in_sem, w_sem, out_sem = tail[17:]
    i = pl.program_id(0)
    width = act_b.shape[2]
    hidden = gate_w.shape[0]
    src = pl.ds(pl.multiple_of(i * SLAB, SLAB), SLAB)
    base = first + i * count * SLAB
    stored = ((act_b, act_all), (dy_b, dy_all), (hid_b, hid_all), (dg_b, dg_all), (du_b, du_all))
    weights = [
        pltpu.make_async_copy(v, w, w_sem.at[k])
        for k, (v, w) in enumerate(zip(weights_hbm, (gate_w, up_w, down_w)))
    ]

    piece = pl.num_programs(0) * SLAB

    def load(k, p):
        if k == 0:
            return pltpu.make_async_copy(acts[p].at[src], act_b.at[p], in_sem.at[0, p])
        rows = pl.ds(pl.multiple_of(where_ref[count + p] * piece + i * SLAB, SLAB), SLAB)
        return pltpu.make_async_copy(dys[p // (count // 2)].at[rows], dy_b.at[p], in_sem.at[1, p])

    def stores(p):
        rows = pl.ds(pl.multiple_of(base + p * SLAB, SLAB), SLAB)
        return [
            pltpu.make_async_copy(v.at[p], to.at[rows], out_sem.at[k, p])
            for k, (v, to) in enumerate(stored)
        ]

    def give(p, place, to):
        return pltpu.make_async_copy(din_b.at[p], to.at[place, src], out_sem.at[5, p])

    load(0, 0).start()

    @pl.when(i == 0)
    def _():
        weights[0].start()
        weights[1].start()

    load(1, 0).start()

    @pl.when(i == 0)
    def _():
        weights[2].start()

    for p in range(1, count):
        load(0, p).start()
        load(1, p).start()
    for p in range(count):
        mark_b[p] = marks[p][0]

    @pl.when(i == 0)
    def _():
        weights[0].wait()
        weights[1].wait()

    def one(p, carry):
        for k, buffer in enumerate((act_b, dy_b)):
            pltpu.make_async_copy(acts[0].at[src], buffer.at[p], in_sem.at[k, p]).wait()
        act = act_b[p]
        mark = mark_b[p]
        logits = nn(act, router_ref[...])
        top = jnp.max(jnp.where(mark > 0.5, logits, -1e30), axis=1, keepdims=True)
        parts = jnp.where(mark > 0.5, jnp.exp(logits - top), 0.0)
        parts = parts / jnp.sum(parts, axis=1, keepdims=True)
        gates = jnp.where(mark > 1.5, parts, 0.0)
        high = gates.astype(bf16)
        low = (gates - high.astype(f32)).astype(bf16)

        @pl.when((p == 0) & (i == 0))
        def _():
            weights[2].wait()

        place = place_ref[...]
        wide = nn(high, place) + nn(low, place)
        gate = nt(act, gate_w[...])
        up = nt(act, up_w[...])
        dyw = nt(dy_b[p], down_w[...])
        sig = 0.5 * jnp.tanh(0.5 * gate) + 0.5
        silu = gate * sig
        hid = silu * up
        hid_b[p] = (wide * hid).astype(bf16)
        share = nt((hid * dyw).astype(bf16), place)
        d_hid = wide * dyw
        dg_b[p] = (d_hid * up * (sig + silu * (1.0 - sig))).astype(bf16)
        du_b[p] = (d_hid * silu).astype(bf16)
        din_b[p, :, width:] = jnp.where(mark > 1.5, share, 0.0).astype(bf16)
        for w in range(0, width, 512):
            cols = slice(w, w + 512)
            total = nn(dg_b[p], gate_w[:, cols]) + nn(du_b[p], up_w[:, cols])
            din_b[p, :, cols] = total.astype(bf16)
        for copy in stores(p):
            copy.start()

        @pl.when(p < count // 2)
        def _():
            give(p, p, near).start()

        @pl.when(p >= count // 2)
        def _():
            give(p, p - count // 2, far).start()

        return carry

    lax.fori_loop(0, count, one, 0)
    for p in range(count):
        for copy in stores(p):
            copy.wait()
        give(p, p % (count // 2), (near, far)[p // (count // 2)]).wait()


def expert_pieces(first, where, acts, dys, marks, consts, held, total_rows):
    count = len(acts)
    rows, width = acts[0].shape
    hidden = consts[2].shape[0]
    routed = consts[0].shape[1]
    left = pl.BlockSpec(memory_space=pl.ANY)
    in_specs = [left] * (count + 2)
    in_specs += [
        pl.BlockSpec((1, SLAB, routed), lambda i, w, p=p: (w[p], i, 0)) for p in range(count)
    ]
    in_specs += [
        pl.BlockSpec(v.shape, lambda i, w: (0, 0), pipeline_mode=pl.Buffered(1)) for v in consts[:2]
    ]
    in_specs += [left] * 3
    out_shape = [jax.ShapeDtypeStruct((total_rows, width), bf16)] * 2
    out_shape += [jax.ShapeDtypeStruct((total_rows, hidden), bf16)] * 3
    out_shape += [jax.ShapeDtypeStruct((count // 2, rows, width + routed), bf16)] * 2
    args = [where, *acts, *dys, *([marks] * count), *consts]
    aliases = {}
    if held is not None:
        for k, v in enumerate(held):
            aliases[len(args)] = k
            args.append(v)
            in_specs.append(left)
    outs = pl.pallas_call(
        functools.partial(expert_kernel, count, first),
        grid_spec=pltpu.PrefetchScalarGridSpec(
            num_scalar_prefetch=1,
            grid=(rows // SLAB,),
            in_specs=in_specs,
            out_specs=[left] * 7,
            scratch_shapes=[pltpu.VMEM((count, SLAB, width), bf16)] * 2
            + [pltpu.VMEM((count, SLAB, hidden), bf16)] * 3
            + [pltpu.VMEM((count, SLAB, width + routed), bf16)]
            + [pltpu.VMEM((count, SLAB, routed), f32)]
            + [pltpu.VMEM((hidden, width), bf16)] * 3
            + [pltpu.SemaphoreType.DMA((2, count))]
            + [pltpu.SemaphoreType.DMA((3,))]
            + [pltpu.SemaphoreType.DMA((6, count))],
        ),
        out_shape=out_shape,
        input_output_aliases=aliases,
        compiler_params=pltpu.CompilerParams(vmem_limit_bytes=56 << 20),
        cost_estimate=pl.CostEstimate(flops=1000, bytes_accessed=1000, transcendentals=0),
    )(*args)
    return outs[:5], outs[5:]


def attend_back_kernel(heads, scale, q_ref, raw_ref, kv_ref, bias_ref, dm_ref, cos_ref, sin_ref, gain_ref, dq_ref, dkv_ref, gq_ref, rows_q, rows_m, rows_p, rows_s):
    span = q_ref.shape[0]
    hd = gain_ref.shape[1]
    keys, values = kv_ref[0, :, :hd], kv_ref[0, :, hd:]
    bias = bias_ref[0]
    cosine, sine = cos_ref[...], sin_ref[...]
    gain = gain_ref[...]

    @pl.when(pl.program_id(0) == 0)
    def _():
        gq_ref[...] = jnp.zeros_like(gq_ref)

    total = jnp.zeros((1, hd), f32)
    for h in range(heads):
        cols = slice(h * hd, (h + 1) * hd)
        lines = slice(h * span, (h + 1) * span)
        q = q_ref[:, cols]
        dm = dm_ref[:, cols]
        rows_q[lines, :] = q
        rows_m[lines, :] = dm
        scores = nt(q, keys) * scale + bias
        weight = jnp.exp(scores - jnp.max(scores, axis=1, keepdims=True))
        probs = weight / jnp.sum(weight, axis=1, keepdims=True)
        d_probs = nt(dm, values)
        d_scores = probs * (d_probs - jnp.sum(probs * d_probs, axis=1, keepdims=True))
        low = d_scores.astype(bf16)
        rows_p[lines, :] = probs.astype(bf16)
        rows_s[lines, :] = low
        d_q = nn(low, keys) * scale
        grad = d_q * cosine - pltpu.roll(d_q, hd // 2, 1) * sine
        raw = raw_ref[:, cols]
        d_raw, gain_rows = norm_back(raw, inv_rms(raw), gain, grad)
        dq_ref[:, cols] = d_raw.astype(bf16)
        total = total + jnp.sum(gain_rows, axis=0, keepdims=True)
    gq_ref[...] += total
    dkv_ref[0, :, :hd] = (tn(rows_s[...], rows_q[...]) * scale).astype(bf16)
    dkv_ref[0, :, hd:] = tn(rows_p[...], rows_m[...]).astype(bf16)


def attend_back(q, qkv, window, bias, d_mixed, cosine, sine, gain):
    micro, reach, pair = window.shape
    hd = pair // 2
    span, q_cols = q.shape[0] // micro, q.shape[1]
    heads = q_cols // hd
    row = lambda m: (m, 0)
    flat = lambda m: (0, 0)
    deep = lambda m: (m, 0, 0)
    return pl.pallas_call(
        functools.partial(attend_back_kernel, heads, hd ** (-0.5)),
        grid=(micro,),
        in_specs=[
            pl.BlockSpec((span, q_cols), row),
            pl.BlockSpec((span, q_cols), row),
            pl.BlockSpec((1, reach, pair), deep),
            pl.BlockSpec((1, span, reach), deep),
            pl.BlockSpec((span, q_cols), row),
            pl.BlockSpec((span, hd), flat),
            pl.BlockSpec((span, hd), flat),
            pl.BlockSpec((1, hd), flat),
        ],
        out_specs=[
            pl.BlockSpec((span, q_cols), row),
            pl.BlockSpec((1, reach, pair), deep),
            pl.BlockSpec((1, hd), flat),
        ],
        out_shape=[
            jax.ShapeDtypeStruct(q.shape, bf16),
            jax.ShapeDtypeStruct(window.shape, bf16),
            jax.ShapeDtypeStruct((1, hd), f32),
        ],
        scratch_shapes=[pltpu.VMEM((heads * span, hd), bf16)] * 2
        + [pltpu.VMEM((heads * span, reach), bf16)] * 2,
        compiler_params=pltpu.CompilerParams(vmem_limit_bytes=32 << 20),
        cost_estimate=pl.CostEstimate(
            flops=10 * micro * heads * span * reach * hd,
            bytes_accessed=10 * micro * span * q_cols,
            transcendentals=micro * heads * span * reach,
        ),
    )(q, qkv, window, bias, d_mixed, cosine, sine, gain)


def turn_back_kernel(experts, got_ref, act_ref, mid_ref, dy_ref, chosen_ref, router_ref, gain_ref, dn_ref, low_ref, dl_ref, gain_out):
    width = mid_ref.shape[1]
    total = got_ref[0].astype(f32)
    for k in range(1, got_ref.shape[0]):
        total = total + got_ref[k].astype(f32)
    d_gates = total[:, width:]
    router = router_ref[...]
    chosen = chosen_ref[...]
    logits = nn(act_ref[...], router)
    real = lax.broadcasted_iota(jnp.int32, logits.shape, 1) < experts
    logits = jnp.where(real, logits, -1e30)
    weight = jnp.exp(logits - jnp.max(logits, axis=1, keepdims=True))
    probs = weight / jnp.sum(weight, axis=1, keepdims=True)
    picked = probs * chosen
    picked_sum = jnp.sum(picked, axis=1, keepdims=True)
    lean = jnp.sum(d_gates * picked / picked_sum, axis=1, keepdims=True)
    c_grad = chosen * (d_gates - lean) / picked_sum
    d_logits = probs * (c_grad - jnp.sum(probs * c_grad, axis=1, keepdims=True))
    d_logits = jnp.where(real, d_logits, 0.0).astype(bf16)
    dl_ref[...] = d_logits
    d_act = total[:, :width] + nt(d_logits, router)
    middle = mid_ref[...]
    d_norm, gain_rows = norm_back(middle, inv_rms(middle), gain_ref[...], d_act)
    dn_ref[...] = d_norm
    low_ref[...] = (dy_ref[...].astype(f32) + d_norm).astype(bf16)
    gain_out[...] = jnp.sum(gain_rows, axis=0, keepdims=True)


def turn_back(experts, got, act2, middle, dy_slice, chosen, router, gain):
    cut, width = middle.shape
    routed = router.shape[1]
    return pl.pallas_call(
        functools.partial(turn_back_kernel, experts),
        out_shape=[
            jax.ShapeDtypeStruct((cut, width), f32),
            jax.ShapeDtypeStruct((cut, width), bf16),
            jax.ShapeDtypeStruct((cut, routed), bf16),
            jax.ShapeDtypeStruct((1, width), f32),
        ],
        compiler_params=pltpu.CompilerParams(vmem_limit_bytes=32 << 20),
        cost_estimate=pl.CostEstimate(
            flops=4 * cut * width * routed, bytes_accessed=20 * cut * width, transcendentals=cut * routed
        ),
    )(got, act2, middle, dy_slice, chosen, router, gain)


def out_kernel(where_ref, hid_ref, down_ref, near_ref, far_ref):
    p = pl.program_id(0)
    value = nn(hid_ref[...], down_ref[...]).astype(bf16)

    @pl.when(p % 2 == 0)
    def _():
        near_ref[0] = value

    @pl.when(p % 2 == 1)
    def _():
        far_ref[0] = value


def out_pieces(hid, down, blocks, homes, piece_rows):
    hidden, width = down.shape
    count = lax.axis_size(T)
    n_slab = piece_rows // SLAB
    where = jnp.concatenate([jnp.asarray(blocks, jnp.int32), homes])
    n = len(blocks)
    home = lambda p, w: (w[n + p // 2], (p // 2) % n_slab, 0)
    return pl.pallas_call(
        out_kernel,
        grid_spec=pltpu.PrefetchScalarGridSpec(
            num_scalar_prefetch=1,
            grid=(n,),
            in_specs=[
                pl.BlockSpec((SLAB, hidden), lambda p, w: (w[p], 0)),
                pl.BlockSpec((hidden, width), lambda p, w: (0, 0), pipeline_mode=pl.Buffered(1)),
            ],
            out_specs=[pl.BlockSpec((1, SLAB, width), home)] * 2,
        ),
        out_shape=[jax.ShapeDtypeStruct((count, piece_rows, width), bf16)] * 2,
        compiler_params=pltpu.CompilerParams(vmem_limit_bytes=32 << 20),
        cost_estimate=pl.CostEstimate(flops=1000, bytes_accessed=1000, transcendentals=0),
    )(where, hid, down)


def sum_t_permute(v):
    count = lax.axis_size(T)
    cut = v.shape[0] // count
    t = lax.axis_index(T)
    low = v.astype(bf16)
    block = lambda k: lax.dynamic_slice(low, ((t ^ k) * cut, 0), (cut, v.shape[1]))
    total = block(0).astype(f32)
    for k in range(1, count):
        total = total + across(block(k), k).astype(f32)
    return total


def body(
    hidden_in,
    segment_ids,
    expert_ids,
    capacity,
    norm_attn,
    norm_ffn,
    norm_query,
    norm_key,
    w_query,
    w_key,
    w_value,
    w_out,
    w_router,
    w_gate,
    w_up,
    w_down,
    grad_out,
):
    micro, _, span, width = hidden_in.shape
    rows = micro * span
    hd = norm_query.shape[0]
    topk = expert_ids.shape[3]
    experts = w_router.shape[1]
    mine = w_gate.shape[0]
    nb, nc, nt_ = lax.axis_size(B), lax.axis_size(C), lax.axis_size(T)
    sources = nb * nc
    cut = rows // nt_
    b, c, t = lax.axis_index(B), lax.axis_index(C), lax.axis_index(T)
    place = b * nc + c
    seq = span * nc
    back = (seq // 2 - 1 + span - 1) // span
    heads = w_query.shape[1] // hd
    q_cols = heads * hd
    scale = hd ** (-0.5)
    routed = -(-experts // 128) * 128

    x = hidden_in.reshape(rows, width)
    dy = grad_out.reshape(rows, width)

    w_qkv = lax.all_gather(
        jnp.concatenate([w_query, w_key, w_value], axis=1), BC, axis=0, tiled=True
    )
    ids_own = expert_ids.reshape(rows, topk).T
    info = jnp.concatenate([ids_own, segment_ids.reshape(1, rows)], axis=0)
    info = jnp.pad(info, ((0, -(-(topk + 1) // 8) * 8 - topk - 1), (0, 0)))
    tall = info.shape[0]
    info = lax.all_to_all(jnp.concatenate([info] * sources, axis=0), BC, 0, 0, tiled=True)
    info = info.reshape(sources, tall, rows)
    ids_all = info[:, :topk]
    seg_all = info[:, topk].reshape(nb, nc, micro, span)
    local = place * mine + jnp.arange(mine)
    hot = jnp.sum((ids_all[:, :, None, :] == local[None, None, :, None]).astype(f32), axis=1)
    hot = hot.reshape(sources, mine, micro, span)
    upper = (jnp.arange(span)[:, None] < jnp.arange(span)[None, :]).astype(bf16)
    within = nn(hot.astype(bf16).reshape(-1, span), upper).reshape(hot.shape)
    totals = jnp.sum(hot, axis=-1)
    earlier = jnp.arange(sources)[:, None] < jnp.arange(sources)[None, :]
    before = jnp.sum(jnp.where(earlier[:, :, None, None], totals[:, None], 0.0), axis=0)
    rank = within + before[..., None]
    room = lax.dynamic_slice(capacity, (place * mine,), (mine,)).astype(f32)
    kept = jnp.where(rank < room[None, :, None, None], hot, 0.0)
    kept = kept.reshape(nb, nc, mine, nt_, cut).transpose(0, 3, 1, 4, 2).reshape(-1, mine)
    ids_rows = ids_all.reshape(nb, nc, topk, nt_, cut).transpose(0, 3, 1, 4, 2).reshape(-1, topk)
    names = jnp.arange(routed)
    marks = jnp.sum((ids_rows[:, :, None] == names).astype(f32), axis=1)
    for e in range(mine):
        marks = marks + jnp.where(names[None, :] == place * mine + e, kept[:, e : e + 1], 0.0)
    piece_rows = nc * cut
    marks = marks.reshape(nb * nt_, piece_rows, routed)
    total_rows = nb * nt_ * piece_rows
    ids_slice = lax.dynamic_slice(expert_ids.reshape(rows, topk), (t * cut, 0), (cut, topk))
    chosen = jnp.sum((ids_slice[:, :, None] == names).astype(f32), axis=1)

    xf = x.astype(f32)
    act1 = (xf * inv_rms(xf) * norm_attn).astype(bf16)
    positions = c * span + jnp.arange(span)
    cosine, sine = angles(positions, hd)
    cosine = jnp.concatenate([cosine] * micro, axis=0)
    sine = jnp.concatenate([sine] * micro, axis=0)
    act1_slice = lax.dynamic_slice(act1, (t * cut, 0), (cut, width))
    own_cols = width // sources

    def columns(v):
        v = gather_t(to_features(v)).reshape(nt_, sources, cut, own_cols)
        return v.transpose(1, 0, 2, 3).reshape(-1, own_cols)

    act1_cols = columns(act1_slice)
    w_or = jnp.concatenate([w_out, pad_cols(w_router, routed)], axis=1)
    w_qkv, w_or, marks, act1, act1_cols, cosine, sine = after(
        w_qkv, w_or, marks, act1, act1_cols, cosine, sine
    )
    w_or = lax.all_gather(w_or, BC, axis=0, tiled=True)
    dy_slice = lax.dynamic_slice(dy, (t * cut, 0), (cut, width))
    dy_tied, w_or = after(dy_slice, w_or)
    dy_own = gather_c(dy_tied)
    out_w = w_or[:, :q_cols]
    router_wide = w_or[:, q_cols:]
    router_w = router_wide[:, :experts]
    n_slab = piece_rows // SLAB
    groups = ((0,), 6 * piece_rows), ((1, 2, 3), 0)
    hidden = mine * w_gate.shape[1]
    gate_w = w_gate.reshape(hidden, width)
    up_w = w_up.reshape(hidden, width)
    down_w = w_down.reshape(hidden, width)
    qkv = nn(act1, w_qkv)
    q_raw = qkv[:, :q_cols].reshape(rows, heads, hd)
    k_raw = qkv[:, q_cols : q_cols + hd]
    q = heads_forward(q_raw, norm_query, cosine[:, None], sine[:, None])
    k = heads_forward(k_raw, norm_key, cosine, sine)
    kv = jnp.concatenate([k, qkv[:, q_cols + hd :].astype(bf16)], axis=1)
    blocks = [
        lax.ppermute(kv, C, [(i, i + s) for i in range(nc - s)]) for s in range(back, 0, -1)
    ]
    window = jnp.stack(blocks + [kv]).reshape(back + 1, micro, span, 2 * hd)
    window = window.transpose(1, 0, 2, 3).reshape(micro, (back + 1) * span, 2 * hd)
    keys, values = window[..., :hd], window[..., hd:]
    seg_seq = lax.dynamic_index_in_dim(seg_all, b, 0, False)
    seg_seq = jnp.pad(seg_seq, ((back, 0), (0, 0), (0, 0)), constant_values=-1)
    seg_win = lax.dynamic_slice(seg_seq, (c, 0, 0), (back + 1, micro, span))
    seg_win = seg_win.transpose(1, 0, 2).reshape(micro, -1)
    seg_own = segment_ids.reshape(micro, span)
    allowed = (seg_own[:, :, None] == seg_win[:, None, :]) & (
        jnp.arange((back + 1) * span)[None, None, :] <= back * span + jnp.arange(span)[None, :, None]
    )
    qg = q.reshape(micro, span, heads, hd).transpose(0, 2, 1, 3)
    qg = qg.reshape(micro, heads * span, hd)
    scores = bdot(qg, keys, 2, 2).reshape(micro, heads, span, -1) * scale
    bias = jnp.where(allowed, 0.0, -1e30)
    side = jnp.where(jnp.arange(hd) < hd // 2, -1.0, 1.0)
    cos_own, sin_own = cosine[:span], sine[:span] * side
    scores = scores + bias[:, None]
    top = jnp.max(scores, axis=-1, keepdims=True)
    weight = jnp.exp(scores - top)
    total = jnp.sum(weight, axis=-1, keepdims=True)
    probs = weight / total
    probs_low = probs.astype(bf16).reshape(micro, heads * span, -1)
    mixed = bdot(probs_low, values, 2, 1).astype(bf16).reshape(micro, heads, span, hd)
    mixed = mixed.transpose(0, 2, 1, 3).reshape(rows, q_cols)
    branch = sum_t_permute(nt(mixed, out_w))
    x_slice = lax.dynamic_slice(x, (t * cut, 0), (cut, width)).astype(f32)
    middle = x_slice + branch
    r2 = inv_rms(middle)
    act2 = (middle * r2 * norm_ffn).astype(bf16)
    dy_own, act2 = after(dy_own, act2)
    act2_own = gather_c(act2)
    dy_plane = lax.all_gather(dy_own, T, axis=0, tiled=True)
    mixed_later, act2_own, router_wide = after(mixed, act2_own, router_wide)
    mixed_all = lax.all_gather(mixed_later, BC, axis=0, tiled=True)

    places = (
        jnp.arange(routed)[:, None] == place * mine + jnp.arange(hidden)[None, :] // w_gate.shape[1]
    ).astype(bf16)
    consts = (router_wide, places, gate_w, up_w, down_w)

    def experts_on(group, base, near, dys, held):
        pairs = [(side, k) for side in (0, 1) for k in group]
        where = [(b ^ side) * nt_ + (t ^ k) for side, k in pairs]
        where += [(t ^ k) * (dys[0].shape[0] // (nt_ * piece_rows)) for side, k in pairs]
        acts = near + [swap(v) for v in near]
        return expert_pieces(base, jnp.stack(where), acts, dys, marks, consts, held, total_rows)

    half = piece_rows // 2
    from_x, from_y = across(act2_own, 1), across(act2_own, 2)
    held, own_sums = experts_on((0,), 6 * piece_rows, [act2_own], [dy_own, swap(dy_own)], None)
    *held, from_x, from_y, dy_plane = after(*held, from_x, from_y, dy_plane)
    low, high = across(from_x[:half], 2), across(from_y[half:], 1)
    corner = jnp.concatenate([low, high], axis=0)
    held, sums = experts_on((1, 2, 3), 0, [from_x, from_y, corner], [dy_plane, swap(dy_plane)], held)
    ring_sums, corner_sums = [v[:2] for v in sums], [v[2:] for v in sums]
    act_all, dy_all, hid_gated, d_gate, d_up = held
    d_in_plane, (hid_later, act2_later) = sum_plane(
        own_sums, ring_sums, corner_sums, (hid_gated, act2)
    )
    blocks, homes = [], []
    for g, start in groups:
        for n, k in enumerate(g):
            for i in range(n_slab):
                first = start // SLAB + i * 2 * len(g) + n
                blocks += [first, first + len(g)]
                homes.append(t ^ k)
    out_near, out_far = out_pieces(hid_later, down_w, blocks, jnp.stack(homes), piece_rows)
    d_in_plane, out_near, out_far, mixed_all = after(d_in_plane, out_near, out_far, mixed_all)
    d_in_got = send_c(d_in_plane)
    out_chip = add_low(out_near, swap(out_far)).reshape(-1, width)
    grad_up = tn(d_up, act_all)
    d_in_got, grad_up, out_chip = after(d_in_got, grad_up, out_chip)
    out_plane = lax.psum_scatter(out_chip, T, scatter_dimension=0, tiled=True)

    d_norm, d_branch_slice, d_logits, gain_ffn = turn_back(
        experts, d_in_got, act2_later, middle, dy_slice, chosen, router_wide, norm_ffn[None]
    )
    d_branch = gather_t(d_branch_slice)
    grad_gate = tn(d_gate, act_all)
    d_branch, grad_gate, act2_late, d_logits = after(d_branch, grad_gate, act2_later, d_logits)
    d_branch_cols = to_features(d_branch)
    devices = sources * nt_
    router_part = tn(act2_late, d_logits)[:, :experts]

    d_mixed = nn(d_branch, out_w).astype(bf16)
    d_q, d_window, gain_q = attend_back(
        q.reshape(rows, q_cols), qkv, window, bias, d_mixed, cos_own, sin_own, norm_query[None]
    )
    d_window, out_plane = after(d_window, out_plane)
    out_sum = sum_c_permute(out_plane)
    d_kv = d_window.reshape(micro, back + 1, span, 2 * hd)
    d_kv_own = d_kv[:, back].reshape(rows, 2 * hd).astype(f32)
    for s in range(1, back + 1):
        piece = d_kv[:, back - s].reshape(rows, 2 * hd)
        d_kv_own = d_kv_own + lax.ppermute(piece, C, [(i + s, i) for i in range(nc - s)]).astype(f32)
    d_k_raw, gain_k_rows = heads_back(k_raw, norm_key, cosine, sine, d_kv_own[:, :hd])
    gain_k = jnp.sum(gain_k_rows, axis=0)
    d_qkv = jnp.concatenate([d_q, d_k_raw.astype(bf16), d_kv_own[:, hd:].astype(bf16)], axis=1)
    d_qkv, out_sum, d_branch_cols = after(d_qkv, out_sum, d_branch_cols)
    late = lax.all_gather(d_qkv, BC, axis=0, tiled=True)
    d_act1 = sum_t(nt(d_qkv, w_qkv))
    d_norm1, gain1_rows = norm_back(x_slice, inv_rms(x_slice), norm_attn, d_act1)
    gain_attn = jnp.sum(gain1_rows, axis=0)

    pieces = [v.reshape(devices, -1) for v in (router_part, gain_attn, gain_ffn, gain_q, gain_k)]
    sizes = [v.shape[1] for v in pieces]
    flat = jnp.concatenate(pieces, axis=1).astype(bf16)
    flat = lax.all_to_all(pad_cols(flat, -(-flat.shape[1] // 128) * 128), ALL, 0, 0, tiled=True)
    flat = jnp.sum(flat.astype(f32), axis=0, keepdims=True)
    lines = -(-flat.shape[1] // width)
    flat = pad_cols(flat, lines * width).reshape(lines, width)
    flat = jnp.pad(flat, ((0, -lines % 16), (0, 0)))
    final = jnp.concatenate([branch + out_sum, d_norm + d_norm1, flat], axis=0).astype(bf16)
    final, dy_all, mixed_all = after(final, dy_all, mixed_all)
    final = gather_t(final).astype(f32).reshape(nt_, -1, width)
    hidden_out = final[:, :cut].reshape(rows, width) + xf
    grad_in = final[:, cut : 2 * cut].reshape(rows, width) + dy.astype(f32)
    flat = final[:, 2 * cut : 2 * cut + lines].reshape(nt_, lines * width)
    gains, start = [], 0
    for size in sizes:
        gains.append(flat[:, start : start + size].reshape(-1))
        start += size
    grad_router = gains.pop(0).reshape(-1, experts)
    grad_down = tn(hid_gated, dy_all)
    grad_out_w = tn(d_branch_cols, mixed_all)
    grad_qkv = tn(act1_cols, late)
    shape = hidden_in.shape
    return (
        hidden_out.reshape(shape),
        grad_in.reshape(shape),
        gains[0],
        gains[1],
        gains[2],
        gains[3],
        grad_qkv[:, :q_cols],
        grad_qkv[:, q_cols : q_cols + hd],
        grad_qkv[:, q_cols + hd :],
        grad_out_w,
        grad_router,
        grad_gate.reshape(w_gate.shape),
        grad_up.reshape(w_up.shape),
        grad_down.reshape(w_down.shape),
    )


def solution(mesh):
    rows = P(None, B, C, None)
    ids = P(None, B, C)
    whole = P()
    matrix = P(BC, T)
    router = P(BC, None)
    expert = P(BC, T, None)
    vector = P(BC)
    in_specs = (rows, ids, rows) + (whole,) * 5 + (matrix,) * 4 + (router,) + (expert,) * 3 + (rows,)
    out_specs = (rows, rows) + (vector,) * 4 + (matrix,) * 4 + (router,) + (expert,) * 3
    return jax.shard_map(body, mesh=mesh, in_specs=in_specs, out_specs=out_specs, check_vma=False)
```

time: 758 us -> 605 us (0.80)
  the two profiles are of different devices: /device:TPU:0 before, /device:TPU:8 now
where the time goes in v1:
time: 605 us; the launch traced here: 594 us
  waiting for transfers between devices  219 us (36%)
  starting transfers between devices  94.9 us (16%)
  Pallas kernels  79.9 us (13%)
  matrix products  66.7 us (11%)
  other arithmetic  63.3 us (10%)
  local copies, waits for them, and re-layouts  54.6 us (9%)
  between operations  15.7 us (3%)
    ppermute x11, waiting for transfers between devices, across(): return lax.ppermute(v, T, [(i, i ^ k) for i in range(lax.axis_size(T))])  71 us
    pallas_call x2, Pallas kernels, expert_pieces(): pl.pallas_call(functools.partial(expert_kernel, count, first), grid_spec=...  60.6 us
    dot_general x11, matrix products, dot(): lax.dot_general(a, b, (((ca,), (cb,)), ((), ())), preferred_element_type=...  60.4 us
    all_to_all x3, waiting for transfers between devices, gather_t(): lax.all_to_all(jnp.concatenate([v] * count, axis=0), T, 0, 0, tiled=True)  24.6 us
    ppermute x3, waiting for transfers between devices, sum_c_permute(): lax.ppermute(block(k), C, [(i, (i + k) % count) for i in range(count)])  21.4 us
    all_to_all x2, waiting for transfers between devices, gather_c(): lax.all_to_all(jnp.concatenate([v] * count, axis=0), C, 0, 0, tiled=True)  21.4 us
    all_to_all x2, waiting for transfers between devices, to_features(): return lax.all_to_all(v, BC, 1, 0, tiled=True)  19.3 us
    unnamed x151, local copies, waits for them, and re-layouts  17.8 us
  transfers between devices with their start and end apart: 45, of which 29 were waited for; matrix products, arithmetic and copies ran while one was open for 27% of the time, Pallas kernels for 6%

profile of v1, /device:TPU:8, one launch (start us, length us, event | category | flops | bytes accessed | tf_op | source)
XLA Modules:
  0.0 594.1 jit_solution(2585919642529259277)
XLA Ops:
  14.9 5.5 all-to-all-start
  26.4 8.5 %all-to-all-start.1 = ((bf16[64,8,256]{2,0,1:T(8,128)(2,1)}), bf16[64,8,256]{2,0,1:T(8,128)(2,1)S(1)}, u32[]{:S(2)}, u32[]{:S(2)}) async-start(bf16[64,8,256]{2,0,1:T(8,128)(2,1)} %bitcast.200), calls=%async_computation.1 | async-start | bytes 524288 | tf_op jit(solution)/shard_map/all_to_all | solution.py:133
  36.5 13.0 %all-to-all-done.1 = bf16[64,8,256]{2,0,1:T(8,128)(2,1)S(1)} async-done(((bf16[64,8,256]{2,0,1:T(8,128)(2,1)}), bf16[64,8,256]{2,0,1:T(8,128)(2,1)S(1)}, u32[]{:S(2)}, u32[]{:S(2)}) %all-to-all-start.1) | async-done | bytes 262176 | tf_op jit(solution)/shard_map/all_to_all | solution.py:133
  50.5 3.7 all-to-all-start.2
  54.3 11.4 %convert_reduce_fusion = f32[2048,128]{1,0:T(8,128)S(1)} fusion(s32[2048,8]{1,0:T(8,128)S(1)} %bitcast.240), kind=kLoop, calls=%fused_computation.2 | loop fusion | flops 6029312 | bytes 1114112 | tf_op jit(solution)/shard_map/reduce_sum | solution.py:563
  76.2 4.6 add.359
  80.8 4.0 fusion.64.raw_ref
  86.1 5.8 collective-permute-start
  96.9 6.1 %collective-permute-done = bf16[256,256]{1,0:T(8,128)(2,1)S(1)} collective-permute-done((bf16[256,256]{1,0:T(8,128)(2,1)S(1)}, bf16[256,256]{1,0:T(8,128)(2,1)S(1)}, u32[]{:S(2)}, u32[]{:S(2)}) %collective-permute-start) | collective-permute-done | bytes 131104 | tf_op jit(solution)/shard_map/ppermute | solution.py:610
  102.9 11.7 %collective-permute-done.1 = bf16[256,256]{1,0:T(8,128)(2,1)S(1)} collective-permute-done((bf16[256,256]{1,0:T(8,128)(2,1)S(1)}, bf16[256,256]{1,0:T(8,128)(2,1)S(1)}, u32[]{:S(2)}, u32[]{:S(2)}) %collective-permute-start.1) | collective-permute-done | bytes 131104 | tf_op jit(solution)/shard_map/ppermute | solution.py:610
  117.0 3.5 fusion.63
  120.5 4.0 fusion.12
  124.8 6.6 %all-gather.8.cloned.1.call-done = bf16[2048,1152]{1,0:T(8,128)(2,1)} async-done(((bf16[256,1152]{1,0:T(8,128)(2,1)}), bf16[2048,1152]{1,0:T(8,128)(2,1)}) %all-gather.8.cloned.1.call-update) | async-done | bytes 4718608 | tf_op jit(solution)/shard_map/all_gather | solution.py:590
  132.6 7.6 %all-to-all-start.3 = ((bf16[4,64,2048]{2,1,0:T(8,128)(2,1)}), bf16[4,64,2048]{2,1,0:T(8,128)(2,1)S(1)}, u32[]{:S(2)}, u32[]{:S(2)}) async-start(bf16[4,64,2048]{2,1,0:T(8,128)(2,1)} %bitcast.41), calls=%async_computation.3 | async-start | bytes 2097152 | tf_op jit(solution)/shard_map/all_to_all | solution.py:108
  147.3 5.7 collective-permute-done.2
  153.0 5.7 collective-permute-done.3
  165.1 6.9 %all-to-all-start.4 = ((bf16[4,64,2048]{2,1,0:T(8,128)(2,1)}), bf16[4,64,2048]{2,1,0:T(8,128)(2,1)S(1)}, u32[]{:S(2)}, u32[]{:S(2)}) async-start(bf16[4,64,2048]{2,1,0:T(8,128)(2,1)} %bitcast.43), calls=%async_computation.4 | async-start | bytes 2097152 | tf_op jit(solution)/shard_map/all_to_all | solution.py:108
  175.1 18.9 %all-to-all-done.4 = bf16[4,64,2048]{2,1,0:T(8,128)(2,1)S(1)} async-done(((bf16[4,64,2048]{2,1,0:T(8,128)(2,1)}), bf16[4,64,2048]{2,1,0:T(8,128)(2,1)S(1)}, u32[]{:S(2)}, u32[]{:S(2)}) %all-to-all-start.4) | async-done | bytes 1048608 | tf_op jit(solution)/shard_map/all_to_all | solution.py:108
  198.5 17.7 %shard_map.281 = (bf16[2048,2048]{1,0:T(8,128)(2,1)}, bf16[2048,2048]{1,0:T(8,128)(2,1)}, bf16[2048,768]{1,0:T(8,128)(2,1)}, bf16[2048,768]{1,0:T(8,128)(2,1)}, ...) custom-call(s32[4]{0:T(128)} %pad_add_fusion.1.where_ref, ...), custom_call_target="tpu_custom_call" | custom-call | flops 1000 | bytes 1000 | tf_op jit(solution)/shard_map/pallas_call | solution.py:298
  216.3 24.8 %collective-permute-done.8.refs_0_ = bf16[256,2048]{1,0:T(8,128)(2,1)S(1)} collective-permute-done((bf16[256,2048]{1,0:T(8,128)(2,1)S(1)}, bf16[256,2048]{1,0:T(8,128)(2,1)S(1)}, u32[]{:S(2)}, u32[]{:S(2)}) %collective-permute-start.8) | collective-permute-done | bytes 1048608 | tf_op jit(solution)/shard_map/ppermute | solution.py:96
  244.9 10.6 %collective-permute-done.10 = bf16[128,2048]{1,0:T(8,128)(2,1)S(1)} collective-permute-done((bf16[128,2048]{1,0:T(8,128)(2,1)S(1)}, bf16[128,2048]{1,0:T(8,128)(2,1)S(1)}, u32[]{:S(2)}, u32[]{:S(2)}) %collective-permute-start.10) | collective-permute-done | bytes 524320 | tf_op jit(solution)/shard_map/ppermute | solution.py:96
  260.8 42.9 %shard_map.282 = (bf16[2048,2048]{1,0:T(8,128)(2,1)}, bf16[2048,2048]{1,0:T(8,128)(2,1)}, bf16[2048,768]{1,0:T(8,128)(2,1)}, bf16[2048,768]{1,0:T(8,128)(2,1)}, ...) custom-call(s32[12]{0:T(128)} %stack.76.where_ref, ...), custom_call_target="tpu_custom_call", output_to_operand_aliasing={{0}: (20, {}), {1}: (21, {}), {2}: (22, {}), {3}: (23, {}),... | custom-call | flops 1000 | bytes 1000 | tf_op jit(solution)/shard_map/pallas_call | solution.py:298
  318.5 12.5 %collective-permute-done.18 = bf16[128,2176]{1,0:T(8,128)(2,1)S(1)} collective-permute-done((bf16[128,2176]{1,0:T(8,128)(2,1)S(1)}, bf16[128,2176]{1,0:T(8,128)(2,1)S(1)}, u32[]{:S(2)}, u32[]{:S(2)}) %collective-permute-start.18) | collective-permute-done | bytes 557088 | tf_op jit(solution)/shard_map/ppermute | solution.py:96
  338.5 9.2 %shard_map.283 = (bf16[4,256,2048]{2,1,0:T(8,128)(2,1)S(1)}, bf16[4,256,2048]{2,1,0:T(8,128)(2,1)S(1)}) custom-call(s32[12]{0:T(128)S(1)} %concatenate.98.where_ref, bf16[2048,768]{1,0:T(8,128)(2,1)S(1)} %copy-done.1, bf16[768,2048]{1,0:T(8,128)(2,1)S(1)} %bitcast.204), custom_call_target="tpu_custom_call" | custom-call | flops 1000 | bytes 1000 | tf_op jit(solution)/shard_map/pallas_call | solution.py:469
  351.8 6.7 %collective-permute-done.20 = bf16[256,2176]{1,0:T(8,128)(2,1)} collective-permute-done((bf16[256,2176]{1,0:T(8,128)(2,1)}, bf16[256,2176]{1,0:T(8,128)(2,1)}, u32[]{:S(2)}, u32[]{:S(2)}) %collective-permute-start.20) | collective-permute-done | bytes 1114144 | tf_op jit(solution)/shard_map/ppermute | solution.py:96
  364.3 5.1 all-to-all-start.5
  369.5 11.9 %fusion.65 = f32[768,2048]{1,0:T(8,128)} fusion(bf16[2048,768]{1,0:T(8,128)(2,1)} %get-tuple-element.119, bf16[2048,2048]{1,0:T(8,128)(2,1)} %get-tuple-element.120), kind=kOutput, calls=%fused_computation.205 | convolution fusion | flops 6442450944 | bytes 17825792 | tf_op jit(solution)/shard_map/dot_general | solution.py:19
  381.4 6.1 %add_convert_fusion = bf16[4,256,2048]{2,1,0:T(8,128)(2,1)} fusion(bf16[4,256,2048]{2,1,0:T(8,128)(2,1)} %collective-permute-done.22, bf16[4,256,2048]{2,1,0:T(8,128)(2,1)S(1)} %copy-done.9), kind=kLoop, calls=%fused_computation.1 | loop fusion | flops 8388608 | bytes 12582912 | tf_op jit(solution)/shard_map/convert_element_type | solution.py:103
  387.5 6.5 %all-to-all-done.5.got_ref = bf16[4,64,2176]{2,1,0:T(8,128)(2,1)S(1)} async-done(((bf16[4,64,2176]{2,1,0:T(8,128)(2,1)}), bf16[4,64,2176]{2,1,0:T(8,128)(2,1)S(1)}, u32[]{:S(2)}, u32[]{:S(2)}) %all-to-all-start.5) | async-done | bytes 1114144 | tf_op jit(solution)/shard_map/all_to_all | solution.py:138
  396.6 3.7 all-to-all-start.6
  400.3 12.5 %fusion.66 = f32[768,2048]{1,0:T(8,128)} fusion(bf16[2048,768]{1,0:T(8,128)(2,1)} %get-tuple-element.126, bf16[2048,2048]{1,0:T(8,128)(2,1)} %get-tuple-element.120), kind=kOutput, calls=%fused_computation.206 | convolution fusion | flops 6442450944 | bytes 17825792 | tf_op jit(solution)/shard_map/dot_general | solution.py:19
  412.8 12.2 %all-to-all-done.6 = bf16[4,64,2048]{2,1,0:T(8,128)(2,1)S(1)} async-done(((bf16[4,64,2048]{2,1,0:T(8,128)(2,1)}), bf16[4,64,2048]{2,1,0:T(8,128)(2,1)S(1)}, u32[]{:S(2)}, u32[]{:S(2)}) %all-to-all-start.6) | async-done | bytes 1048608 | tf_op jit(solution)/shard_map/all_to_all | solution.py:81
  426.3 8.3 %all-to-all-start.7 = ((bf16[256,8,256]{0,2,1:T(8,128)(2,1)}), bf16[256,8,256]{0,2,1:T(8,128)(2,1)}, u32[]{:S(2)}, u32[]{:S(2)}) async-start(bf16[256,8,256]{0,2,1:T(8,128)(2,1)} %bitcast.238), calls=%async_computation.8 | async-start | bytes 2097152 | tf_op jit(solution)/shard_map/all_to_all | solution.py:133
  442.5 8.9 %shard_map.285 = (bf16[256,1024]{1,0:T(8,128)(2,1)S(1)}, bf16[2,384,256]{2,1,0:T(8,128)(2,1)S(1)}, f32[1,128]{1,0:T(1,128)S(1)}) custom-call(bf16[256,1024]{1,0:T(8,128)(2,1)S(1)} %fusion.22.q_ref, f32[256,1280]{1,0:T(8,128)S(1)} %copy-done.5, bf16[2,384,256]{2,1,0:T(8,128)(2,1)S(1)} %bitcast.207, f32[2,128,384]{2,1,0:T(8,128)S(1)} %copy-done.13, ...), custom_call_target="tpu_custom_call" | custom-call | flops 1006632960 | bytes 2621440 | tf_op jit(solution)/shard_map/pallas_call | solution.py:369
  451.5 6.3 %all-to-all-done.7 = bf16[256,8,256]{0,2,1:T(8,128)(2,1)} async-done(((bf16[256,8,256]{0,2,1:T(8,128)(2,1)}), bf16[256,8,256]{0,2,1:T(8,128)(2,1)}, u32[]{:S(2)}, u32[]{:S(2)}) %all-to-all-start.7) | async-done | bytes 1048608 | tf_op jit(solution)/shard_map/all_to_all | solution.py:133
  460.1 4.9 collective-permute-start.23
  475.6 12.5 %collective-permute-done.25 = bf16[64,2048]{1,0:T(8,128)(2,1)} collective-permute-done((bf16[64,2048]{1,0:T(8,128)(2,1)}, bf16[64,2048]{1,0:T(8,128)(2,1)}, u32[]{:S(2)}, u32[]{:S(2)}) %collective-permute-start.25) | collective-permute-done | bytes 262176 | tf_op jit(solution)/shard_map/ppermute | solution.py:152
  488.1 4.7 collective-permute-done.26
  492.8 4.2 collective-permute-done.27
  498.5 5.0 convolution_convert_fusion
  503.5 4.5 all-to-all-start.8
  510.8 10.8 %all-to-all-done.8 = bf16[4,64,2048]{2,1,0:T(8,128)(2,1)} async-done(((bf16[4,64,2048]{2,1,0:T(8,128)(2,1)}), bf16[4,64,2048]{2,1,0:T(8,128)(2,1)}, u32[]{:S(2)}, u32[]{:S(2)}) %all-to-all-start.8) | async-done | bytes 1048608 | tf_op jit(solution)/shard_map/all_to_all | solution.py:86
  528.6 10.0 %all-to-all-done.9 = bf16[32,2,1152]{2,1,0:T(2,128)(2,1)S(1)} async-done(((bf16[32,2,1152]{2,1,0:T(2,128)(2,1)}), bf16[32,2,1152]{2,1,0:T(2,128)(2,1)S(1)}, u32[]{:S(2)}, u32[]{:S(2)}) %all-to-all-start.9) | async-done | bytes 147488 | tf_op jit(solution)/shard_map/all_to_all | solution.py:720
  540.9 3.8 all-to-all-start.10
  544.7 4.6 fusion.69
  549.3 10.9 %fusion.70 = f32[768,2048]{1,0:T(8,128)} fusion(bf16[2048,768]{1,0:T(8,128)(2,1)S(1)} %copy-done.2, bf16[2048,2048]{1,0:T(8,128)(2,1)} %get-tuple-element.149), kind=kOutput, calls=%fused_computation.210 | convolution fusion | flops 6442450944 | bytes 17825792 | tf_op jit(solution)/shard_map/dot_general | solution.py:19
  560.3 12.4 %all-to-all-done.10 = bf16[4,144,2048]{2,1,0:T(8,128)(2,1)S(1)} async-done(((bf16[4,144,2048]{2,1,0:T(8,128)(2,1)}), bf16[4,144,2048]{2,1,0:T(8,128)(2,1)S(1)}, u32[]{:S(2)}, u32[]{:S(2)}) %all-to-all-start.10) | async-done | bytes 2359328 | tf_op jit(solution)/shard_map/all_to_all | solution.py:81
  581.1 4.0 fusion.68
  (375 shorter events, 146.8 us)
Async XLA Ops:
  7.2 64.7 %all-gather.6.cloned.1.call-start = ((), (), s32[]{:S(2)}) async-start(), calls=%async_computation.12 | async-start | bytes 5898240 | tf_op jit(solution)/shard_map/all_gather | solution.py:538
  14.9 11.5 %all-to-all-start = ((s32[8,16,256]{2,1,0:T(8,128)}), s32[8,16,256]{2,1,0:T(8,128)S(1)}, u32[]{:S(2)}, u32[]{:S(2)}) async-start(s32[8,16,256]{2,1,0:T(8,128)} %bitcast.3), calls=%async_computation | async-start | bytes 262144 | tf_op jit(solution)/shard_map/all_to_all | solution.py:545
  24.5 61.5 %copy-start.32 = (f32[256,128]{1,0:T(8,128)}, f32[256,128]{1,0:T(8,128)S(1)}, u32[]{:S(2)}) copy-start(f32[256,128]{1,0:T(8,128)S(1)} %get-tuple-element.85) | copy-start | bytes 393220
  26.4 24.1 %copy-start.50 = (s32[8,16,256]{2,1,0:T(8,128)}, s32[8,16,256]{2,1,0:T(8,128)S(1)}, u32[]{:S(2)}) copy-start(s32[8,16,256]{2,1,0:T(8,128)S(1)} %all-to-all-done) | copy-start | bytes 393220
  26.4 23.1 %all-to-all-start.1 = ((bf16[64,8,256]{2,0,1:T(8,128)(2,1)}), bf16[64,8,256]{2,0,1:T(8,128)(2,1)S(1)}, u32[]{:S(2)}, u32[]{:S(2)}) async-start(bf16[64,8,256]{2,0,1:T(8,128)(2,1)} %bitcast.200), calls=%async_computation.1 | async-start | bytes 524288 | tf_op jit(solution)/shard_map/all_to_all | solution.py:133
  50.5 17.2 %all-to-all-start.2 = ((bf16[4,512,256]{2,1,0:T(8,128)(2,1)}), bf16[4,512,256]{2,1,0:T(8,128)(2,1)S(1)}, u32[]{:S(2)}, u32[]{:S(2)}) async-start(bf16[4,512,256]{2,1,0:T(8,128)(2,1)} %bitcast.14), calls=%async_computation.2 | async-start | bytes 2097152 | tf_op jit(solution)/shard_map/all_to_all | solution.py:81
  54.2 77.3 %all-gather.8.cloned.1.call-start = ((), (), s32[]{:S(2)}) async-start(), calls=%async_computation.13 | async-start | bytes 5308416 | tf_op jit(solution)/shard_map/all_gather | solution.py:590
  73.0 58.4 %copy-start.10 = (bf16[64,2048]{1,0:T(8,128)(2,1)}, bf16[64,2048]{1,0:T(8,128)(2,1)S(1)}, u32[]{:S(2)}) copy-start(bf16[64,2048]{1,0:T(8,128)(2,1)S(1)} %constant_dynamic-slice_fusion.7.dy_ref) | copy-start | bytes 786436
  86.1 16.8 %collective-permute-start = (bf16[256,256]{1,0:T(8,128)(2,1)S(1)}, bf16[256,256]{1,0:T(8,128)(2,1)S(1)}, u32[]{:S(2)}, u32[]{:S(2)}) collective-permute-start(bf16[256,256]{1,0:T(8,128)(2,1)S(1)} %pad_maximum_fusion.11), channel_id=1, source_target_pairs={{0,8},{4,12},{1,9},{5,13},{2,10},{6,14},{3,11},{7,15},{16,24},{20,... | collective-permute-start | bytes 393224 | tf_op jit(solution)/shard_map/ppermute | solution.py:610
  91.9 22.7 %collective-permute-start.1 = (bf16[256,256]{1,0:T(8,128)(2,1)S(1)}, bf16[256,256]{1,0:T(8,128)(2,1)S(1)}, u32[]{:S(2)}, u32[]{:S(2)}) collective-permute-start(bf16[256,256]{1,0:T(8,128)(2,1)S(1)} %pad_maximum_fusion.11), channel_id=1, source_target_pairs={{0,4},{4,8},{8,12},{1,5},{5,9},{9,13},{2,6},{6,10},{10,14},{3,7},{... | collective-permute-start | bytes 393224 | tf_op jit(solution)/shard_map/ppermute | solution.py:610
  132.6 30.4 %all-to-all-start.3 = ((bf16[4,64,2048]{2,1,0:T(8,128)(2,1)}), bf16[4,64,2048]{2,1,0:T(8,128)(2,1)S(1)}, u32[]{:S(2)}, u32[]{:S(2)}) async-start(bf16[4,64,2048]{2,1,0:T(8,128)(2,1)} %bitcast.41), calls=%async_computation.3 | async-start | bytes 2097152 | tf_op jit(solution)/shard_map/all_to_all | solution.py:108
  140.1 101.0 %all-gather.10.cloned.1.call-start = ((), (), s32[]{:S(2)}) async-start(), calls=%async_computation.14 | async-start | bytes 5242880 | tf_op jit(solution)/shard_map/all_gather | solution.py:644
  143.7 9.3 %collective-permute-start.2 = (bf16[64,2048]{1,0:T(8,128)(2,1)S(1)}, bf16[64,2048]{1,0:T(8,128)(2,1)S(1)}, u32[]{:S(2)}, u32[]{:S(2)}) collective-permute-start(bf16[64,2048]{1,0:T(8,128)(2,1)S(1)} %get-tuple-element.244), channel_id=1, source_target_pairs={{0,1},{1,0},{2,3},{3,2},{4,5},{5,4},{6,7},{7,6},{8,9},{9,8},{10,11... | collective-permute-start | bytes 786440 | tf_op jit(solution)/shard_map/ppermute | solution.py:96
  145.5 13.2 %collective-permute-start.3 = (bf16[64,2048]{1,0:T(8,128)(2,1)S(1)}, bf16[64,2048]{1,0:T(8,128)(2,1)S(1)}, u32[]{:S(2)}, u32[]{:S(2)}) collective-permute-start(bf16[64,2048]{1,0:T(8,128)(2,1)S(1)} %get-tuple-element.246), channel_id=1, source_target_pairs={{0,2},{1,3},{2,0},{3,1},{4,6},{5,7},{6,4},{7,5},{8,10},{9,11},{10,... | collective-permute-start | bytes 786440 | tf_op jit(solution)/shard_map/ppermute | solution.py:96
  147.0 11.7 %collective-permute-start.4 = (bf16[64,2048]{1,0:T(8,128)(2,1)S(1)}, bf16[64,2048]{1,0:T(8,128)(2,1)S(1)}, u32[]{:S(2)}, u32[]{:S(2)}) collective-permute-start(bf16[64,2048]{1,0:T(8,128)(2,1)S(1)} %get-tuple-element.245), channel_id=1, source_target_pairs={{0,3},{1,2},{2,1},{3,0},{4,7},{5,6},{6,5},{7,4},{8,11},{9,10},{10,... | collective-permute-start | bytes 786440 | tf_op jit(solution)/shard_map/ppermute | solution.py:96
  165.1 28.9 %all-to-all-start.4 = ((bf16[4,64,2048]{2,1,0:T(8,128)(2,1)}), bf16[4,64,2048]{2,1,0:T(8,128)(2,1)S(1)}, u32[]{:S(2)}, u32[]{:S(2)}) async-start(bf16[4,64,2048]{2,1,0:T(8,128)(2,1)} %bitcast.43), calls=%async_computation.4 | async-start | bytes 2097152 | tf_op jit(solution)/shard_map/all_to_all | solution.py:108
  172.0 192.3 %all-gather.12.cloned.1.call-start = ((), (), s32[]{:S(2)}) async-start(), calls=%async_computation.15 | async-start | bytes 4718592 | tf_op jit(solution)/shard_map/all_gather | solution.py:646
  175.1 23.4 %collective-permute-start.6 = (bf16[256,2048]{1,0:T(8,128)(2,1)S(1)}, bf16[256,2048]{1,0:T(8,128)(2,1)}, u32[]{:S(2)}, u32[]{:S(2)}) collective-permute-start(bf16[256,2048]{1,0:T(8,128)(2,1)S(1)} %bitcast.223), channel_id=1, source_target_pairs={{0,16},{16,0},{1,17},{17,1},{2,18},{18,2},{3,19},{19,3},{4,20},{20... | collective-permute-start | bytes 3145736 | tf_op jit(solution)/shard_map/ppermute | solution.py:92
  194.0 4.5 collective-permute-start.5
  194.0 47.0 %collective-permute-start.8 = (bf16[256,2048]{1,0:T(8,128)(2,1)S(1)}, bf16[256,2048]{1,0:T(8,128)(2,1)S(1)}, u32[]{:S(2)}, u32[]{:S(2)}) collective-permute-start(bf16[256,2048]{1,0:T(8,128)(2,1)S(1)} %bitcast.232), channel_id=1, source_target_pairs={{0,1},{1,0},{2,3},{3,2},{4,5},{5,4},{6,7},{7,6},{8,9},{9,8},{10,11... | collective-permute-start | bytes 3145736 | tf_op jit(solution)/shard_map/ppermute | solution.py:96
  195.7 45.4 %collective-permute-start.9 = (bf16[256,2048]{1,0:T(8,128)(2,1)S(1)}, bf16[256,2048]{1,0:T(8,128)(2,1)}, u32[]{:S(2)}, u32[]{:S(2)}) collective-permute-start(bf16[256,2048]{1,0:T(8,128)(2,1)S(1)} %bitcast.233), channel_id=1, source_target_pairs={{0,2},{1,3},{2,0},{3,1},{4,6},{5,7},{6,4},{7,5},{8,10},{9,11},{10,... | collective-permute-start | bytes 3145736 | tf_op jit(solution)/shard_map/ppermute | solution.py:96
  241.1 19.7 %collective-permute-start.15 = (bf16[1024,2048]{1,0:T(8,128)(2,1)}, bf16[1024,2048]{1,0:T(8,128)(2,1)}, u32[]{:S(2)}, u32[]{:S(2)}) collective-permute-start(bf16[1024,2048]{1,0:T(8,128)(2,1)} %all-gather.10.cloned.1.call-done.refs_6_), channel_id=1, source_target_pairs={{0,16},{16,0},{1,17},{17,1},{2,18},{18,2},{3,19},{19,3},{4,20},{20... | collective-permute-start | bytes 12582920 | tf_op jit(solution)/shard_map/ppermute | solution.py:92
  241.2 14.4 %collective-permute-start.10 = (bf16[128,2048]{1,0:T(8,128)(2,1)S(1)}, bf16[128,2048]{1,0:T(8,128)(2,1)S(1)}, u32[]{:S(2)}, u32[]{:S(2)}) collective-permute-start(bf16[128,2048]{1,0:T(8,128)(2,1)S(1)} %slice.198), channel_id=1, source_target_pairs={{0,2},{1,3},{2,0},{3,1},{4,6},{5,7},{6,4},{7,5},{8,10},{9,11},{10,... | collective-permute-start | bytes 1572872 | tf_op jit(solution)/shard_map/ppermute | solution.py:96
  243.8 14.1 %collective-permute-start.11 = (bf16[128,2048]{1,0:T(8,128)(2,1)S(1)}, bf16[128,2048]{1,0:T(8,128)(2,1)S(1)}, u32[]{:S(2)}, u32[]{:S(2)}) collective-permute-start(bf16[128,2048]{1,0:T(8,128)(2,1)S(1)} %slice.199), channel_id=1, source_target_pairs={{0,1},{1,0},{2,3},{3,2},{4,5},{5,4},{6,7},{7,6},{8,9},{9,8},{10,11... | collective-permute-start | bytes 1572872 | tf_op jit(solution)/shard_map/ppermute | solution.py:96
  244.4 14.3 %collective-permute-start.12 = (bf16[256,2048]{1,0:T(8,128)(2,1)S(1)}, bf16[256,2048]{1,0:T(8,128)(2,1)S(1)}, u32[]{:S(2)}, u32[]{:S(2)}) collective-permute-start(bf16[256,2048]{1,0:T(8,128)(2,1)S(1)} %collective-permute-done.8.refs_0_), channel_id=1, source_target_pairs={{0,16},{16,0},{1,17},{17,1},{2,18},{18,2},{3,19},{19,3},{4,20},{20... | collective-permute-start | bytes 3145736 | tf_op jit(solution)/shard_map/ppermute | solution.py:92
  244.4 14.3 %collective-permute-start.13 = (bf16[256,2048]{1,0:T(8,128)(2,1)}, bf16[256,2048]{1,0:T(8,128)(2,1)}, u32[]{:S(2)}, u32[]{:S(2)}) collective-permute-start(bf16[256,2048]{1,0:T(8,128)(2,1)} %collective-permute-done.9.refs_1_), channel_id=1, source_target_pairs={{0,16},{16,0},{1,17},{17,1},{2,18},{18,2},{3,19},{19,3},{4,20},{20... | collective-permute-start | bytes 3145736 | tf_op jit(solution)/shard_map/ppermute | solution.py:92
  257.9 2.9 collective-permute-start.14
  306.9 6.3 %collective-permute-start.16 = (bf16[2,256,2176]{2,1,0:T(8,128)(2,1)}, bf16[2,256,2176]{2,1,0:T(8,128)(2,1)S(1)}, u32[]{:S(2)}, u32[]{:S(2)}) collective-permute-start(bf16[2,256,2176]{2,1,0:T(8,128)(2,1)} %slice.201), channel_id=1, source_target_pairs={{0,16},{16,0},{1,17},{17,1},{2,18},{18,2},{3,19},{19,3},{4,20},{20... | collective-permute-start | bytes 6684680 | tf_op jit(solution)/shard_map/ppermute | solution.py:92
  309.3 3.8 collective-permute-start.17
  309.7 42.1 %collective-permute-start.7 = (bf16[1,256,2176]{2,1,0:T(8,128)(2,1)}, bf16[1,256,2176]{2,1,0:T(8,128)(2,1)}, u32[]{:S(2)}, u32[]{:S(2)}) collective-permute-start(bf16[1,256,2176]{2,1,0:T(8,128)(2,1)} %get-tuple-element.95), channel_id=1, source_target_pairs={{0,16},{16,0},{1,17},{17,1},{2,18},{18,2},{3,19},{19,3},{4,20},{20... | collective-permute-start | bytes 3342344 | tf_op jit(solution)/shard_map/ppermute | solution.py:92
  316.3 14.7 %collective-permute-start.18 = (bf16[128,2176]{1,0:T(8,128)(2,1)S(1)}, bf16[128,2176]{1,0:T(8,128)(2,1)S(1)}, u32[]{:S(2)}, u32[]{:S(2)}) collective-permute-start(bf16[128,2176]{1,0:T(8,128)(2,1)S(1)} %get-tuple-element.239), channel_id=1, source_target_pairs={{0,1},{1,0},{2,3},{3,2},{4,5},{5,4},{6,7},{7,6},{8,9},{9,8},{10,11... | collective-permute-start | bytes 1671176 | tf_op jit(solution)/shard_map/ppermute | solution.py:96
  316.9 14.4 %collective-permute-start.19 = (bf16[128,2176]{1,0:T(8,128)(2,1)S(1)}, bf16[128,2176]{1,0:T(8,128)(2,1)S(1)}, u32[]{:S(2)}, u32[]{:S(2)}) collective-permute-start(bf16[128,2176]{1,0:T(8,128)(2,1)S(1)} %get-tuple-element.238), channel_id=1, source_target_pairs={{0,2},{1,3},{2,0},{3,1},{4,6},{5,7},{6,4},{7,5},{8,10},{9,11},{10,... | collective-permute-start | bytes 1671176 | tf_op jit(solution)/shard_map/ppermute | solution.py:96
  332.6 25.9 %collective-permute-start.20 = (bf16[256,2176]{1,0:T(8,128)(2,1)}, bf16[256,2176]{1,0:T(8,128)(2,1)}, u32[]{:S(2)}, u32[]{:S(2)}) collective-permute-start(bf16[256,2176]{1,0:T(8,128)(2,1)} %pad_maximum_fusion.1), channel_id=1, source_target_pairs={{0,1},{1,0},{2,3},{3,2},{4,5},{5,4},{6,7},{7,6},{8,9},{9,8},{10,11... | collective-permute-start | bytes 3342344 | tf_op jit(solution)/shard_map/ppermute | solution.py:96
  335.3 25.6 %collective-permute-start.21 = (bf16[256,2176]{1,0:T(8,128)(2,1)}, bf16[256,2176]{1,0:T(8,128)(2,1)}, u32[]{:S(2)}, u32[]{:S(2)}) collective-permute-start(bf16[256,2176]{1,0:T(8,128)(2,1)} %pad_maximum_fusion.2), channel_id=1, source_target_pairs={{0,2},{1,3},{2,0},{3,1},{4,6},{5,7},{6,4},{7,5},{8,10},{9,11},{10,... | collective-permute-start | bytes 3342344 | tf_op jit(solution)/shard_map/ppermute | solution.py:96
  364.3 17.1 %collective-permute-start.22 = (bf16[4,256,2048]{2,1,0:T(8,128)(2,1)}, bf16[4,256,2048]{2,1,0:T(8,128)(2,1)}, u32[]{:S(2)}, u32[]{:S(2)}) collective-permute-start(bf16[4,256,2048]{2,1,0:T(8,128)(2,1)} %copy-done.18), channel_id=1, source_target_pairs={{0,16},{16,0},{1,17},{17,1},{2,18},{18,2},{3,19},{19,3},{4,20},{20... | collective-permute-start | bytes 12582920 | tf_op jit(solution)/shard_map/ppermute | solution.py:92
  364.3 29.7 %all-to-all-start.5 = ((bf16[4,64,2176]{2,1,0:T(8,128)(2,1)}), bf16[4,64,2176]{2,1,0:T(8,128)(2,1)S(1)}, u32[]{:S(2)}, u32[]{:S(2)}) async-start(bf16[4,64,2176]{2,1,0:T(8,128)(2,1)} %bitcast.230), calls=%async_computation.5 | async-start | bytes 2228224 | tf_op jit(solution)/shard_map/all_to_all | solution.py:138
  369.4 90.6 %reduce-scatter.2.cloned.1.call-start = ((), (), s32[]{:S(2)}) async-start(), calls=%async_computation.16 | async-start | bytes 5242880 | tf_op jit(solution)/shard_map/reduce_scatter | solution.py:685
  396.6 28.4 %all-to-all-start.6 = ((bf16[4,64,2048]{2,1,0:T(8,128)(2,1)}), bf16[4,64,2048]{2,1,0:T(8,128)(2,1)S(1)}, u32[]{:S(2)}, u32[]{:S(2)}) async-start(bf16[4,64,2048]{2,1,0:T(8,128)(2,1)} %bitcast.68), calls=%async_computation.6 | async-start | bytes 2097152 | tf_op jit(solution)/shard_map/all_to_all | solution.py:81
  426.3 31.5 %all-to-all-start.7 = ((bf16[256,8,256]{0,2,1:T(8,128)(2,1)}), bf16[256,8,256]{0,2,1:T(8,128)(2,1)}, u32[]{:S(2)}, u32[]{:S(2)}) async-start(bf16[256,8,256]{0,2,1:T(8,128)(2,1)} %bitcast.238), calls=%async_computation.8 | async-start | bytes 2097152 | tf_op jit(solution)/shard_map/all_to_all | solution.py:133
  434.6 146.5 %all-gather.14.cloned.1.call-start = ((), (), s32[]{:S(2)}) async-start(), calls=%async_computation.17 | async-start | bytes 5898240 | tf_op jit(solution)/shard_map/all_gather | solution.py:712
  460.1 13.8 %collective-permute-start.23 = (bf16[256,256]{1,0:T(8,128)(2,1)S(1)}, bf16[256,256]{1,0:T(8,128)(2,1)S(1)}, u32[]{:S(2)}, u32[]{:S(2)}) collective-permute-start(bf16[256,256]{1,0:T(8,128)(2,1)S(1)} %bitcast.264), channel_id=1, source_target_pairs={{4,0},{8,4},{12,8},{5,1},{9,5},{13,9},{6,2},{10,6},{14,10},{7,3},{... | collective-permute-start | bytes 393224 | tf_op jit(solution)/shard_map/ppermute | solution.py:707
  465.1 8.9 %collective-permute-start.24 = (bf16[256,256]{1,0:T(8,128)(2,1)S(1)}, bf16[256,256]{1,0:T(8,128)(2,1)S(1)}, u32[]{:S(2)}, u32[]{:S(2)}) collective-permute-start(bf16[256,256]{1,0:T(8,128)(2,1)S(1)} %bitcast.263), channel_id=1, source_target_pairs={{8,0},{12,4},{9,1},{13,5},{10,2},{14,6},{11,3},{15,7},{24,16},{28,... | collective-permute-start | bytes 393224 | tf_op jit(solution)/shard_map/ppermute | solution.py:707
  468.4 19.7 %collective-permute-start.25 = (bf16[64,2048]{1,0:T(8,128)(2,1)}, bf16[64,2048]{1,0:T(8,128)(2,1)}, u32[]{:S(2)}, u32[]{:S(2)}) collective-permute-start(bf16[64,2048]{1,0:T(8,128)(2,1)} %get-tuple-element.241), channel_id=1, source_target_pairs={{0,4},{4,8},{8,12},{12,0},{1,5},{5,9},{9,13},{13,1},{2,6},{6,10},{... | collective-permute-start | bytes 786440 | tf_op jit(solution)/shard_map/ppermute | solution.py:152
  469.9 22.9 %collective-permute-start.26 = (bf16[64,2048]{1,0:T(8,128)(2,1)}, bf16[64,2048]{1,0:T(8,128)(2,1)}, u32[]{:S(2)}, u32[]{:S(2)}) collective-permute-start(bf16[64,2048]{1,0:T(8,128)(2,1)} %get-tuple-element.243), channel_id=1, source_target_pairs={{0,8},{4,12},{8,0},{12,4},{1,9},{5,13},{9,1},{13,5},{2,10},{6,14},... | collective-permute-start | bytes 786440 | tf_op jit(solution)/shard_map/ppermute | solution.py:152
  472.0 25.0 %collective-permute-start.27 = (bf16[64,2048]{1,0:T(8,128)(2,1)}, bf16[64,2048]{1,0:T(8,128)(2,1)}, u32[]{:S(2)}, u32[]{:S(2)}) collective-permute-start(bf16[64,2048]{1,0:T(8,128)(2,1)} %get-tuple-element.242), channel_id=1, source_target_pairs={{0,12},{4,0},{8,4},{12,8},{1,13},{5,1},{9,5},{13,9},{2,14},{6,2},{... | collective-permute-start | bytes 786440 | tf_op jit(solution)/shard_map/ppermute | solution.py:152
  503.5 18.1 %all-to-all-start.8 = ((bf16[4,64,2048]{2,1,0:T(8,128)(2,1)}), bf16[4,64,2048]{2,1,0:T(8,128)(2,1)}, u32[]{:S(2)}, u32[]{:S(2)}) async-start(bf16[4,64,2048]{2,1,0:T(8,128)(2,1)} %bitcast.255), calls=%async_computation.9 | async-start | bytes 2097152 | tf_op jit(solution)/shard_map/all_to_all | solution.py:86
  525.3 13.3 %all-to-all-start.9 = ((bf16[32,2,1152]{2,1,0:T(2,128)(2,1)}), bf16[32,2,1152]{2,1,0:T(2,128)(2,1)S(1)}, u32[]{:S(2)}, u32[]{:S(2)}) async-start(bf16[32,2,1152]{2,1,0:T(2,128)(2,1)} %reshape.570), calls=%async_computation.10 | async-start | bytes 294912 | tf_op jit(solution)/shard_map/all_to_all | solution.py:720
  540.9 31.7 %all-to-all-start.10 = ((bf16[4,144,2048]{2,1,0:T(8,128)(2,1)}), bf16[4,144,2048]{2,1,0:T(8,128)(2,1)S(1)}, u32[]{:S(2)}, u32[]{:S(2)}) async-start(bf16[4,144,2048]{2,1,0:T(8,128)(2,1)} %bitcast.224), calls=%async_computation.11 | async-start | bytes 4718592 | tf_op jit(solution)/shard_map/all_to_all | solution.py:81
  (64 other events, 509.4 us)
Sparse Core Ops, SparseCore 0:
  10.2 61.6 all-gather.5
  74.1 57.3 all-gather.7
  164.1 76.4 all-gather.9
  309.9 45.6 all-gather.11
  394.1 64.5 reduce-scatter.1
  498.4 54.7 all-gather.13

commit v2 on v1

--- a/solution.py
+++ b/solution.py
@@ -158,11 +158,16 @@
     acts, dys, marks = refs[:count], refs[count : count + 2], refs[count + 2 : 2 * count + 2]
     router_ref, place_ref = refs[2 * count + 2 : 2 * count + 4]
     weights_hbm = refs[2 * count + 4 : 2 * count + 7]
-    tail = refs[-20:]
-    act_all, dy_all, hid_all, dg_all, du_all, near, far = tail[:7]
-    act_b, dy_b, hid_b, dg_b, du_b, din_b, mark_b = tail[7:14]
-    gate_w, up_w, down_w = tail[14:17]
-    in_sem, w_sem, out_sem = tail[17:]
+    act_b, dy_b, hid_b, dg_b, du_b, din_b, mark_b = refs[-13:-6]
+    gate_w, up_w, down_w = refs[-6:-3]
+    in_sem, w_sem, out_sem = refs[-3:]
+    sizes = [min(2, count // 2)] + [1] * (count // 2 > 2)
+    outs = refs[-18 - 2 * len(sizes) : -13]
+    act_all, dy_all, hid_all, dg_all, du_all = outs[:5]
+    given, low_p = [], 0
+    for size, to in zip(sizes * 2, outs[5:]):
+        given.append((low_p, size, to))
+        low_p += size
     i = pl.program_id(0)
     width = act_b.shape[2]
     hidden = gate_w.shape[0]
@@ -254,13 +259,11 @@
         for copy in stores(p):
             copy.start()
 
-        @pl.when(p < count // 2)
-        def _():
-            give(p, p, near).start()
-
-        @pl.when(p >= count // 2)
-        def _():
-            give(p, p - count // 2, far).start()
+        for low_p, size, to in given:
+
+            @pl.when((p >= low_p) & (p < low_p + size))
+            def _(low_p=low_p, to=to):
+                give(p, p - low_p, to).start()
 
         return carry
 
@@ -268,7 +271,9 @@
     for p in range(count):
         for copy in stores(p):
             copy.wait()
-        give(p, p % (count // 2), (near, far)[p // (count // 2)]).wait()
+        for low_p, size, to in given:
+            if low_p <= p < low_p + size:
+                give(p, p - low_p, to).wait()
 
 
 def expert_pieces(first, where, acts, dys, marks, consts, held, total_rows):
@@ -287,7 +292,8 @@
     in_specs += [left] * 3
     out_shape = [jax.ShapeDtypeStruct((total_rows, width), bf16)] * 2
     out_shape += [jax.ShapeDtypeStruct((total_rows, hidden), bf16)] * 3
-    out_shape += [jax.ShapeDtypeStruct((count // 2, rows, width + routed), bf16)] * 2
+    sizes = [min(2, count // 2)] + [1] * (count // 2 > 2)
+    out_shape += [jax.ShapeDtypeStruct((size, rows, width + routed), bf16) for size in sizes * 2]
     args = [where, *acts, *dys, *([marks] * count), *consts]
     aliases = {}
     if held is not None:
@@ -301,7 +307,7 @@
             num_scalar_prefetch=1,
             grid=(rows // SLAB,),
             in_specs=in_specs,
-            out_specs=[left] * 7,
+            out_specs=[left] * len(out_shape),
             scratch_shapes=[pltpu.VMEM((count, SLAB, width), bf16)] * 2
             + [pltpu.VMEM((count, SLAB, hidden), bf16)] * 3
             + [pltpu.VMEM((count, SLAB, width + routed), bf16)]
@@ -584,16 +590,12 @@
 
     act1_cols = columns(act1_slice)
     w_or = jnp.concatenate([w_out, pad_cols(w_router, routed)], axis=1)
-    w_qkv, w_or, marks, act1, act1_cols, cosine, sine = after(
-        w_qkv, w_or, marks, act1, act1_cols, cosine, sine
+    dy_slice = lax.dynamic_slice(dy, (t * cut, 0), (cut, width))
+    w_qkv, w_or, marks, act1, act1_cols, cosine, sine, dy_tied = after(
+        w_qkv, w_or, marks, act1, act1_cols, cosine, sine, dy_slice
     )
     w_or = lax.all_gather(w_or, BC, axis=0, tiled=True)
-    dy_slice = lax.dynamic_slice(dy, (t * cut, 0), (cut, width))
-    dy_tied, w_or = after(dy_slice, w_or)
     dy_own = gather_c(dy_tied)
-    out_w = w_or[:, :q_cols]
-    router_wide = w_or[:, q_cols:]
-    router_w = router_wide[:, :experts]
     n_slab = piece_rows // SLAB
     groups = ((0,), 6 * piece_rows), ((1, 2, 3), 0)
     hidden = mine * w_gate.shape[1]
@@ -634,14 +636,16 @@
     probs_low = probs.astype(bf16).reshape(micro, heads * span, -1)
     mixed = bdot(probs_low, values, 2, 1).astype(bf16).reshape(micro, heads, span, hd)
     mixed = mixed.transpose(0, 2, 1, 3).reshape(rows, q_cols)
+    w_or, dy_own, mixed = after(w_or, dy_own, mixed)
+    dy_plane = lax.all_gather(dy_own, T, axis=0, tiled=True)
+    out_w = w_or[:, :q_cols]
+    router_wide = w_or[:, q_cols:]
     branch = sum_t_permute(nt(mixed, out_w))
     x_slice = lax.dynamic_slice(x, (t * cut, 0), (cut, width)).astype(f32)
     middle = x_slice + branch
     r2 = inv_rms(middle)
     act2 = (middle * r2 * norm_ffn).astype(bf16)
-    dy_own, act2 = after(dy_own, act2)
     act2_own = gather_c(act2)
-    dy_plane = lax.all_gather(dy_own, T, axis=0, tiled=True)
     mixed_later, act2_own, router_wide = after(mixed, act2_own, router_wide)
     mixed_all = lax.all_gather(mixed_later, BC, axis=0, tiled=True)
 
@@ -664,7 +668,7 @@
     low, high = across(from_x[:half], 2), across(from_y[half:], 1)
     corner = jnp.concatenate([low, high], axis=0)
     held, sums = experts_on((1, 2, 3), 0, [from_x, from_y, corner], [dy_plane, swap(dy_plane)], held)
-    ring_sums, corner_sums = [v[:2] for v in sums], [v[2:] for v in sums]
+    ring_sums, corner_sums = sums[0::2], sums[1::2]
     act_all, dy_all, hid_gated, d_gate, d_up = held
     d_in_plane, (hid_later, act2_later) = sum_plane(
         own_sums, ring_sums, corner_sums, (hid_gated, act2)
@@ -682,14 +686,16 @@
     out_chip = add_low(out_near, swap(out_far)).reshape(-1, width)
     grad_up = tn(d_up, act_all)
     d_in_got, grad_up, out_chip = after(d_in_got, grad_up, out_chip)
-    out_plane = lax.psum_scatter(out_chip, T, scatter_dimension=0, tiled=True)
 
     d_norm, d_branch_slice, d_logits, gain_ffn = turn_back(
         experts, d_in_got, act2_later, middle, dy_slice, chosen, router_wide, norm_ffn[None]
     )
     d_branch = gather_t(d_branch_slice)
     grad_gate = tn(d_gate, act_all)
-    d_branch, grad_gate, act2_late, d_logits = after(d_branch, grad_gate, act2_later, d_logits)
+    d_branch, grad_gate, act2_late, d_logits, out_chip = after(
+        d_branch, grad_gate, act2_later, d_logits, out_chip
+    )
+    out_plane = lax.psum_scatter(out_chip, T, scatter_dimension=0, tiled=True)
     d_branch_cols = to_features(d_branch)
     devices = sources * nt_
     router_part = tn(act2_late, d_logits)[:, :experts]
@@ -698,8 +704,6 @@
     d_q, d_window, gain_q = attend_back(
         q.reshape(rows, q_cols), qkv, window, bias, d_mixed, cos_own, sin_own, norm_query[None]
     )
-    d_window, out_plane = after(d_window, out_plane)
-    out_sum = sum_c_permute(out_plane)
     d_kv = d_window.reshape(micro, back + 1, span, 2 * hd)
     d_kv_own = d_kv[:, back].reshape(rows, 2 * hd).astype(f32)
     for s in range(1, back + 1):
@@ -708,11 +712,12 @@
     d_k_raw, gain_k_rows = heads_back(k_raw, norm_key, cosine, sine, d_kv_own[:, :hd])
     gain_k = jnp.sum(gain_k_rows, axis=0)
     d_qkv = jnp.concatenate([d_q, d_k_raw.astype(bf16), d_kv_own[:, hd:].astype(bf16)], axis=1)
-    d_qkv, out_sum, d_branch_cols = after(d_qkv, out_sum, d_branch_cols)
+    d_qkv, d_branch_cols = after(d_qkv, d_branch_cols)
     late = lax.all_gather(d_qkv, BC, axis=0, tiled=True)
-    d_act1 = sum_t(nt(d_qkv, w_qkv))
-    d_norm1, gain1_rows = norm_back(x_slice, inv_rms(x_slice), norm_attn, d_act1)
-    gain_attn = jnp.sum(gain1_rows, axis=0)
+    d_act1_part = nt(d_qkv, w_qkv)
+    gain_attn = jnp.sum(d_act1_part * (xf * inv_rms(xf)), axis=0)
+    d_act1 = sum_t_permute(d_act1_part)
+    d_norm1, _ = norm_back(x_slice, inv_rms(x_slice), norm_attn, d_act1)
 
     pieces = [v.reshape(devices, -1) for v in (router_part, gain_attn, gain_ffn, gain_q, gain_k)]
     sizes = [v.shape[1] for v in pieces]
@@ -722,12 +727,15 @@
     lines = -(-flat.shape[1] // width)
     flat = pad_cols(flat, lines * width).reshape(lines, width)
     flat = jnp.pad(flat, ((0, -lines % 16), (0, 0)))
-    final = jnp.concatenate([branch + out_sum, d_norm + d_norm1, flat], axis=0).astype(bf16)
-    final, dy_all, mixed_all = after(final, dy_all, mixed_all)
+    final = jnp.concatenate([d_norm + d_norm1, flat], axis=0).astype(bf16)
+    final, out_plane, dy_all, mixed_all = after(final, out_plane, dy_all, mixed_all)
+    out_sum = sum_c_permute(out_plane)
     final = gather_t(final).astype(f32).reshape(nt_, -1, width)
-    hidden_out = final[:, :cut].reshape(rows, width) + xf
-    grad_in = final[:, cut : 2 * cut].reshape(rows, width) + dy.astype(f32)
-    flat = final[:, 2 * cut : 2 * cut + lines].reshape(nt_, lines * width)
+    grad_in = final[:, :cut].reshape(rows, width) + dy.astype(f32)
+    grad_qkv = tn(act1_cols, late)
+    hidden_out, grad_qkv = after(gather_t((branch + out_sum).astype(bf16)), grad_qkv)
+    hidden_out = hidden_out.astype(f32) + xf
+    flat = final[:, cut : cut + lines].reshape(nt_, lines * width)
     gains, start = [], 0
     for size in sizes:
         gains.append(flat[:, start : start + size].reshape(-1))
@@ -735,7 +743,6 @@
     grad_router = gains.pop(0).reshape(-1, experts)
     grad_down = tn(hid_gated, dy_all)
     grad_out_w = tn(d_branch_cols, mixed_all)
-    grad_qkv = tn(act1_cols, late)
     shape = hidden_in.shape
     return (
         hidden_out.reshape(shape),

time: 605 us -> 576 us (0.952)
  waiting for transfers between devices: 219 us -> 193 us
    all_to_all x2, waiting for transfers between devices: 21.4 us -> 49 us  [gather_c(): lax.all_to_all(jnp.concatenate([v] * count, axis=0), C, 0, 0, tiled=True)]
    all_to_all x3 -> x4, waiting for transfers between devices: 24.6 us -> 3.09 us  [gather_t(): lax.all_to_all(jnp.concatenate([v] * count, axis=0), T, 0, 0, tiled=True)]
    ppermute x2, waiting for transfers between devices: 0.01 us -> 14.8 us  [body(): lax.ppermute(piece, C, [(i + s, i) for i in range(nc - s)]).astype(f32)]
    ppermute x2, waiting for transfers between devices: 17.8 us -> 5.57 us  [body(): lax.ppermute(kv, C, [(i, i + s) for i in range(nc - s)])]
    all_to_all x1 -> x0, waiting for transfers between devices: 10.8 us -> none  [sum_t(): got = lax.all_to_all(v.astype(bf16), T, 0, 0, tiled=True)]
    all_to_all x2, waiting for transfers between devices: 19.3 us -> 9.09 us  [to_features(): return lax.all_to_all(v, BC, 1, 0, tiled=True)]
    ppermute x11 -> x14, waiting for transfers between devices: 71 us -> 62.8 us  [across(): return lax.ppermute(v, T, [(i, i ^ k) for i in range(lax.axis_size(T))])]
    all_gather x1, waiting for transfers between devices: 6.62 us -> 0.01 us  [body(): w_or = lax.all_gather(w_or, BC, axis=0, tiled=True)]
  transfers between devices with their start and end apart: 45 -> 48, of which waited for: 29 -> 27; matrix products, arithmetic and copies ran while one was open for 27% -> 29% of each run, Pallas kernels for 6% -> 6%
where the time goes in v2:
time: 576 us; the launch traced here: 568 us
  waiting for transfers between devices  193 us (34%)
  starting transfers between devices  93.7 us (16%)
  Pallas kernels  79.9 us (14%)
  other arithmetic  68.2 us (12%)
  matrix products  64.1 us (11%)
  local copies, waits for them, and re-layouts  54 us (9%)
  between operations  15.8 us (3%)
    ppermute x14, waiting for transfers between devices, across(): return lax.ppermute(v, T, [(i, i ^ k) for i in range(lax.axis_size(T))])  62.8 us
    pallas_call x2, Pallas kernels, expert_pieces(): pl.pallas_call(functools.partial(expert_kernel, count, first), grid_spec=...  60.7 us
    dot_general x11, matrix products, dot(): lax.dot_general(a, b, (((ca,), (cb,)), ((), ())), preferred_element_type=...  57 us
    all_to_all x2, waiting for transfers between devices, gather_c(): lax.all_to_all(jnp.concatenate([v] * count, axis=0), C, 0, 0, tiled=True)  49 us
    ppermute x3, waiting for transfers between devices, sum_c_permute(): lax.ppermute(block(k), C, [(i, (i + k) % count) for i in range(count)])  27.4 us
    unnamed x165, local copies, waits for them, and re-layouts  18.4 us
    ppermute x14, starting transfers between devices, across(): return lax.ppermute(v, T, [(i, i ^ k) for i in range(lax.axis_size(T))])  16.1 us
    all_to_all x4, starting transfers between devices, gather_t(): lax.all_to_all(jnp.concatenate([v] * count, axis=0), T, 0, 0, tiled=True)  15.2 us
  transfers between devices with their start and end apart: 48, of which 27 were waited for; matrix products, arithmetic and copies ran while one was open for 29% of the time, Pallas kernels for 6%

profile of v2, /device:TPU:8, one launch (start us, length us, event | category | flops | bytes accessed | tf_op | source)
XLA Modules:
  0.0 568.4 jit_solution(7500492752009053157)
XLA Ops:
  14.9 5.3 all-to-all-start
  26.9 6.6 %all-to-all-start.1 = ((bf16[64,8,256]{2,0,1:T(8,128)(2,1)}), bf16[64,8,256]{2,0,1:T(8,128)(2,1)S(1)}, u32[]{:S(2)}, u32[]{:S(2)}) async-start(bf16[64,8,256]{2,0,1:T(8,128)(2,1)} %bitcast.205), calls=%async_computation.1 | async-start | bytes 524288 | tf_op jit(solution)/shard_map/all_to_all | solution.py:133
  37.2 9.1 %all-to-all-done.1 = bf16[64,8,256]{2,0,1:T(8,128)(2,1)S(1)} async-done(((bf16[64,8,256]{2,0,1:T(8,128)(2,1)}), bf16[64,8,256]{2,0,1:T(8,128)(2,1)S(1)}, u32[]{:S(2)}, u32[]{:S(2)}) %all-to-all-start.1) | async-done | bytes 262176 | tf_op jit(solution)/shard_map/all_to_all | solution.py:133
  47.4 3.8 all-to-all-start.2
  51.2 12.4 %convert_reduce_fusion = f32[2048,128]{1,0:T(8,128)S(1)} fusion(s32[2048,8]{1,0:T(8,128)} %bitcast.244), kind=kLoop, calls=%fused_computation.2 | loop fusion | flops 6029312 | bytes 1114112 | tf_op jit(solution)/shard_map/reduce_sum | solution.py:569
  63.5 2.9 select_add_fusion.refs_4_.refs_5_.refs_8_.refs_9_.refs_10_.refs_11_.refs_12_.refs_13_
  67.5 4.4 all-gather.6.cloned.1.call-done
  75.1 4.6 add.372
  79.7 4.0 fusion.66.raw_ref
  85.7 6.2 %collective-permute-start = (bf16[256,256]{1,0:T(8,128)(2,1)}, bf16[256,256]{1,0:T(8,128)(2,1)}, u32[]{:S(2)}, u32[]{:S(2)}) collective-permute-start(bf16[256,256]{1,0:T(8,128)(2,1)} %pad_maximum_fusion.12), channel_id=1, source_target_pairs={{0,8},{4,12},{1,9},{5,13},{2,10},{6,14},{3,11},{7,15},{16,24},{20,... | collective-permute-start | bytes 393224 | tf_op jit(solution)/shard_map/ppermute | solution.py:612
  95.3 6.3 %all-to-all-start.3 = ((bf16[4,64,2048]{2,1,0:T(8,128)(2,1)}), bf16[4,64,2048]{2,1,0:T(8,128)(2,1)S(1)}, u32[]{:S(2)}, u32[]{:S(2)}) async-start(bf16[4,64,2048]{2,1,0:T(8,128)(2,1)} %bitcast.239), calls=%async_computation.3 | async-start | bytes 2097152 | tf_op jit(solution)/shard_map/all_to_all | solution.py:108
  104.2 5.6 collective-permute-done.1
  113.2 3.4 fusion.65
  116.6 4.8 fusion.15
  122.9 30.8 %all-to-all-done.3 = bf16[4,64,2048]{2,1,0:T(8,128)(2,1)S(1)} async-done(((bf16[4,64,2048]{2,1,0:T(8,128)(2,1)}), bf16[4,64,2048]{2,1,0:T(8,128)(2,1)S(1)}, u32[]{:S(2)}, u32[]{:S(2)}) %all-to-all-start.3) | async-done | bytes 1048608 | tf_op jit(solution)/shard_map/all_to_all | solution.py:108
  154.8 3.5 fusion.5
  161.9 5.7 collective-permute-done.2
  167.6 6.9 %collective-permute-done.3 = bf16[64,2048]{1,0:T(8,128)(2,1)S(1)} collective-permute-done((bf16[64,2048]{1,0:T(8,128)(2,1)S(1)}, bf16[64,2048]{1,0:T(8,128)(2,1)S(1)}, u32[]{:S(2)}, u32[]{:S(2)}) %collective-permute-start.3) | collective-permute-done | bytes 262176 | tf_op jit(solution)/shard_map/ppermute | solution.py:96
  174.5 3.2 collective-permute-done.4
  180.1 6.8 %all-to-all-start.4 = ((bf16[4,64,2048]{2,1,0:T(8,128)(2,1)}), bf16[4,64,2048]{2,1,0:T(8,128)(2,1)S(1)}, u32[]{:S(2)}, u32[]{:S(2)}) async-start(bf16[4,64,2048]{2,1,0:T(8,128)(2,1)} %bitcast.42), calls=%async_computation.4 | async-start | bytes 2097152 | tf_op jit(solution)/shard_map/all_to_all | solution.py:108
  189.0 18.1 %all-to-all-done.4 = bf16[4,64,2048]{2,1,0:T(8,128)(2,1)S(1)} async-done(((bf16[4,64,2048]{2,1,0:T(8,128)(2,1)}), bf16[4,64,2048]{2,1,0:T(8,128)(2,1)S(1)}, u32[]{:S(2)}, u32[]{:S(2)}) %all-to-all-start.4) | async-done | bytes 1048608 | tf_op jit(solution)/shard_map/all_to_all | solution.py:108
  211.4 17.7 %shard_map.281 = (bf16[2048,2048]{1,0:T(8,128)(2,1)}, bf16[2048,2048]{1,0:T(8,128)(2,1)}, bf16[2048,768]{1,0:T(8,128)(2,1)}, bf16[2048,768]{1,0:T(8,128)(2,1)}, ...) custom-call(s32[4]{0:T(128)} %pad_add_fusion.1.where_ref, ...), custom_call_target="tpu_custom_call" | custom-call | flops 1000 | bytes 1000 | tf_op jit(solution)/shard_map/pallas_call | solution.py:304
  229.1 9.4 %collective-permute-done.8.refs_0_ = bf16[256,2048]{1,0:T(8,128)(2,1)S(1)} collective-permute-done((bf16[256,2048]{1,0:T(8,128)(2,1)S(1)}, bf16[256,2048]{1,0:T(8,128)(2,1)S(1)}, u32[]{:S(2)}, u32[]{:S(2)}) %collective-permute-start.8) | collective-permute-done | bytes 1048608 | tf_op jit(solution)/shard_map/ppermute | solution.py:96
  242.4 10.6 %collective-permute-done.10 = bf16[128,2048]{1,0:T(8,128)(2,1)S(1)} collective-permute-done((bf16[128,2048]{1,0:T(8,128)(2,1)S(1)}, bf16[128,2048]{1,0:T(8,128)(2,1)S(1)}, u32[]{:S(2)}, u32[]{:S(2)}) %collective-permute-start.10) | collective-permute-done | bytes 524320 | tf_op jit(solution)/shard_map/ppermute | solution.py:96
  258.3 43.0 %shard_map.282 = (bf16[2048,2048]{1,0:T(8,128)(2,1)}, bf16[2048,2048]{1,0:T(8,128)(2,1)}, bf16[2048,768]{1,0:T(8,128)(2,1)}, bf16[2048,768]{1,0:T(8,128)(2,1)}, ...) custom-call(s32[12]{0:T(128)} %stack.76.where_ref, ...), custom_call_target="tpu_custom_call", output_to_operand_aliasing={{0}: (20, {}), {1}: (21, {}), {2}: (22, {}), {3}: (23, {}),... | custom-call | flops 1000 | bytes 1000 | tf_op jit(solution)/shard_map/pallas_call | solution.py:304
  308.9 12.6 %collective-permute-done.18 = bf16[128,2176]{1,0:T(8,128)(2,1)S(1)} collective-permute-done((bf16[128,2176]{1,0:T(8,128)(2,1)S(1)}, bf16[128,2176]{1,0:T(8,128)(2,1)S(1)}, u32[]{:S(2)}, u32[]{:S(2)}) %collective-permute-start.18) | collective-permute-done | bytes 557088 | tf_op jit(solution)/shard_map/ppermute | solution.py:96
  329.6 9.2 %shard_map.283 = (bf16[4,256,2048]{2,1,0:T(8,128)(2,1)S(1)}, bf16[4,256,2048]{2,1,0:T(8,128)(2,1)S(1)}) custom-call(s32[12]{0:T(128)S(1)} %concatenate.100.where_ref, bf16[2048,768]{1,0:T(8,128)(2,1)S(1)} %copy-done.1, bf16[768,2048]{1,0:T(8,128)(2,1)S(1)} %bitcast.209), custom_call_target="tpu_custom_call" | custom-call | flops 1000 | bytes 1000 | tf_op jit(solution)/shard_map/pallas_call | solution.py:475
  342.9 6.7 %collective-permute-done.20 = bf16[256,2176]{1,0:T(8,128)(2,1)} collective-permute-done((bf16[256,2176]{1,0:T(8,128)(2,1)}, bf16[256,2176]{1,0:T(8,128)(2,1)}, u32[]{:S(2)}, u32[]{:S(2)}) %collective-permute-start.20) | collective-permute-done | bytes 1114144 | tf_op jit(solution)/shard_map/ppermute | solution.py:96
  352.0 3.5 fusion.11
  355.8 5.1 all-to-all-start.5
  360.9 11.9 %fusion.67 = f32[768,2048]{1,0:T(8,128)} fusion(bf16[2048,768]{1,0:T(8,128)(2,1)} %get-tuple-element.124, bf16[2048,2048]{1,0:T(8,128)(2,1)} %get-tuple-element.125), kind=kOutput, calls=%fused_computation.208 | convolution fusion | flops 6442450944 | bytes 17825792 | tf_op jit(solution)/shard_map/dot_general | solution.py:19
  372.9 6.2 %add_convert_fusion = bf16[4,256,2048]{2,1,0:T(8,128)(2,1)} fusion(bf16[4,256,2048]{2,1,0:T(8,128)(2,1)} %collective-permute-done.22, bf16[4,256,2048]{2,1,0:T(8,128)(2,1)S(1)} %copy-done.9), kind=kLoop, calls=%fused_computation.1 | loop fusion | flops 8388608 | bytes 12582912 | tf_op jit(solution)/shard_map/convert_element_type | solution.py:103
  379.1 6.4 %all-to-all-done.5.got_ref = bf16[4,64,2176]{2,1,0:T(8,128)(2,1)S(1)} async-done(((bf16[4,64,2176]{2,1,0:T(8,128)(2,1)}), bf16[4,64,2176]{2,1,0:T(8,128)(2,1)S(1)}, u32[]{:S(2)}, u32[]{:S(2)}) %all-to-all-start.5) | async-done | bytes 1114144 | tf_op jit(solution)/shard_map/all_to_all | solution.py:138
  387.6 3.5 all-to-all-start.6
  391.2 12.0 %fusion.68 = f32[768,2048]{1,0:T(8,128)} fusion(bf16[2048,768]{1,0:T(8,128)(2,1)} %get-tuple-element.132, bf16[2048,2048]{1,0:T(8,128)(2,1)} %get-tuple-element.125), kind=kOutput, calls=%fused_computation.209 | convolution fusion | flops 6442450944 | bytes 17825792 | tf_op jit(solution)/shard_map/dot_general | solution.py:19
  411.0 7.5 %all-to-all-start.7 = ((bf16[256,8,256]{0,2,1:T(8,128)(2,1)}), bf16[256,8,256]{0,2,1:T(8,128)(2,1)}, u32[]{:S(2)}, u32[]{:S(2)}) async-start(bf16[256,8,256]{0,2,1:T(8,128)(2,1)} %bitcast.75), calls=%async_computation.7 | async-start | bytes 2097152 | tf_op jit(solution)/shard_map/all_to_all | solution.py:133
  418.6 3.9 fusion.16.dm_ref
  422.5 8.9 %shard_map.285 = (bf16[256,1024]{1,0:T(8,128)(2,1)S(1)}, bf16[2,384,256]{2,1,0:T(8,128)(2,1)S(1)}, f32[1,128]{1,0:T(1,128)S(1)}) custom-call(bf16[256,1024]{1,0:T(8,128)(2,1)S(1)} %copy-done.16, f32[256,1280]{1,0:T(8,128)S(1)} %copy-done.5, bf16[2,384,256]{2,1,0:T(8,128)(2,1)S(1)} %bitcast.212, f32[2,128,384]{2,1,0:T(8,128)S(1)} %copy-done.13, ...), custom_call_target="tpu_custom_call" | custom-call | flops 1006632960 | bytes 2621440 | tf_op jit(solution)/shard_map/pallas_call | solution.py:375
  435.0 14.8 %collective-permute-done.23 = bf16[256,256]{1,0:T(8,128)(2,1)S(1)} collective-permute-done((bf16[256,256]{1,0:T(8,128)(2,1)S(1)}, bf16[256,256]{1,0:T(8,128)(2,1)S(1)}, u32[]{:S(2)}, u32[]{:S(2)}) %collective-permute-start.23) | collective-permute-done | bytes 131104 | tf_op jit(solution)/shard_map/ppermute | solution.py:711
  455.4 4.1 fusion.60
  466.8 6.0 %all-to-all-start.8 = ((bf16[32,2,1152]{2,1,0:T(2,128)(2,1)}), bf16[32,2,1152]{2,1,0:T(2,128)(2,1)S(1)}, u32[]{:S(2)}, u32[]{:S(2)}) async-start(bf16[32,2,1152]{2,1,0:T(2,128)(2,1)} %reshape.566), calls=%async_computation.8 | async-start | bytes 294912 | tf_op jit(solution)/shard_map/all_to_all | solution.py:725
  478.0 5.2 all-to-all-done.8
  487.7 3.1 collective-permute-start.29
  492.4 4.3 all-to-all-start.10
  496.8 11.0 %fusion.72 = f32[768,2048]{1,0:T(8,128)} fusion(bf16[2048,768]{1,0:T(8,128)(2,1)S(1)} %copy-done.2, bf16[2048,2048]{1,0:T(8,128)(2,1)} %get-tuple-element.155), kind=kOutput, calls=%fused_computation.213 | convolution fusion | flops 6442450944 | bytes 17825792 | tf_op jit(solution)/shard_map/dot_general | solution.py:19
  510.9 23.9 %collective-permute-done.29 = bf16[64,2048]{1,0:T(8,128)(2,1)} collective-permute-done((bf16[64,2048]{1,0:T(8,128)(2,1)}, bf16[64,2048]{1,0:T(8,128)(2,1)}, u32[]{:S(2)}, u32[]{:S(2)}) %collective-permute-start.29) | collective-permute-done | bytes 262176 | tf_op jit(solution)/shard_map/ppermute | solution.py:152
  540.2 3.5 all-to-all-start.9
  552.0 4.0 fusion.70
  (394 shorter events, 140.0 us)
Async XLA Ops:
  7.2 64.7 %all-gather.6.cloned.1.call-start = ((), (), s32[]{:S(2)}) async-start(), calls=%async_computation.12 | async-start | bytes 5898240 | tf_op jit(solution)/shard_map/all_gather | solution.py:544
  14.9 12.0 %all-to-all-start = ((s32[8,16,256]{2,1,0:T(8,128)}), s32[8,16,256]{2,1,0:T(8,128)S(1)}, u32[]{:S(2)}, u32[]{:S(2)}) async-start(s32[8,16,256]{2,1,0:T(8,128)} %bitcast.3), calls=%async_computation | async-start | bytes 262144 | tf_op jit(solution)/shard_map/all_to_all | solution.py:551
  26.9 19.4 %all-to-all-start.1 = ((bf16[64,8,256]{2,0,1:T(8,128)(2,1)}), bf16[64,8,256]{2,0,1:T(8,128)(2,1)S(1)}, u32[]{:S(2)}, u32[]{:S(2)}) async-start(bf16[64,8,256]{2,0,1:T(8,128)(2,1)} %bitcast.205), calls=%async_computation.1 | async-start | bytes 524288 | tf_op jit(solution)/shard_map/all_to_all | solution.py:133
  47.4 19.0 %all-to-all-start.2 = ((bf16[4,512,256]{2,1,0:T(8,128)(2,1)}), bf16[4,512,256]{2,1,0:T(8,128)(2,1)S(1)}, u32[]{:S(2)}, u32[]{:S(2)}) async-start(bf16[4,512,256]{2,1,0:T(8,128)(2,1)} %bitcast.14), calls=%async_computation.2 | async-start | bytes 2097152 | tf_op jit(solution)/shard_map/all_to_all | solution.py:81
  51.2 102.6 %all-gather.8.cloned.1.call-start = ((), (), s32[]{:S(2)}) async-start(), calls=%async_computation.13 | async-start | bytes 5308416 | tf_op jit(solution)/shard_map/all_gather | solution.py:597
  85.7 18.5 %collective-permute-start = (bf16[256,256]{1,0:T(8,128)(2,1)}, bf16[256,256]{1,0:T(8,128)(2,1)}, u32[]{:S(2)}, u32[]{:S(2)}) collective-permute-start(bf16[256,256]{1,0:T(8,128)(2,1)} %pad_maximum_fusion.12), channel_id=1, source_target_pairs={{0,8},{4,12},{1,9},{5,13},{2,10},{6,14},{3,11},{7,15},{16,24},{20,... | collective-permute-start | bytes 393224 | tf_op jit(solution)/shard_map/ppermute | solution.py:612
  91.9 17.8 %collective-permute-start.1 = (bf16[256,256]{1,0:T(8,128)(2,1)}, bf16[256,256]{1,0:T(8,128)(2,1)}, u32[]{:S(2)}, u32[]{:S(2)}) collective-permute-start(bf16[256,256]{1,0:T(8,128)(2,1)} %pad_maximum_fusion.12), channel_id=1, source_target_pairs={{0,4},{4,8},{8,12},{1,5},{5,9},{9,13},{2,6},{6,10},{10,14},{3,7},{... | collective-permute-start | bytes 393224 | tf_op jit(solution)/shard_map/ppermute | solution.py:612
  95.3 58.5 %all-to-all-start.3 = ((bf16[4,64,2048]{2,1,0:T(8,128)(2,1)}), bf16[4,64,2048]{2,1,0:T(8,128)(2,1)S(1)}, u32[]{:S(2)}, u32[]{:S(2)}) async-start(bf16[4,64,2048]{2,1,0:T(8,128)(2,1)} %bitcast.239), calls=%async_computation.3 | async-start | bytes 2097152 | tf_op jit(solution)/shard_map/all_to_all | solution.py:108
  101.6 137.0 %all-gather.10.cloned.1.call-start = ((), (), s32[]{:S(2)}) async-start(), calls=%async_computation.14 | async-start | bytes 5242880 | tf_op jit(solution)/shard_map/all_gather | solution.py:640
  158.4 9.2 %collective-permute-start.2 = (bf16[64,2048]{1,0:T(8,128)(2,1)S(1)}, bf16[64,2048]{1,0:T(8,128)(2,1)S(1)}, u32[]{:S(2)}, u32[]{:S(2)}) collective-permute-start(bf16[64,2048]{1,0:T(8,128)(2,1)S(1)} %get-tuple-element.265), channel_id=1, source_target_pairs={{0,1},{1,0},{2,3},{3,2},{4,5},{5,4},{6,7},{7,6},{8,9},{9,8},{10,11... | collective-permute-start | bytes 786440 | tf_op jit(solution)/shard_map/ppermute | solution.py:96
  160.1 14.3 %collective-permute-start.3 = (bf16[64,2048]{1,0:T(8,128)(2,1)S(1)}, bf16[64,2048]{1,0:T(8,128)(2,1)S(1)}, u32[]{:S(2)}, u32[]{:S(2)}) collective-permute-start(bf16[64,2048]{1,0:T(8,128)(2,1)S(1)} %get-tuple-element.267), channel_id=1, source_target_pairs={{0,2},{1,3},{2,0},{3,1},{4,6},{5,7},{6,4},{7,5},{8,10},{9,11},{10,... | collective-permute-start | bytes 786440 | tf_op jit(solution)/shard_map/ppermute | solution.py:96
  161.6 16.1 %collective-permute-start.4 = (bf16[64,2048]{1,0:T(8,128)(2,1)S(1)}, bf16[64,2048]{1,0:T(8,128)(2,1)S(1)}, u32[]{:S(2)}, u32[]{:S(2)}) collective-permute-start(bf16[64,2048]{1,0:T(8,128)(2,1)S(1)} %get-tuple-element.266), channel_id=1, source_target_pairs={{0,3},{1,2},{2,1},{3,0},{4,7},{5,6},{6,5},{7,4},{8,11},{9,10},{10,... | collective-permute-start | bytes 786440 | tf_op jit(solution)/shard_map/ppermute | solution.py:96
  180.1 27.0 %all-to-all-start.4 = ((bf16[4,64,2048]{2,1,0:T(8,128)(2,1)}), bf16[4,64,2048]{2,1,0:T(8,128)(2,1)S(1)}, u32[]{:S(2)}, u32[]{:S(2)}) async-start(bf16[4,64,2048]{2,1,0:T(8,128)(2,1)} %bitcast.42), calls=%async_computation.4 | async-start | bytes 2097152 | tf_op jit(solution)/shard_map/all_to_all | solution.py:108
  186.9 168.5 %all-gather.12.cloned.1.call-start = ((), (), s32[]{:S(2)}) async-start(), calls=%async_computation.15 | async-start | bytes 4718592 | tf_op jit(solution)/shard_map/all_gather | solution.py:650
  189.0 22.4 %collective-permute-start.6 = (bf16[256,2048]{1,0:T(8,128)(2,1)S(1)}, bf16[256,2048]{1,0:T(8,128)(2,1)}, u32[]{:S(2)}, u32[]{:S(2)}) collective-permute-start(bf16[256,2048]{1,0:T(8,128)(2,1)S(1)} %bitcast.228), channel_id=1, source_target_pairs={{0,16},{16,0},{1,17},{17,1},{2,18},{18,2},{3,19},{19,3},{4,20},{20... | collective-permute-start | bytes 3145736 | tf_op jit(solution)/shard_map/ppermute | solution.py:92
  207.1 4.3 collective-permute-start.5
  207.1 31.4 %collective-permute-start.8 = (bf16[256,2048]{1,0:T(8,128)(2,1)S(1)}, bf16[256,2048]{1,0:T(8,128)(2,1)S(1)}, u32[]{:S(2)}, u32[]{:S(2)}) collective-permute-start(bf16[256,2048]{1,0:T(8,128)(2,1)S(1)} %bitcast.236), channel_id=1, source_target_pairs={{0,1},{1,0},{2,3},{3,2},{4,5},{5,4},{6,7},{7,6},{8,9},{9,8},{10,11... | collective-permute-start | bytes 3145736 | tf_op jit(solution)/shard_map/ppermute | solution.py:96
  209.5 29.1 %collective-permute-start.9 = (bf16[256,2048]{1,0:T(8,128)(2,1)S(1)}, bf16[256,2048]{1,0:T(8,128)(2,1)}, u32[]{:S(2)}, u32[]{:S(2)}) collective-permute-start(bf16[256,2048]{1,0:T(8,128)(2,1)S(1)} %bitcast.237), channel_id=1, source_target_pairs={{0,2},{1,3},{2,0},{3,1},{4,6},{5,7},{6,4},{7,5},{8,10},{9,11},{10,... | collective-permute-start | bytes 3145736 | tf_op jit(solution)/shard_map/ppermute | solution.py:96
  238.6 19.7 %collective-permute-start.15 = (bf16[1024,2048]{1,0:T(8,128)(2,1)}, bf16[1024,2048]{1,0:T(8,128)(2,1)}, u32[]{:S(2)}, u32[]{:S(2)}) collective-permute-start(bf16[1024,2048]{1,0:T(8,128)(2,1)} %all-gather.10.cloned.1.call-done.refs_6_), channel_id=1, source_target_pairs={{0,16},{16,0},{1,17},{17,1},{2,18},{18,2},{3,19},{19,3},{4,20},{20... | collective-permute-start | bytes 12582920 | tf_op jit(solution)/shard_map/ppermute | solution.py:92
  238.8 14.3 %collective-permute-start.10 = (bf16[128,2048]{1,0:T(8,128)(2,1)S(1)}, bf16[128,2048]{1,0:T(8,128)(2,1)S(1)}, u32[]{:S(2)}, u32[]{:S(2)}) collective-permute-start(bf16[128,2048]{1,0:T(8,128)(2,1)S(1)} %slice.183), channel_id=1, source_target_pairs={{0,2},{1,3},{2,0},{3,1},{4,6},{5,7},{6,4},{7,5},{8,10},{9,11},{10,... | collective-permute-start | bytes 1572872 | tf_op jit(solution)/shard_map/ppermute | solution.py:96
  241.3 14.1 %collective-permute-start.11 = (bf16[128,2048]{1,0:T(8,128)(2,1)S(1)}, bf16[128,2048]{1,0:T(8,128)(2,1)S(1)}, u32[]{:S(2)}, u32[]{:S(2)}) collective-permute-start(bf16[128,2048]{1,0:T(8,128)(2,1)S(1)} %slice.184), channel_id=1, source_target_pairs={{0,1},{1,0},{2,3},{3,2},{4,5},{5,4},{6,7},{7,6},{8,9},{9,8},{10,11... | collective-permute-start | bytes 1572872 | tf_op jit(solution)/shard_map/ppermute | solution.py:96
  241.9 14.4 %collective-permute-start.12 = (bf16[256,2048]{1,0:T(8,128)(2,1)S(1)}, bf16[256,2048]{1,0:T(8,128)(2,1)S(1)}, u32[]{:S(2)}, u32[]{:S(2)}) collective-permute-start(bf16[256,2048]{1,0:T(8,128)(2,1)S(1)} %collective-permute-done.8.refs_0_), channel_id=1, source_target_pairs={{0,16},{16,0},{1,17},{17,1},{2,18},{18,2},{3,19},{19,3},{4,20},{20... | collective-permute-start | bytes 3145736 | tf_op jit(solution)/shard_map/ppermute | solution.py:92
  241.9 14.4 %collective-permute-start.13 = (bf16[256,2048]{1,0:T(8,128)(2,1)}, bf16[256,2048]{1,0:T(8,128)(2,1)}, u32[]{:S(2)}, u32[]{:S(2)}) collective-permute-start(bf16[256,2048]{1,0:T(8,128)(2,1)} %collective-permute-done.9.refs_1_), channel_id=1, source_target_pairs={{0,16},{16,0},{1,17},{17,1},{2,18},{18,2},{3,19},{19,3},{4,20},{20... | collective-permute-start | bytes 3145736 | tf_op jit(solution)/shard_map/ppermute | solution.py:92
  255.4 2.9 collective-permute-start.14
  301.2 3.4 collective-permute-start.17
  301.4 20.4 %collective-permute-start.16 = (bf16[2,256,2176]{2,1,0:T(8,128)(2,1)}, bf16[2,256,2176]{2,1,0:T(8,128)(2,1)S(1)}, u32[]{:S(2)}, u32[]{:S(2)}) collective-permute-start(bf16[2,256,2176]{2,1,0:T(8,128)(2,1)} %get-tuple-element.113), channel_id=1, source_target_pairs={{0,16},{16,0},{1,17},{17,1},{2,18},{18,2},{3,19},{19,3},{4,20},{20... | collective-permute-start | bytes 6684680 | tf_op jit(solution)/shard_map/ppermute | solution.py:92
  306.8 14.7 %collective-permute-start.18 = (bf16[128,2176]{1,0:T(8,128)(2,1)S(1)}, bf16[128,2176]{1,0:T(8,128)(2,1)S(1)}, u32[]{:S(2)}, u32[]{:S(2)}) collective-permute-start(bf16[128,2176]{1,0:T(8,128)(2,1)S(1)} %get-tuple-element.258), channel_id=1, source_target_pairs={{0,1},{1,0},{2,3},{3,2},{4,5},{5,4},{6,7},{7,6},{8,9},{9,8},{10,11... | collective-permute-start | bytes 1671176 | tf_op jit(solution)/shard_map/ppermute | solution.py:96
  307.5 14.4 %collective-permute-start.19 = (bf16[128,2176]{1,0:T(8,128)(2,1)S(1)}, bf16[128,2176]{1,0:T(8,128)(2,1)S(1)}, u32[]{:S(2)}, u32[]{:S(2)}) collective-permute-start(bf16[128,2176]{1,0:T(8,128)(2,1)S(1)} %get-tuple-element.257), channel_id=1, source_target_pairs={{0,2},{1,3},{2,0},{3,1},{4,6},{5,7},{6,4},{7,5},{8,10},{9,11},{10,... | collective-permute-start | bytes 1671176 | tf_op jit(solution)/shard_map/ppermute | solution.py:96
  308.9 34.0 %collective-permute-start.7 = (bf16[1,256,2176]{2,1,0:T(8,128)(2,1)}, bf16[1,256,2176]{2,1,0:T(8,128)(2,1)}, u32[]{:S(2)}, u32[]{:S(2)}) collective-permute-start(bf16[1,256,2176]{2,1,0:T(8,128)(2,1)} %get-tuple-element.98), channel_id=1, source_target_pairs={{0,16},{16,0},{1,17},{17,1},{2,18},{18,2},{3,19},{19,3},{4,20},{20... | collective-permute-start | bytes 3342344 | tf_op jit(solution)/shard_map/ppermute | solution.py:92
  323.7 25.9 %collective-permute-start.20 = (bf16[256,2176]{1,0:T(8,128)(2,1)}, bf16[256,2176]{1,0:T(8,128)(2,1)}, u32[]{:S(2)}, u32[]{:S(2)}) collective-permute-start(bf16[256,2176]{1,0:T(8,128)(2,1)} %pad_maximum_fusion.1), channel_id=1, source_target_pairs={{0,1},{1,0},{2,3},{3,2},{4,5},{5,4},{6,7},{7,6},{8,9},{9,8},{10,11... | collective-permute-start | bytes 3342344 | tf_op jit(solution)/shard_map/ppermute | solution.py:96
  326.4 25.6 %collective-permute-start.21 = (bf16[256,2176]{1,0:T(8,128)(2,1)}, bf16[256,2176]{1,0:T(8,128)(2,1)}, u32[]{:S(2)}, u32[]{:S(2)}) collective-permute-start(bf16[256,2176]{1,0:T(8,128)(2,1)} %pad_maximum_fusion.2), channel_id=1, source_target_pairs={{0,2},{1,3},{2,0},{3,1},{4,6},{5,7},{6,4},{7,5},{8,10},{9,11},{10,... | collective-permute-start | bytes 3342344 | tf_op jit(solution)/shard_map/ppermute | solution.py:96
  355.4 17.4 %collective-permute-start.22 = (bf16[4,256,2048]{2,1,0:T(8,128)(2,1)}, bf16[4,256,2048]{2,1,0:T(8,128)(2,1)}, u32[]{:S(2)}, u32[]{:S(2)}) collective-permute-start(bf16[4,256,2048]{2,1,0:T(8,128)(2,1)} %copy-done.19), channel_id=1, source_target_pairs={{0,16},{16,0},{1,17},{17,1},{2,18},{18,2},{3,19},{19,3},{4,20},{20... | collective-permute-start | bytes 12582920 | tf_op jit(solution)/shard_map/ppermute | solution.py:92
  355.8 29.7 %all-to-all-start.5 = ((bf16[4,64,2176]{2,1,0:T(8,128)(2,1)}), bf16[4,64,2176]{2,1,0:T(8,128)(2,1)S(1)}, u32[]{:S(2)}, u32[]{:S(2)}) async-start(bf16[4,64,2176]{2,1,0:T(8,128)(2,1)} %bitcast.234), calls=%async_computation.5 | async-start | bytes 2228224 | tf_op jit(solution)/shard_map/all_to_all | solution.py:138
  387.6 17.0 %all-to-all-start.6 = ((bf16[4,64,2048]{2,1,0:T(8,128)(2,1)}), bf16[4,64,2048]{2,1,0:T(8,128)(2,1)S(1)}, u32[]{:S(2)}, u32[]{:S(2)}) async-start(bf16[4,64,2048]{2,1,0:T(8,128)(2,1)} %bitcast.68), calls=%async_computation.6 | async-start | bytes 2097152 | tf_op jit(solution)/shard_map/all_to_all | solution.py:81
  391.2 92.6 %reduce-scatter.2.cloned.1.call-start = ((), (), s32[]{:S(2)}) async-start(), calls=%async_computation.16 | async-start | bytes 5242880 | tf_op jit(solution)/shard_map/reduce_scatter | solution.py:698
  411.0 40.3 %all-to-all-start.7 = ((bf16[256,8,256]{0,2,1:T(8,128)(2,1)}), bf16[256,8,256]{0,2,1:T(8,128)(2,1)}, u32[]{:S(2)}, u32[]{:S(2)}) async-start(bf16[256,8,256]{0,2,1:T(8,128)(2,1)} %bitcast.75), calls=%async_computation.7 | async-start | bytes 2097152 | tf_op jit(solution)/shard_map/all_to_all | solution.py:133
  418.5 133.5 %all-gather.14.cloned.1.call-start = ((), (), s32[]{:S(2)}) async-start(), calls=%async_computation.17 | async-start | bytes 5898240 | tf_op jit(solution)/shard_map/all_gather | solution.py:716
  431.5 18.3 %collective-permute-start.23 = (bf16[256,256]{1,0:T(8,128)(2,1)S(1)}, bf16[256,256]{1,0:T(8,128)(2,1)S(1)}, u32[]{:S(2)}, u32[]{:S(2)}) collective-permute-start(bf16[256,256]{1,0:T(8,128)(2,1)S(1)} %bitcast.268), channel_id=1, source_target_pairs={{4,0},{8,4},{12,8},{5,1},{9,5},{13,9},{6,2},{10,6},{14,10},{7,3},{... | collective-permute-start | bytes 393224 | tf_op jit(solution)/shard_map/ppermute | solution.py:711
  433.7 16.1 %collective-permute-start.24 = (bf16[256,256]{1,0:T(8,128)(2,1)S(1)}, bf16[256,256]{1,0:T(8,128)(2,1)S(1)}, u32[]{:S(2)}, u32[]{:S(2)}) collective-permute-start(bf16[256,256]{1,0:T(8,128)(2,1)S(1)} %bitcast.267), channel_id=1, source_target_pairs={{8,0},{12,4},{9,1},{13,5},{10,2},{14,6},{11,3},{15,7},{24,16},{28,... | collective-permute-start | bytes 393224 | tf_op jit(solution)/shard_map/ppermute | solution.py:711
  461.2 11.6 %collective-permute-start.25 = (bf16[64,2048]{1,0:T(8,128)(2,1)}, bf16[64,2048]{1,0:T(8,128)(2,1)S(1)}, u32[]{:S(2)}, u32[]{:S(2)}) collective-permute-start(bf16[64,2048]{1,0:T(8,128)(2,1)} %get-tuple-element.262), channel_id=1, source_target_pairs={{0,1},{1,0},{2,3},{3,2},{4,5},{5,4},{6,7},{7,6},{8,9},{9,8},{10,11... | collective-permute-start | bytes 786440 | tf_op jit(solution)/shard_map/ppermute | solution.py:96
  462.6 10.3 %collective-permute-start.26 = (bf16[64,2048]{1,0:T(8,128)(2,1)S(1)}, bf16[64,2048]{1,0:T(8,128)(2,1)S(1)}, u32[]{:S(2)}, u32[]{:S(2)}) collective-permute-start(bf16[64,2048]{1,0:T(8,128)(2,1)S(1)} %get-tuple-element.264), channel_id=1, source_target_pairs={{0,2},{1,3},{2,0},{3,1},{4,6},{5,7},{6,4},{7,5},{8,10},{9,11},{10,... | collective-permute-start | bytes 786440 | tf_op jit(solution)/shard_map/ppermute | solution.py:96
  463.2 12.3 %collective-permute-start.27 = (bf16[64,2048]{1,0:T(8,128)(2,1)S(1)}, bf16[64,2048]{1,0:T(8,128)(2,1)S(1)}, u32[]{:S(2)}, u32[]{:S(2)}) collective-permute-start(bf16[64,2048]{1,0:T(8,128)(2,1)S(1)} %get-tuple-element.263), channel_id=1, source_target_pairs={{0,3},{1,2},{2,1},{3,0},{4,7},{5,6},{6,5},{7,4},{8,11},{9,10},{10,... | collective-permute-start | bytes 786440 | tf_op jit(solution)/shard_map/ppermute | solution.py:96
  466.8 16.4 %all-to-all-start.8 = ((bf16[32,2,1152]{2,1,0:T(2,128)(2,1)}), bf16[32,2,1152]{2,1,0:T(2,128)(2,1)S(1)}, u32[]{:S(2)}, u32[]{:S(2)}) async-start(bf16[32,2,1152]{2,1,0:T(2,128)(2,1)} %reshape.566), calls=%async_computation.8 | async-start | bytes 294912 | tf_op jit(solution)/shard_map/all_to_all | solution.py:725
  485.8 25.1 %collective-permute-start.28 = (bf16[64,2048]{1,0:T(8,128)(2,1)}, bf16[64,2048]{1,0:T(8,128)(2,1)}, u32[]{:S(2)}, u32[]{:S(2)}) collective-permute-start(bf16[64,2048]{1,0:T(8,128)(2,1)} %get-tuple-element.259), channel_id=1, source_target_pairs={{0,4},{4,8},{8,12},{12,0},{1,5},{5,9},{9,13},{13,1},{2,6},{6,10},{... | collective-permute-start | bytes 786440 | tf_op jit(solution)/shard_map/ppermute | solution.py:152
  487.7 47.1 %collective-permute-start.29 = (bf16[64,2048]{1,0:T(8,128)(2,1)}, bf16[64,2048]{1,0:T(8,128)(2,1)}, u32[]{:S(2)}, u32[]{:S(2)}) collective-permute-start(bf16[64,2048]{1,0:T(8,128)(2,1)} %get-tuple-element.261), channel_id=1, source_target_pairs={{0,8},{4,12},{8,0},{12,4},{1,9},{5,13},{9,1},{13,5},{2,10},{6,14},... | collective-permute-start | bytes 786440 | tf_op jit(solution)/shard_map/ppermute | solution.py:152
  490.9 46.6 %collective-permute-start.30 = (bf16[64,2048]{1,0:T(8,128)(2,1)}, bf16[64,2048]{1,0:T(8,128)(2,1)}, u32[]{:S(2)}, u32[]{:S(2)}) collective-permute-start(bf16[64,2048]{1,0:T(8,128)(2,1)} %get-tuple-element.260), channel_id=1, source_target_pairs={{0,12},{4,0},{8,4},{12,8},{1,13},{5,1},{9,5},{13,9},{2,14},{6,2},{... | collective-permute-start | bytes 786440 | tf_op jit(solution)/shard_map/ppermute | solution.py:152
  492.4 47.7 %all-to-all-start.10 = ((bf16[4,80,2048]{2,1,0:T(8,128)(2,1)}), bf16[4,80,2048]{2,1,0:T(8,128)(2,1)}, u32[]{:S(2)}, u32[]{:S(2)}) async-start(bf16[4,80,2048]{2,1,0:T(8,128)(2,1)} %bitcast.233), calls=%async_computation.11 | async-start | bytes 2621440 | tf_op jit(solution)/shard_map/all_to_all | solution.py:81
  540.2 17.6 %all-to-all-start.9 = ((bf16[4,64,2048]{2,1,0:T(8,128)(2,1)}), bf16[4,64,2048]{2,1,0:T(8,128)(2,1)S(1)}, u32[]{:S(2)}, u32[]{:S(2)}) async-start(bf16[4,64,2048]{2,1,0:T(8,128)(2,1)} %bitcast.79), calls=%async_computation.10 | async-start | bytes 2097152 | tf_op jit(solution)/shard_map/all_to_all | solution.py:81
  (74 other events, 718.7 us)
Sparse Core Ops, SparseCore 0:
  10.2 61.6 all-gather.5
  74.1 78.5 all-gather.7
  155.1 66.5 all-gather.9
  302.0 45.6 all-gather.11
  404.8 53.5 reduce-scatter.1
  460.5 77.2 all-gather.13

commit v3 on v2

--- a/solution.py
+++ b/solution.py
@@ -118,15 +118,20 @@
 def sum_plane(own, ring, corner, held=()):
     diagonal = add_low(corner[0][0], swap(corner[1])[0])
     half = diagonal.shape[0] // 2
+    ring_far = swap(ring[1])
+    east = add_low(ring[0][0, :half], ring_far[0, :half])
+    north = add_low(ring[0][1, half:], ring_far[1, half:])
+    diagonal, east, north = after(diagonal, east, north)
     from_x, from_y = across(diagonal[:half], 1), across(diagonal[half:], 2)
-    ring_far = swap(ring[1])
+    east_top, north_low = across(east, 1), across(north, 2)
     own_far = swap(own[1])
-    from_x, from_y, *held = after(from_x, from_y, *held)
-    east = add_low(ring[0][0], ring_far[0])
-    north = add_low(ring[0][1], ring_far[1])
-    east = jnp.concatenate([east[:half], add_low(east[half:], from_y)], axis=0)
-    north = jnp.concatenate([add_low(north[:half], from_x), north[half:]], axis=0)
-    return add_low(own[0][0], own_far[0], across(east, 1), across(north, 2)), held
+    east = add_low(ring[0][0, half:], ring_far[0, half:], from_y)
+    north = add_low(ring[0][1, :half], ring_far[1, :half], from_x)
+    east, north, *held = after(east, north, *held)
+    east_low, north_top = across(east, 1), across(north, 2)
+    top = add_low(own[0][0, :half], own_far[0, :half], east_top, north_top)
+    low = add_low(own[0][0, half:], own_far[0, half:], east_low, north_low)
+    return jnp.concatenate([top, low], axis=0), held
 
 
 def to_features(v):
@@ -210,9 +215,6 @@
     def _():
         weights[2].start()
 
-    for p in range(1, count):
-        load(0, p).start()
-        load(1, p).start()
     for p in range(count):
         mark_b[p] = marks[p][0]
 
@@ -224,6 +226,13 @@
     def one(p, carry):
         for k, buffer in enumerate((act_b, dy_b)):
             pltpu.make_async_copy(acts[0].at[src], buffer.at[p], in_sem.at[k, p]).wait()
+        for q in range(1, count):
+
+            @pl.when(p == q - 1)
+            def _(q=q):
+                load(0, q).start()
+                load(1, q).start()
+
         act = act_b[p]
         mark = mark_b[p]
         logits = nn(act, router_ref[...])
@@ -585,10 +594,10 @@
     own_cols = width // sources
 
     def columns(v):
-        v = gather_t(to_features(v)).reshape(nt_, sources, cut, own_cols)
+        v = gather_t(v).reshape(nt_, sources, cut, own_cols)
         return v.transpose(1, 0, 2, 3).reshape(-1, own_cols)
 
-    act1_cols = columns(act1_slice)
+    act1_cols = columns(to_features(act1_slice))
     w_or = jnp.concatenate([w_out, pad_cols(w_router, routed)], axis=1)
     dy_slice = lax.dynamic_slice(dy, (t * cut, 0), (cut, width))
     w_qkv, w_or, marks, act1, act1_cols, cosine, sine, dy_tied = after(
@@ -692,15 +701,17 @@
     )
     d_branch = gather_t(d_branch_slice)
     grad_gate = tn(d_gate, act_all)
-    d_branch, grad_gate, act2_late, d_logits, out_chip = after(
-        d_branch, grad_gate, act2_later, d_logits, out_chip
+    d_branch, grad_gate, act2_late, d_logits, out_chip, d_branch_slice = after(
+        d_branch, grad_gate, act2_later, d_logits, out_chip, d_branch_slice
     )
     out_plane = lax.psum_scatter(out_chip, T, scatter_dimension=0, tiled=True)
-    d_branch_cols = to_features(d_branch)
+    d_branch_part = to_features(d_branch_slice)
     devices = sources * nt_
     router_part = tn(act2_late, d_logits)[:, :experts]
 
     d_mixed = nn(d_branch, out_w).astype(bf16)
+    d_mixed, d_branch_part = after(d_mixed, d_branch_part)
+    d_branch_cols = columns(d_branch_part)
     d_q, d_window, gain_q = attend_back(
         q.reshape(rows, q_cols), qkv, window, bias, d_mixed, cos_own, sin_own, norm_query[None]
     )
@@ -712,11 +723,10 @@
     d_k_raw, gain_k_rows = heads_back(k_raw, norm_key, cosine, sine, d_kv_own[:, :hd])
     gain_k = jnp.sum(gain_k_rows, axis=0)
     d_qkv = jnp.concatenate([d_q, d_k_raw.astype(bf16), d_kv_own[:, hd:].astype(bf16)], axis=1)
-    d_qkv, d_branch_cols = after(d_qkv, d_branch_cols)
     late = lax.all_gather(d_qkv, BC, axis=0, tiled=True)
     d_act1_part = nt(d_qkv, w_qkv)
     gain_attn = jnp.sum(d_act1_part * (xf * inv_rms(xf)), axis=0)
-    d_act1 = sum_t_permute(d_act1_part)
+    d_act1, d_branch_cols = after(sum_t_permute(d_act1_part), d_branch_cols)
     d_norm1, _ = norm_back(x_slice, inv_rms(x_slice), norm_attn, d_act1)
 
     pieces = [v.reshape(devices, -1) for v in (router_part, gain_attn, gain_ffn, gain_q, gain_k)]

time: 576 us -> 572 us (level)
  waiting for transfers between devices: 193 us -> 186 us
    ppermute x3, waiting for transfers between devices: 27.4 us -> 6.94 us  [sum_c_permute(): lax.ppermute(block(k), C, [(i, (i + k) % count) for i in range(count)])]
    ppermute x14 -> x16, waiting for transfers between devices: 62.8 us -> 79.4 us  [across(): return lax.ppermute(v, T, [(i, i ^ k) for i in range(lax.axis_size(T))])]
    ppermute x2, waiting for transfers between devices: 14.8 us -> 6.92 us  [body(): lax.ppermute(piece, C, [(i + s, i) for i in range(nc - s)]).astype(f32)]
    all_to_all x4 -> x5, starting transfers between devices: 15.2 us -> 19.2 us  [gather_t(): lax.all_to_all(jnp.concatenate([v] * count, axis=0), T, 0, 0, tiled=True)]
    ppermute x14 -> x16, starting transfers between devices: 16.1 us -> 18.3 us  [across(): return lax.ppermute(v, T, [(i, i ^ k) for i in range(lax.axis_size(T))])]
    convert_element_type x6 -> x5, other arithmetic: 12.4 us -> 12.8 us  [add_low(): return total.astype(bf16)]
    unnamed x165 -> x191, local copies, waits for them, and re-layouts: 18.4 us -> 18.2 us
  transfers between devices with their start and end apart: 48 -> 51, of which waited for: 27 -> 29; matrix products, arithmetic and copies ran while one was open for 29% -> 30% of each run, Pallas kernels for 6% -> 14%
where the time goes in v3:
time: 572 us; the launch traced here: 564 us
  waiting for transfers between devices  186 us (33%)
  starting transfers between devices  98.4 us (17%)
  Pallas kernels  78.3 us (14%)
  other arithmetic  67.6 us (12%)
  matrix products  66.2 us (12%)
  local copies, waits for them, and re-layouts  51.3 us (9%)
  between operations  15.9 us (3%)
    ppermute x16, waiting for transfers between devices, across(): return lax.ppermute(v, T, [(i, i ^ k) for i in range(lax.axis_size(T))])  79.4 us
    dot_general x11, matrix products, dot(): lax.dot_general(a, b, (((ca,), (cb,)), ((), ())), preferred_element_type=...  59.1 us
    pallas_call x2, Pallas kernels, expert_pieces(): pl.pallas_call(functools.partial(expert_kernel, count, first), grid_spec=...  59 us
    all_to_all x2, waiting for transfers between devices, gather_c(): lax.all_to_all(jnp.concatenate([v] * count, axis=0), C, 0, 0, tiled=True)  48.8 us
    all_to_all x5, starting transfers between devices, gather_t(): lax.all_to_all(jnp.concatenate([v] * count, axis=0), T, 0, 0, tiled=True)  19.2 us
    ppermute x16, starting transfers between devices, across(): return lax.ppermute(v, T, [(i, i ^ k) for i in range(lax.axis_size(T))])  18.3 us
    unnamed x191, local copies, waits for them, and re-layouts  18.2 us
    all_to_all x2, starting transfers between devices, to_features(): return lax.all_to_all(v, BC, 1, 0, tiled=True)  13.2 us
  transfers between devices with their start and end apart: 51, of which 29 were waited for; matrix products, arithmetic and copies ran while one was open for 30% of the time, Pallas kernels for 14%

profile of v3, /device:TPU:8, one launch (start us, length us, event | category | flops | bytes accessed | tf_op | source)
XLA Modules:
  0.0 563.9 jit_solution(15372189129809970078)
XLA Ops:
  14.9 5.3 all-to-all-start
  26.9 6.6 %all-to-all-start.1 = ((bf16[64,8,256]{2,0,1:T(8,128)(2,1)}), bf16[64,8,256]{2,0,1:T(8,128)(2,1)S(1)}, u32[]{:S(2)}, u32[]{:S(2)}) async-start(bf16[64,8,256]{2,0,1:T(8,128)(2,1)} %bitcast.215), calls=%async_computation.1 | async-start | bytes 524288 | tf_op jit(solution)/shard_map/all_to_all | solution.py:138
  37.2 9.1 %all-to-all-done.1 = bf16[64,8,256]{2,0,1:T(8,128)(2,1)S(1)} async-done(((bf16[64,8,256]{2,0,1:T(8,128)(2,1)}), bf16[64,8,256]{2,0,1:T(8,128)(2,1)S(1)}, u32[]{:S(2)}, u32[]{:S(2)}) %all-to-all-start.1) | async-done | bytes 262176 | tf_op jit(solution)/shard_map/all_to_all | solution.py:138
  47.4 3.8 all-to-all-start.2
  51.2 12.4 %convert_reduce_fusion = f32[2048,128]{1,0:T(8,128)S(1)} fusion(s32[2048,8]{1,0:T(8,128)} %bitcast.254), kind=kLoop, calls=%fused_computation.2 | loop fusion | flops 6029312 | bytes 1114112 | tf_op jit(solution)/shard_map/reduce_sum | solution.py:578
  67.4 4.5 all-gather.6.cloned.1.call-done
  75.1 4.6 add.396
  79.7 4.0 fusion.73.raw_ref
  85.7 6.2 %collective-permute-start = (bf16[256,256]{1,0:T(8,128)(2,1)}, bf16[256,256]{1,0:T(8,128)(2,1)}, u32[]{:S(2)}, u32[]{:S(2)}) collective-permute-start(bf16[256,256]{1,0:T(8,128)(2,1)} %pad_maximum_fusion.12), channel_id=1, source_target_pairs={{0,8},{4,12},{1,9},{5,13},{2,10},{6,14},{3,11},{7,15},{16,24},{20,... | collective-permute-start | bytes 393224 | tf_op jit(solution)/shard_map/ppermute | solution.py:621
  95.3 6.3 %all-to-all-start.3 = ((bf16[4,64,2048]{2,1,0:T(8,128)(2,1)}), bf16[4,64,2048]{2,1,0:T(8,128)(2,1)S(1)}, u32[]{:S(2)}, u32[]{:S(2)}) async-start(bf16[4,64,2048]{2,1,0:T(8,128)(2,1)} %bitcast.250), calls=%async_computation.3 | async-start | bytes 2097152 | tf_op jit(solution)/shard_map/all_to_all | solution.py:108
  104.3 5.5 collective-permute-done.1
  113.2 3.6 fusion.72
  116.7 4.9 fusion.13
  123.1 30.7 %all-to-all-done.3 = bf16[4,64,2048]{2,1,0:T(8,128)(2,1)S(1)} async-done(((bf16[4,64,2048]{2,1,0:T(8,128)(2,1)}), bf16[4,64,2048]{2,1,0:T(8,128)(2,1)S(1)}, u32[]{:S(2)}, u32[]{:S(2)}) %all-to-all-start.3) | async-done | bytes 1048608 | tf_op jit(solution)/shard_map/all_to_all | solution.py:108
  161.9 5.7 %collective-permute-done.2 = bf16[64,2048]{1,0:T(8,128)(2,1)S(1)} collective-permute-done((bf16[64,2048]{1,0:T(8,128)(2,1)S(1)}, bf16[64,2048]{1,0:T(8,128)(2,1)S(1)}, u32[]{:S(2)}, u32[]{:S(2)}) %collective-permute-start.2) | collective-permute-done | bytes 262176 | tf_op jit(solution)/shard_map/ppermute | solution.py:96
  167.6 6.9 %collective-permute-done.3 = bf16[64,2048]{1,0:T(8,128)(2,1)S(1)} collective-permute-done((bf16[64,2048]{1,0:T(8,128)(2,1)S(1)}, bf16[64,2048]{1,0:T(8,128)(2,1)S(1)}, u32[]{:S(2)}, u32[]{:S(2)}) %collective-permute-start.3) | collective-permute-done | bytes 262176 | tf_op jit(solution)/shard_map/ppermute | solution.py:96
  180.1 6.8 %all-to-all-start.4 = ((bf16[4,64,2048]{2,1,0:T(8,128)(2,1)}), bf16[4,64,2048]{2,1,0:T(8,128)(2,1)S(1)}, u32[]{:S(2)}, u32[]{:S(2)}) async-start(bf16[4,64,2048]{2,1,0:T(8,128)(2,1)} %bitcast.42), calls=%async_computation.4 | async-start | bytes 2097152 | tf_op jit(solution)/shard_map/all_to_all | solution.py:108
  189.0 18.1 %all-to-all-done.4 = bf16[4,64,2048]{2,1,0:T(8,128)(2,1)S(1)} async-done(((bf16[4,64,2048]{2,1,0:T(8,128)(2,1)}), bf16[4,64,2048]{2,1,0:T(8,128)(2,1)S(1)}, u32[]{:S(2)}, u32[]{:S(2)}) %all-to-all-start.4) | async-done | bytes 1048608 | tf_op jit(solution)/shard_map/all_to_all | solution.py:108
  211.4 17.7 %shard_map.281 = (bf16[2048,2048]{1,0:T(8,128)(2,1)}, bf16[2048,2048]{1,0:T(8,128)(2,1)}, bf16[2048,768]{1,0:T(8,128)(2,1)}, bf16[2048,768]{1,0:T(8,128)(2,1)}, ...) custom-call(s32[4]{0:T(128)} %pad_add_fusion.1.where_ref, ...), custom_call_target="tpu_custom_call" | custom-call | flops 1000 | bytes 1000 | tf_op jit(solution)/shard_map/pallas_call | solution.py:313
  229.1 9.4 %collective-permute-done.8.refs_0_ = bf16[256,2048]{1,0:T(8,128)(2,1)S(1)} collective-permute-done((bf16[256,2048]{1,0:T(8,128)(2,1)S(1)}, bf16[256,2048]{1,0:T(8,128)(2,1)S(1)}, u32[]{:S(2)}, u32[]{:S(2)}) %collective-permute-start.8) | collective-permute-done | bytes 1048608 | tf_op jit(solution)/shard_map/ppermute | solution.py:96
  242.4 10.6 %collective-permute-done.10 = bf16[128,2048]{1,0:T(8,128)(2,1)S(1)} collective-permute-done((bf16[128,2048]{1,0:T(8,128)(2,1)S(1)}, bf16[128,2048]{1,0:T(8,128)(2,1)S(1)}, u32[]{:S(2)}, u32[]{:S(2)}) %collective-permute-start.10) | collective-permute-done | bytes 524320 | tf_op jit(solution)/shard_map/ppermute | solution.py:96
  258.3 41.3 %shard_map.282 = (bf16[2048,2048]{1,0:T(8,128)(2,1)}, bf16[2048,2048]{1,0:T(8,128)(2,1)}, bf16[2048,768]{1,0:T(8,128)(2,1)}, bf16[2048,768]{1,0:T(8,128)(2,1)}, ...) custom-call(s32[12]{0:T(128)} %stack.76.where_ref, ...), custom_call_target="tpu_custom_call", output_to_operand_aliasing={{0}: (20, {}), {1}: (21, {}), {2}: (22, {}), {3}: (23, {}),... | custom-call | flops 1000 | bytes 1000 | tf_op jit(solution)/shard_map/pallas_call | solution.py:313
  300.2 5.6 %collective-permute-done.16 = bf16[1,256,2176]{2,1,0:T(8,128)(2,1)S(1)} collective-permute-done((bf16[1,256,2176]{2,1,0:T(8,128)(2,1)}, bf16[1,256,2176]{2,1,0:T(8,128)(2,1)S(1)}, u32[]{:S(2)}, u32[]{:S(2)}) %collective-permute-start.16) | collective-permute-done | bytes 1114144 | tf_op jit(solution)/shard_map/ppermute | solution.py:92
  312.9 11.4 %collective-permute-done.19 = bf16[128,2176]{1,0:T(8,128)(2,1)S(1)} collective-permute-done((bf16[128,2176]{1,0:T(8,128)(2,1)S(1)}, bf16[128,2176]{1,0:T(8,128)(2,1)S(1)}, u32[]{:S(2)}, u32[]{:S(2)}) %collective-permute-start.19) | collective-permute-done | bytes 557088 | tf_op jit(solution)/shard_map/ppermute | solution.py:96
  330.2 9.2 %shard_map.283 = (bf16[4,256,2048]{2,1,0:T(8,128)(2,1)S(1)}, bf16[4,256,2048]{2,1,0:T(8,128)(2,1)S(1)}) custom-call(s32[12]{0:T(128)S(1)} %concatenate.99.where_ref, bf16[2048,768]{1,0:T(8,128)(2,1)S(1)} %copy-done.1, bf16[768,2048]{1,0:T(8,128)(2,1)S(1)} %bitcast.219), custom_call_target="tpu_custom_call" | custom-call | flops 1000 | bytes 1000 | tf_op jit(solution)/shard_map/pallas_call | solution.py:484
  339.5 8.0 %collective-permute-done.21 = bf16[128,2176]{1,0:T(8,128)(2,1)} collective-permute-done((bf16[128,2176]{1,0:T(8,128)(2,1)}, bf16[128,2176]{1,0:T(8,128)(2,1)}, u32[]{:S(2)}, u32[]{:S(2)}) %collective-permute-start.21) | collective-permute-done | bytes 557088 | tf_op jit(solution)/shard_map/ppermute | solution.py:96
  351.6 5.1 all-to-all-start.5
  356.6 11.9 %fusion.74 = f32[768,2048]{1,0:T(8,128)} fusion(bf16[2048,768]{1,0:T(8,128)(2,1)} %get-tuple-element.133, bf16[2048,2048]{1,0:T(8,128)(2,1)} %get-tuple-element.134), kind=kOutput, calls=%fused_computation.211 | convolution fusion | flops 6442450944 | bytes 17825792 | tf_op jit(solution)/shard_map/dot_general | solution.py:19
  368.6 6.2 %add_convert_fusion = bf16[4,256,2048]{2,1,0:T(8,128)(2,1)} fusion(bf16[4,256,2048]{2,1,0:T(8,128)(2,1)} %collective-permute-done.24, bf16[4,256,2048]{2,1,0:T(8,128)(2,1)S(1)} %copy-done.9), kind=kLoop, calls=%fused_computation.1 | loop fusion | flops 8388608 | bytes 12582912 | tf_op jit(solution)/shard_map/convert_element_type | solution.py:103
  374.8 6.4 %all-to-all-done.5.got_ref = bf16[4,64,2176]{2,1,0:T(8,128)(2,1)S(1)} async-done(((bf16[4,64,2176]{2,1,0:T(8,128)(2,1)}), bf16[4,64,2176]{2,1,0:T(8,128)(2,1)S(1)}, u32[]{:S(2)}, u32[]{:S(2)}) %all-to-all-start.5) | async-done | bytes 1114144 | tf_op jit(solution)/shard_map/all_to_all | solution.py:143
  384.2 3.5 all-to-all-start.6
  387.8 12.0 %fusion.75 = f32[768,2048]{1,0:T(8,128)} fusion(bf16[2048,768]{1,0:T(8,128)(2,1)} %get-tuple-element.141, bf16[2048,2048]{1,0:T(8,128)(2,1)} %get-tuple-element.134), kind=kOutput, calls=%fused_computation.212 | convolution fusion | flops 6442450944 | bytes 17825792 | tf_op jit(solution)/shard_map/dot_general | solution.py:19
  407.0 6.6 %all-to-all-start.7 = ((bf16[64,8,256]{2,0,1:T(8,128)(2,1)}), bf16[64,8,256]{2,0,1:T(8,128)(2,1)S(1)}, u32[]{:S(2)}, u32[]{:S(2)}) async-start(bf16[64,8,256]{2,0,1:T(8,128)(2,1)} %bitcast.214), calls=%async_computation.7 | async-start | bytes 524288 | tf_op jit(solution)/shard_map/all_to_all | solution.py:138
  413.7 4.9 fusion.14.dm_ref
  422.4 8.9 %shard_map.285 = (bf16[256,1024]{1,0:T(8,128)(2,1)S(1)}, bf16[2,384,256]{2,1,0:T(8,128)(2,1)S(1)}, f32[1,128]{1,0:T(1,128)S(1)}) custom-call(bf16[256,1024]{1,0:T(8,128)(2,1)S(1)} %copy-done.18, f32[256,1280]{1,0:T(8,128)S(1)} %copy-done.5, bf16[2,384,256]{2,1,0:T(8,128)(2,1)S(1)} %bitcast.223, f32[2,128,384]{2,1,0:T(8,128)S(1)} %copy-done.13, ...), custom_call_target="tpu_custom_call" | custom-call | flops 1006632960 | bytes 2621440 | tf_op jit(solution)/shard_map/pallas_call | solution.py:384
  431.4 5.0 collective-permute-start.25
  437.7 3.7 collective-permute-done.25
  447.7 5.2 fusion.66
  455.1 4.6 all-to-all-start.9
  460.7 6.7 %all-to-all-done.9 = bf16[32,2,1152]{2,1,0:T(2,128)(2,1)S(1)} async-done(((bf16[32,2,1152]{2,1,0:T(2,128)(2,1)}), bf16[32,2,1152]{2,1,0:T(2,128)(2,1)S(1)}, u32[]{:S(2)}, u32[]{:S(2)}) %all-to-all-start.9) | async-done | bytes 147488 | tf_op jit(solution)/shard_map/all_to_all | solution.py:735
  467.4 3.7 all-to-all-start.8
  475.9 15.9 %collective-permute-done.27 = bf16[64,2048]{1,0:T(8,128)(2,1)S(1)} collective-permute-done((bf16[64,2048]{1,0:T(8,128)(2,1)S(1)}, bf16[64,2048]{1,0:T(8,128)(2,1)S(1)}, u32[]{:S(2)}, u32[]{:S(2)}) %collective-permute-start.27) | collective-permute-done | bytes 262176 | tf_op jit(solution)/shard_map/ppermute | solution.py:96
  491.8 5.3 collective-permute-done.29
  508.5 4.5 all-to-all-start.11
  513.0 11.0 %fusion.79 = f32[768,2048]{1,0:T(8,128)} fusion(bf16[2048,768]{1,0:T(8,128)(2,1)S(1)} %copy-done.2, bf16[2048,2048]{1,0:T(8,128)(2,1)} %get-tuple-element.167), kind=kOutput, calls=%fused_computation.216 | convolution fusion | flops 6442450944 | bytes 17825792 | tf_op jit(solution)/shard_map/dot_general | solution.py:19
  526.2 4.4 collective-permute-done.31
  535.9 3.7 all-to-all-start.10
  547.8 4.0 fusion.77
  (424 shorter events, 146.8 us)
Async XLA Ops:
  7.2 64.7 %all-gather.6.cloned.1.call-start = ((), (), s32[]{:S(2)}) async-start(), calls=%async_computation.13 | async-start | bytes 5898240 | tf_op jit(solution)/shard_map/all_gather | solution.py:553
  14.9 11.9 %all-to-all-start = ((s32[8,16,256]{2,1,0:T(8,128)}), s32[8,16,256]{2,1,0:T(8,128)S(1)}, u32[]{:S(2)}, u32[]{:S(2)}) async-start(s32[8,16,256]{2,1,0:T(8,128)} %bitcast.3), calls=%async_computation | async-start | bytes 262144 | tf_op jit(solution)/shard_map/all_to_all | solution.py:560
  26.9 19.4 %all-to-all-start.1 = ((bf16[64,8,256]{2,0,1:T(8,128)(2,1)}), bf16[64,8,256]{2,0,1:T(8,128)(2,1)S(1)}, u32[]{:S(2)}, u32[]{:S(2)}) async-start(bf16[64,8,256]{2,0,1:T(8,128)(2,1)} %bitcast.215), calls=%async_computation.1 | async-start | bytes 524288 | tf_op jit(solution)/shard_map/all_to_all | solution.py:138
  47.4 19.0 %all-to-all-start.2 = ((bf16[4,512,256]{2,1,0:T(8,128)(2,1)}), bf16[4,512,256]{2,1,0:T(8,128)(2,1)S(1)}, u32[]{:S(2)}, u32[]{:S(2)}) async-start(bf16[4,512,256]{2,1,0:T(8,128)(2,1)} %bitcast.14), calls=%async_computation.2 | async-start | bytes 2097152 | tf_op jit(solution)/shard_map/all_to_all | solution.py:81
  51.2 102.6 %all-gather.8.cloned.1.call-start = ((), (), s32[]{:S(2)}) async-start(), calls=%async_computation.14 | async-start | bytes 5308416 | tf_op jit(solution)/shard_map/all_gather | solution.py:606
  85.7 18.5 %collective-permute-start = (bf16[256,256]{1,0:T(8,128)(2,1)}, bf16[256,256]{1,0:T(8,128)(2,1)}, u32[]{:S(2)}, u32[]{:S(2)}) collective-permute-start(bf16[256,256]{1,0:T(8,128)(2,1)} %pad_maximum_fusion.12), channel_id=1, source_target_pairs={{0,8},{4,12},{1,9},{5,13},{2,10},{6,14},{3,11},{7,15},{16,24},{20,... | collective-permute-start | bytes 393224 | tf_op jit(solution)/shard_map/ppermute | solution.py:621
  91.9 17.8 %collective-permute-start.1 = (bf16[256,256]{1,0:T(8,128)(2,1)}, bf16[256,256]{1,0:T(8,128)(2,1)}, u32[]{:S(2)}, u32[]{:S(2)}) collective-permute-start(bf16[256,256]{1,0:T(8,128)(2,1)} %pad_maximum_fusion.12), channel_id=1, source_target_pairs={{0,4},{4,8},{8,12},{1,5},{5,9},{9,13},{2,6},{6,10},{10,14},{3,7},{... | collective-permute-start | bytes 393224 | tf_op jit(solution)/shard_map/ppermute | solution.py:621
  95.3 58.5 %all-to-all-start.3 = ((bf16[4,64,2048]{2,1,0:T(8,128)(2,1)}), bf16[4,64,2048]{2,1,0:T(8,128)(2,1)S(1)}, u32[]{:S(2)}, u32[]{:S(2)}) async-start(bf16[4,64,2048]{2,1,0:T(8,128)(2,1)} %bitcast.250), calls=%async_computation.3 | async-start | bytes 2097152 | tf_op jit(solution)/shard_map/all_to_all | solution.py:108
  101.6 137.0 %all-gather.10.cloned.1.call-start = ((), (), s32[]{:S(2)}) async-start(), calls=%async_computation.15 | async-start | bytes 5242880 | tf_op jit(solution)/shard_map/all_gather | solution.py:649
  158.4 9.2 %collective-permute-start.2 = (bf16[64,2048]{1,0:T(8,128)(2,1)S(1)}, bf16[64,2048]{1,0:T(8,128)(2,1)S(1)}, u32[]{:S(2)}, u32[]{:S(2)}) collective-permute-start(bf16[64,2048]{1,0:T(8,128)(2,1)S(1)} %get-tuple-element.267), channel_id=1, source_target_pairs={{0,1},{1,0},{2,3},{3,2},{4,5},{5,4},{6,7},{7,6},{8,9},{9,8},{10,11... | collective-permute-start | bytes 786440 | tf_op jit(solution)/shard_map/ppermute | solution.py:96
  160.1 14.3 %collective-permute-start.3 = (bf16[64,2048]{1,0:T(8,128)(2,1)S(1)}, bf16[64,2048]{1,0:T(8,128)(2,1)S(1)}, u32[]{:S(2)}, u32[]{:S(2)}) collective-permute-start(bf16[64,2048]{1,0:T(8,128)(2,1)S(1)} %get-tuple-element.269), channel_id=1, source_target_pairs={{0,2},{1,3},{2,0},{3,1},{4,6},{5,7},{6,4},{7,5},{8,10},{9,11},{10,... | collective-permute-start | bytes 786440 | tf_op jit(solution)/shard_map/ppermute | solution.py:96
  161.6 16.1 %collective-permute-start.4 = (bf16[64,2048]{1,0:T(8,128)(2,1)S(1)}, bf16[64,2048]{1,0:T(8,128)(2,1)S(1)}, u32[]{:S(2)}, u32[]{:S(2)}) collective-permute-start(bf16[64,2048]{1,0:T(8,128)(2,1)S(1)} %get-tuple-element.268), channel_id=1, source_target_pairs={{0,3},{1,2},{2,1},{3,0},{4,7},{5,6},{6,5},{7,4},{8,11},{9,10},{10,... | collective-permute-start | bytes 786440 | tf_op jit(solution)/shard_map/ppermute | solution.py:96
  180.1 27.0 %all-to-all-start.4 = ((bf16[4,64,2048]{2,1,0:T(8,128)(2,1)}), bf16[4,64,2048]{2,1,0:T(8,128)(2,1)S(1)}, u32[]{:S(2)}, u32[]{:S(2)}) async-start(bf16[4,64,2048]{2,1,0:T(8,128)(2,1)} %bitcast.42), calls=%async_computation.4 | async-start | bytes 2097152 | tf_op jit(solution)/shard_map/all_to_all | solution.py:108
  186.9 164.3 %all-gather.12.cloned.1.call-start = ((), (), s32[]{:S(2)}) async-start(), calls=%async_computation.16 | async-start | bytes 4718592 | tf_op jit(solution)/shard_map/all_gather | solution.py:659
  189.0 22.4 %collective-permute-start.6 = (bf16[256,2048]{1,0:T(8,128)(2,1)S(1)}, bf16[256,2048]{1,0:T(8,128)(2,1)}, u32[]{:S(2)}, u32[]{:S(2)}) collective-permute-start(bf16[256,2048]{1,0:T(8,128)(2,1)S(1)} %bitcast.239), channel_id=1, source_target_pairs={{0,16},{16,0},{1,17},{17,1},{2,18},{18,2},{3,19},{19,3},{4,20},{20... | collective-permute-start | bytes 3145736 | tf_op jit(solution)/shard_map/ppermute | solution.py:92
  207.1 31.4 %collective-permute-start.8 = (bf16[256,2048]{1,0:T(8,128)(2,1)S(1)}, bf16[256,2048]{1,0:T(8,128)(2,1)S(1)}, u32[]{:S(2)}, u32[]{:S(2)}) collective-permute-start(bf16[256,2048]{1,0:T(8,128)(2,1)S(1)} %bitcast.247), channel_id=1, source_target_pairs={{0,1},{1,0},{2,3},{3,2},{4,5},{5,4},{6,7},{7,6},{8,9},{9,8},{10,11... | collective-permute-start | bytes 3145736 | tf_op jit(solution)/shard_map/ppermute | solution.py:96
  209.5 29.1 %collective-permute-start.9 = (bf16[256,2048]{1,0:T(8,128)(2,1)S(1)}, bf16[256,2048]{1,0:T(8,128)(2,1)}, u32[]{:S(2)}, u32[]{:S(2)}) collective-permute-start(bf16[256,2048]{1,0:T(8,128)(2,1)S(1)} %bitcast.248), channel_id=1, source_target_pairs={{0,2},{1,3},{2,0},{3,1},{4,6},{5,7},{6,4},{7,5},{8,10},{9,11},{10,... | collective-permute-start | bytes 3145736 | tf_op jit(solution)/shard_map/ppermute | solution.py:96
  238.6 19.7 %collective-permute-start.15 = (bf16[1024,2048]{1,0:T(8,128)(2,1)}, bf16[1024,2048]{1,0:T(8,128)(2,1)}, u32[]{:S(2)}, u32[]{:S(2)}) collective-permute-start(bf16[1024,2048]{1,0:T(8,128)(2,1)} %all-gather.10.cloned.1.call-done.refs_6_), channel_id=1, source_target_pairs={{0,16},{16,0},{1,17},{17,1},{2,18},{18,2},{3,19},{19,3},{4,20},{20... | collective-permute-start | bytes 12582920 | tf_op jit(solution)/shard_map/ppermute | solution.py:92
  238.8 14.3 %collective-permute-start.10 = (bf16[128,2048]{1,0:T(8,128)(2,1)S(1)}, bf16[128,2048]{1,0:T(8,128)(2,1)S(1)}, u32[]{:S(2)}, u32[]{:S(2)}) collective-permute-start(bf16[128,2048]{1,0:T(8,128)(2,1)S(1)} %slice.183), channel_id=1, source_target_pairs={{0,2},{1,3},{2,0},{3,1},{4,6},{5,7},{6,4},{7,5},{8,10},{9,11},{10,... | collective-permute-start | bytes 1572872 | tf_op jit(solution)/shard_map/ppermute | solution.py:96
  241.3 14.1 %collective-permute-start.11 = (bf16[128,2048]{1,0:T(8,128)(2,1)S(1)}, bf16[128,2048]{1,0:T(8,128)(2,1)S(1)}, u32[]{:S(2)}, u32[]{:S(2)}) collective-permute-start(bf16[128,2048]{1,0:T(8,128)(2,1)S(1)} %slice.184), channel_id=1, source_target_pairs={{0,1},{1,0},{2,3},{3,2},{4,5},{5,4},{6,7},{7,6},{8,9},{9,8},{10,11... | collective-permute-start | bytes 1572872 | tf_op jit(solution)/shard_map/ppermute | solution.py:96
  241.9 14.4 %collective-permute-start.12 = (bf16[256,2048]{1,0:T(8,128)(2,1)S(1)}, bf16[256,2048]{1,0:T(8,128)(2,1)S(1)}, u32[]{:S(2)}, u32[]{:S(2)}) collective-permute-start(bf16[256,2048]{1,0:T(8,128)(2,1)S(1)} %collective-permute-done.8.refs_0_), channel_id=1, source_target_pairs={{0,16},{16,0},{1,17},{17,1},{2,18},{18,2},{3,19},{19,3},{4,20},{20... | collective-permute-start | bytes 3145736 | tf_op jit(solution)/shard_map/ppermute | solution.py:92
  241.9 14.4 %collective-permute-start.13 = (bf16[256,2048]{1,0:T(8,128)(2,1)}, bf16[256,2048]{1,0:T(8,128)(2,1)}, u32[]{:S(2)}, u32[]{:S(2)}) collective-permute-start(bf16[256,2048]{1,0:T(8,128)(2,1)} %collective-permute-done.9.refs_1_), channel_id=1, source_target_pairs={{0,16},{16,0},{1,17},{17,1},{2,18},{18,2},{3,19},{19,3},{4,20},{20... | collective-permute-start | bytes 3145736 | tf_op jit(solution)/shard_map/ppermute | solution.py:92
  299.6 7.8 %collective-permute-start.17 = (bf16[2,256,2176]{2,1,0:T(8,128)(2,1)}, bf16[2,256,2176]{2,1,0:T(8,128)(2,1)S(1)}, u32[]{:S(2)}, u32[]{:S(2)}) collective-permute-start(bf16[2,256,2176]{2,1,0:T(8,128)(2,1)} %get-tuple-element.121), channel_id=1, source_target_pairs={{0,16},{16,0},{1,17},{17,1},{2,18},{18,2},{3,19},{19,3},{4,20},{20... | collective-permute-start | bytes 6684680 | tf_op jit(solution)/shard_map/ppermute | solution.py:92
  308.7 15.5 %collective-permute-start.19 = (bf16[128,2176]{1,0:T(8,128)(2,1)S(1)}, bf16[128,2176]{1,0:T(8,128)(2,1)S(1)}, u32[]{:S(2)}, u32[]{:S(2)}) collective-permute-start(bf16[128,2176]{1,0:T(8,128)(2,1)S(1)} %get-tuple-element.260), channel_id=1, source_target_pairs={{0,2},{1,3},{2,0},{3,1},{4,6},{5,7},{6,4},{7,5},{8,10},{9,11},{10,... | collective-permute-start | bytes 1671176 | tf_op jit(solution)/shard_map/ppermute | solution.py:96
  309.3 15.5 %collective-permute-start.20 = (bf16[128,2176]{1,0:T(8,128)(2,1)S(1)}, bf16[128,2176]{1,0:T(8,128)(2,1)S(1)}, u32[]{:S(2)}, u32[]{:S(2)}) collective-permute-start(bf16[128,2176]{1,0:T(8,128)(2,1)S(1)} %get-tuple-element.259), channel_id=1, source_target_pairs={{0,1},{1,0},{2,3},{3,2},{4,5},{5,4},{6,7},{7,6},{8,9},{9,8},{10,11... | collective-permute-start | bytes 1671176 | tf_op jit(solution)/shard_map/ppermute | solution.py:96
  310.8 28.7 %collective-permute-start.7 = (bf16[1,256,2176]{2,1,0:T(8,128)(2,1)}, bf16[1,256,2176]{2,1,0:T(8,128)(2,1)}, u32[]{:S(2)}, u32[]{:S(2)}) collective-permute-start(bf16[1,256,2176]{2,1,0:T(8,128)(2,1)} %get-tuple-element.104), channel_id=1, source_target_pairs={{0,16},{16,0},{1,17},{17,1},{2,18},{18,2},{3,19},{19,3},{4,20},{20... | collective-permute-start | bytes 3342344 | tf_op jit(solution)/shard_map/ppermute | solution.py:92
  310.8 28.7 %collective-permute-start.18 = (bf16[128,2176]{1,0:T(8,128)(2,1)}, bf16[128,2176]{1,0:T(8,128)(2,1)}, u32[]{:S(2)}, u32[]{:S(2)}) collective-permute-start(bf16[128,2176]{1,0:T(8,128)(2,1)} %get-tuple-element.122), channel_id=1, source_target_pairs={{0,1},{1,0},{2,3},{3,2},{4,5},{5,4},{6,7},{7,6},{8,9},{9,8},{10,11... | collective-permute-start | bytes 1671176 | tf_op jit(solution)/shard_map/ppermute | solution.py:96
  311.4 28.2 %collective-permute-start.23 = (bf16[128,2176]{1,0:T(8,128)(2,1)}, bf16[128,2176]{1,0:T(8,128)(2,1)}, u32[]{:S(2)}, u32[]{:S(2)}) collective-permute-start(bf16[128,2176]{1,0:T(8,128)(2,1)} %get-tuple-element.127), channel_id=1, source_target_pairs={{0,2},{1,3},{2,0},{3,1},{4,6},{5,7},{6,4},{7,5},{8,10},{9,11},{10,... | collective-permute-start | bytes 1671176 | tf_op jit(solution)/shard_map/ppermute | solution.py:96
  326.2 21.4 %collective-permute-start.21 = (bf16[128,2176]{1,0:T(8,128)(2,1)}, bf16[128,2176]{1,0:T(8,128)(2,1)}, u32[]{:S(2)}, u32[]{:S(2)}) collective-permute-start(bf16[128,2176]{1,0:T(8,128)(2,1)} %get-tuple-element.125), channel_id=1, source_target_pairs={{0,2},{1,3},{2,0},{3,1},{4,6},{5,7},{6,4},{7,5},{8,10},{9,11},{10,... | collective-permute-start | bytes 1671176 | tf_op jit(solution)/shard_map/ppermute | solution.py:96
  327.7 20.0 %collective-permute-start.22 = (bf16[128,2176]{1,0:T(8,128)(2,1)}, bf16[128,2176]{1,0:T(8,128)(2,1)}, u32[]{:S(2)}, u32[]{:S(2)}) collective-permute-start(bf16[128,2176]{1,0:T(8,128)(2,1)} %get-tuple-element.126), channel_id=1, source_target_pairs={{0,1},{1,0},{2,3},{3,2},{4,5},{5,4},{6,7},{7,6},{8,9},{9,8},{10,11... | collective-permute-start | bytes 1671176 | tf_op jit(solution)/shard_map/ppermute | solution.py:96
  351.2 17.3 %collective-permute-start.24 = (bf16[4,256,2048]{2,1,0:T(8,128)(2,1)}, bf16[4,256,2048]{2,1,0:T(8,128)(2,1)}, u32[]{:S(2)}, u32[]{:S(2)}) collective-permute-start(bf16[4,256,2048]{2,1,0:T(8,128)(2,1)} %copy-done.24), channel_id=1, source_target_pairs={{0,16},{16,0},{1,17},{17,1},{2,18},{18,2},{3,19},{19,3},{4,20},{20... | collective-permute-start | bytes 12582920 | tf_op jit(solution)/shard_map/ppermute | solution.py:92
  351.6 29.6 %all-to-all-start.5 = ((bf16[4,64,2176]{2,1,0:T(8,128)(2,1)}), bf16[4,64,2176]{2,1,0:T(8,128)(2,1)S(1)}, u32[]{:S(2)}, u32[]{:S(2)}) async-start(bf16[4,64,2176]{2,1,0:T(8,128)(2,1)} %bitcast.245), calls=%async_computation.5 | async-start | bytes 2228224 | tf_op jit(solution)/shard_map/all_to_all | solution.py:143
  384.2 17.0 %all-to-all-start.6 = ((bf16[4,64,2048]{2,1,0:T(8,128)(2,1)}), bf16[4,64,2048]{2,1,0:T(8,128)(2,1)S(1)}, u32[]{:S(2)}, u32[]{:S(2)}) async-start(bf16[4,64,2048]{2,1,0:T(8,128)(2,1)} %bitcast.68), calls=%async_computation.6 | async-start | bytes 2097152 | tf_op jit(solution)/shard_map/all_to_all | solution.py:81
  387.7 114.0 %reduce-scatter.2.cloned.1.call-start = ((), (), s32[]{:S(2)}) async-start(), calls=%async_computation.17 | async-start | bytes 5242880 | tf_op jit(solution)/shard_map/reduce_scatter | solution.py:707
  407.0 12.9 %all-to-all-start.7 = ((bf16[64,8,256]{2,0,1:T(8,128)(2,1)}), bf16[64,8,256]{2,0,1:T(8,128)(2,1)S(1)}, u32[]{:S(2)}, u32[]{:S(2)}) async-start(bf16[64,8,256]{2,0,1:T(8,128)(2,1)} %bitcast.214), calls=%async_computation.7 | async-start | bytes 524288 | tf_op jit(solution)/shard_map/all_to_all | solution.py:138
  413.7 134.2 %all-gather.14.cloned.1.call-start = ((), (), s32[]{:S(2)}) async-start(), calls=%async_computation.18 | async-start | bytes 5898240 | tf_op jit(solution)/shard_map/all_gather | solution.py:726
  431.4 10.0 %collective-permute-start.25 = (bf16[256,256]{1,0:T(8,128)(2,1)S(1)}, bf16[256,256]{1,0:T(8,128)(2,1)S(1)}, u32[]{:S(2)}, u32[]{:S(2)}) collective-permute-start(bf16[256,256]{1,0:T(8,128)(2,1)S(1)} %bitcast.280), channel_id=1, source_target_pairs={{4,0},{8,4},{12,8},{5,1},{9,5},{13,9},{6,2},{10,6},{14,10},{7,3},{... | collective-permute-start | bytes 393224 | tf_op jit(solution)/shard_map/ppermute | solution.py:722
  436.4 8.2 %collective-permute-start.26 = (bf16[256,256]{1,0:T(8,128)(2,1)S(1)}, bf16[256,256]{1,0:T(8,128)(2,1)S(1)}, u32[]{:S(2)}, u32[]{:S(2)}) collective-permute-start(bf16[256,256]{1,0:T(8,128)(2,1)S(1)} %bitcast.279), channel_id=1, source_target_pairs={{8,0},{12,4},{9,1},{13,5},{10,2},{14,6},{11,3},{15,7},{24,16},{28,... | collective-permute-start | bytes 393224 | tf_op jit(solution)/shard_map/ppermute | solution.py:722
  455.1 12.3 %all-to-all-start.9 = ((bf16[32,2,1152]{2,1,0:T(2,128)(2,1)}), bf16[32,2,1152]{2,1,0:T(2,128)(2,1)S(1)}, u32[]{:S(2)}, u32[]{:S(2)}) async-start(bf16[32,2,1152]{2,1,0:T(2,128)(2,1)} %reshape.574), calls=%async_computation.9 | async-start | bytes 294912 | tf_op jit(solution)/shard_map/all_to_all | solution.py:735
  467.4 32.7 %all-to-all-start.8 = ((bf16[4,512,256]{2,1,0:T(8,128)(2,1)}), bf16[4,512,256]{2,1,0:T(8,128)(2,1)S(1)}, u32[]{:S(2)}, u32[]{:S(2)}) async-start(bf16[4,512,256]{2,1,0:T(8,128)(2,1)} %bitcast.77), calls=%async_computation.8 | async-start | bytes 2097152 | tf_op jit(solution)/shard_map/all_to_all | solution.py:81
  472.3 19.4 %collective-permute-start.27 = (bf16[64,2048]{1,0:T(8,128)(2,1)S(1)}, bf16[64,2048]{1,0:T(8,128)(2,1)S(1)}, u32[]{:S(2)}, u32[]{:S(2)}) collective-permute-start(bf16[64,2048]{1,0:T(8,128)(2,1)S(1)} %get-tuple-element.264), channel_id=1, source_target_pairs={{0,1},{1,0},{2,3},{3,2},{4,5},{5,4},{6,7},{7,6},{8,9},{9,8},{10,11... | collective-permute-start | bytes 786440 | tf_op jit(solution)/shard_map/ppermute | solution.py:96
  474.4 17.4 %collective-permute-start.28 = (bf16[64,2048]{1,0:T(8,128)(2,1)S(1)}, bf16[64,2048]{1,0:T(8,128)(2,1)}, u32[]{:S(2)}, u32[]{:S(2)}) collective-permute-start(bf16[64,2048]{1,0:T(8,128)(2,1)S(1)} %get-tuple-element.266), channel_id=1, source_target_pairs={{0,2},{1,3},{2,0},{3,1},{4,6},{5,7},{6,4},{7,5},{8,10},{9,11},{10,... | collective-permute-start | bytes 786440 | tf_op jit(solution)/shard_map/ppermute | solution.py:96
  475.9 21.2 %collective-permute-start.29 = (bf16[64,2048]{1,0:T(8,128)(2,1)S(1)}, bf16[64,2048]{1,0:T(8,128)(2,1)}, u32[]{:S(2)}, u32[]{:S(2)}) collective-permute-start(bf16[64,2048]{1,0:T(8,128)(2,1)S(1)} %get-tuple-element.265), channel_id=1, source_target_pairs={{0,3},{1,2},{2,1},{3,0},{4,7},{5,6},{6,5},{7,4},{8,11},{9,10},{10,... | collective-permute-start | bytes 786440 | tf_op jit(solution)/shard_map/ppermute | solution.py:96
  503.7 22.5 %collective-permute-start.30 = (bf16[64,2048]{1,0:T(8,128)(2,1)}, bf16[64,2048]{1,0:T(8,128)(2,1)}, u32[]{:S(2)}, u32[]{:S(2)}) collective-permute-start(bf16[64,2048]{1,0:T(8,128)(2,1)} %get-tuple-element.261), channel_id=1, source_target_pairs={{0,4},{4,8},{8,12},{12,0},{1,5},{5,9},{9,13},{13,1},{2,6},{6,10},{... | collective-permute-start | bytes 786440 | tf_op jit(solution)/shard_map/ppermute | solution.py:157
  503.7 26.8 %collective-permute-start.31 = (bf16[64,2048]{1,0:T(8,128)(2,1)}, bf16[64,2048]{1,0:T(8,128)(2,1)}, u32[]{:S(2)}, u32[]{:S(2)}) collective-permute-start(bf16[64,2048]{1,0:T(8,128)(2,1)} %get-tuple-element.263), channel_id=1, source_target_pairs={{0,8},{4,12},{8,0},{12,4},{1,9},{5,13},{9,1},{13,5},{2,10},{6,14},... | collective-permute-start | bytes 786440 | tf_op jit(solution)/shard_map/ppermute | solution.py:157
  507.2 26.0 %collective-permute-start.32 = (bf16[64,2048]{1,0:T(8,128)(2,1)}, bf16[64,2048]{1,0:T(8,128)(2,1)}, u32[]{:S(2)}, u32[]{:S(2)}) collective-permute-start(bf16[64,2048]{1,0:T(8,128)(2,1)} %get-tuple-element.262), channel_id=1, source_target_pairs={{0,12},{4,0},{8,4},{12,8},{1,13},{5,1},{9,5},{13,9},{2,14},{6,2},{... | collective-permute-start | bytes 786440 | tf_op jit(solution)/shard_map/ppermute | solution.py:157
  508.5 27.4 %all-to-all-start.11 = ((bf16[4,80,2048]{2,1,0:T(8,128)(2,1)}), bf16[4,80,2048]{2,1,0:T(8,128)(2,1)}, u32[]{:S(2)}, u32[]{:S(2)}) async-start(bf16[4,80,2048]{2,1,0:T(8,128)(2,1)} %bitcast.244), calls=%async_computation.12 | async-start | bytes 2621440 | tf_op jit(solution)/shard_map/all_to_all | solution.py:81
  535.9 17.4 %all-to-all-start.10 = ((bf16[4,64,2048]{2,1,0:T(8,128)(2,1)}), bf16[4,64,2048]{2,1,0:T(8,128)(2,1)S(1)}, u32[]{:S(2)}, u32[]{:S(2)}) async-start(bf16[4,64,2048]{2,1,0:T(8,128)(2,1)} %bitcast.82), calls=%async_computation.11 | async-start | bytes 2097152 | tf_op jit(solution)/shard_map/all_to_all | solution.py:81
  (90 other events, 866.1 us)
Sparse Core Ops, SparseCore 0:
  10.2 61.6 all-gather.5
  74.1 78.5 all-gather.7
  155.1 66.5 all-gather.9
  255.6 48.6 all-gather.11
  401.3 53.5 reduce-scatter.1
  457.1 56.5 all-gather.13

commit v4 on v3

--- a/solution.py
+++ b/solution.py
@@ -334,6 +334,51 @@
     return outs[:5], outs[5:]
 
 
+def attend_kernel(heads, scale, raw_ref, kv_ref, bias_ref, cos_ref, sin_ref, gain_ref, q_ref, mixed_ref):
+    hd = gain_ref.shape[1]
+    keys, values = kv_ref[0, :, :hd], kv_ref[0, :, hd:]
+    bias = bias_ref[0]
+    for h in range(heads):
+        cols = slice(h * hd, (h + 1) * hd)
+        raw = raw_ref[:, cols]
+        v = raw * inv_rms(raw) * gain_ref[...]
+        q = (v * cos_ref[...] + pltpu.roll(v, hd // 2, 1) * sin_ref[...]).astype(bf16)
+        q_ref[:, cols] = q
+        scores = nt(q, keys) * scale + bias
+        weight = jnp.exp(scores - jnp.max(scores, axis=1, keepdims=True))
+        probs = weight / jnp.sum(weight, axis=1, keepdims=True)
+        mixed_ref[:, cols] = nn(probs.astype(bf16), values).astype(bf16)
+
+
+def attend(qkv, q_cols, window, bias, cosine, sine, gain):
+    micro, reach, pair = window.shape
+    hd = pair // 2
+    span = qkv.shape[0] // micro
+    row = lambda m: (m, 0)
+    flat = lambda m: (0, 0)
+    deep = lambda m: (m, 0, 0)
+    return pl.pallas_call(
+        functools.partial(attend_kernel, q_cols // hd, hd ** (-0.5)),
+        grid=(micro,),
+        in_specs=[
+            pl.BlockSpec((span, q_cols), row),
+            pl.BlockSpec((1, reach, pair), deep),
+            pl.BlockSpec((1, span, reach), deep),
+            pl.BlockSpec((span, hd), flat),
+            pl.BlockSpec((span, hd), flat),
+            pl.BlockSpec((1, hd), flat),
+        ],
+        out_specs=[pl.BlockSpec((span, q_cols), row)] * 2,
+        out_shape=[jax.ShapeDtypeStruct((micro * span, q_cols), bf16)] * 2,
+        compiler_params=pltpu.CompilerParams(vmem_limit_bytes=32 << 20),
+        cost_estimate=pl.CostEstimate(
+            flops=4 * micro * span * reach * q_cols,
+            bytes_accessed=8 * micro * span * q_cols,
+            transcendentals=micro * span * reach * q_cols // hd,
+        ),
+    )(qkv, window, bias, cosine, sine, gain)
+
+
 def attend_back_kernel(heads, scale, q_ref, raw_ref, kv_ref, bias_ref, dm_ref, cos_ref, sin_ref, gain_ref, dq_ref, dkv_ref, gq_ref, rows_q, rows_m, rows_p, rows_s):
     span = q_ref.shape[0]
     hd = gain_ref.shape[1]
@@ -612,9 +657,7 @@
     up_w = w_up.reshape(hidden, width)
     down_w = w_down.reshape(hidden, width)
     qkv = nn(act1, w_qkv)
-    q_raw = qkv[:, :q_cols].reshape(rows, heads, hd)
     k_raw = qkv[:, q_cols : q_cols + hd]
-    q = heads_forward(q_raw, norm_query, cosine[:, None], sine[:, None])
     k = heads_forward(k_raw, norm_key, cosine, sine)
     kv = jnp.concatenate([k, qkv[:, q_cols + hd :].astype(bf16)], axis=1)
     blocks = [
@@ -622,7 +665,6 @@
     ]
     window = jnp.stack(blocks + [kv]).reshape(back + 1, micro, span, 2 * hd)
     window = window.transpose(1, 0, 2, 3).reshape(micro, (back + 1) * span, 2 * hd)
-    keys, values = window[..., :hd], window[..., hd:]
     seg_seq = lax.dynamic_index_in_dim(seg_all, b, 0, False)
     seg_seq = jnp.pad(seg_seq, ((back, 0), (0, 0), (0, 0)), constant_values=-1)
     seg_win = lax.dynamic_slice(seg_seq, (c, 0, 0), (back + 1, micro, span))
@@ -631,20 +673,10 @@
     allowed = (seg_own[:, :, None] == seg_win[:, None, :]) & (
         jnp.arange((back + 1) * span)[None, None, :] <= back * span + jnp.arange(span)[None, :, None]
     )
-    qg = q.reshape(micro, span, heads, hd).transpose(0, 2, 1, 3)
-    qg = qg.reshape(micro, heads * span, hd)
-    scores = bdot(qg, keys, 2, 2).reshape(micro, heads, span, -1) * scale
     bias = jnp.where(allowed, 0.0, -1e30)
     side = jnp.where(jnp.arange(hd) < hd // 2, -1.0, 1.0)
     cos_own, sin_own = cosine[:span], sine[:span] * side
-    scores = scores + bias[:, None]
-    top = jnp.max(scores, axis=-1, keepdims=True)
-    weight = jnp.exp(scores - top)
-    total = jnp.sum(weight, axis=-1, keepdims=True)
-    probs = weight / total
-    probs_low = probs.astype(bf16).reshape(micro, heads * span, -1)
-    mixed = bdot(probs_low, values, 2, 1).astype(bf16).reshape(micro, heads, span, hd)
-    mixed = mixed.transpose(0, 2, 1, 3).reshape(rows, q_cols)
+    q, mixed = attend(qkv, q_cols, window, bias, cos_own, sin_own, norm_query[None])
     w_or, dy_own, mixed = after(w_or, dy_own, mixed)
     dy_plane = lax.all_gather(dy_own, T, axis=0, tiled=True)
     out_w = w_or[:, :q_cols]
@@ -713,7 +745,7 @@
     d_mixed, d_branch_part = after(d_mixed, d_branch_part)
     d_branch_cols = columns(d_branch_part)
     d_q, d_window, gain_q = attend_back(
-        q.reshape(rows, q_cols), qkv, window, bias, d_mixed, cos_own, sin_own, norm_query[None]
+        q, qkv, window, bias, d_mixed, cos_own, sin_own, norm_query[None]
     )
     d_kv = d_window.reshape(micro, back + 1, span, 2 * hd)
     d_kv_own = d_kv[:, back].reshape(rows, 2 * hd).astype(f32)

time: 572 us -> 572 us (level)
  waiting for transfers between devices: 186 us -> 206 us
  other arithmetic: 67.6 us -> 55.2 us
  local copies, waits for them, and re-layouts: 51.3 us -> 42 us
  matrix products: 66.2 us -> 58.5 us
  Pallas kernels: 78.3 us -> 85.7 us
    ppermute x2, waiting for transfers between devices: 5.52 us -> 52.5 us  [body(): lax.ppermute(kv, C, [(i, i + s) for i in range(nc - s)])]
    all_to_all x2, waiting for transfers between devices: 48.8 us -> 15 us  [gather_c(): lax.all_to_all(jnp.concatenate([v] * count, axis=0), C, 0, 0, tiled=True)]
    pallas_call x0 -> x1, Pallas kernels: none -> 7.2 us  [attend(): pl.pallas_call(functools.partial(attend_kernel, q_cols // hd, hd ** (-0.5...]
    dot_general x2 -> x0, matrix products: 7.11 us -> none  [bdot(): lax.dot_general(a, b, (((ca,), (cb,)), ((0,), (0,))), preferred_element_t...]
    add x2 -> x0, local copies, waits for them, and re-layouts: 6.5 us -> none  [body(): scores = scores + bias[:, None]]
    unnamed x191 -> x148, local copies, waits for them, and re-layouts: 18.2 us -> 18.6 us
  transfers between devices with their start and end apart: 51 -> 51, of which waited for: 29 -> 30; matrix products, arithmetic and copies ran while one was open for 30% -> 24% of each run, Pallas kernels for 14% -> 15%
where the time goes in v4:
time: 572 us; the launch traced here: 562 us
  waiting for transfers between devices  206 us (36%)
  starting transfers between devices  99 us (17%)
  Pallas kernels  85.7 us (15%)
  matrix products  58.5 us (10%)
  other arithmetic  55.2 us (10%)
  local copies, waits for them, and re-layouts  42 us (7%)
  between operations  15.9 us (3%)
    ppermute x16, waiting for transfers between devices, across(): return lax.ppermute(v, T, [(i, i ^ k) for i in range(lax.axis_size(T))])  77.6 us
    pallas_call x2, Pallas kernels, expert_pieces(): pl.pallas_call(functools.partial(expert_kernel, count, first), grid_spec=...  59 us
    dot_general x11, matrix products, dot(): lax.dot_general(a, b, (((ca,), (cb,)), ((), ())), preferred_element_type=...  58.5 us
    ppermute x2, waiting for transfers between devices, body(): lax.ppermute(kv, C, [(i, i + s) for i in range(nc - s)])  52.5 us
    all_to_all x5, starting transfers between devices, gather_t(): lax.all_to_all(jnp.concatenate([v] * count, axis=0), T, 0, 0, tiled=True)  19.9 us
    unnamed x148, local copies, waits for them, and re-layouts  18.6 us
    ppermute x16, starting transfers between devices, across(): return lax.ppermute(v, T, [(i, i ^ k) for i in range(lax.axis_size(T))])  18.2 us
    all_to_all x2, waiting for transfers between devices, gather_c(): lax.all_to_all(jnp.concatenate([v] * count, axis=0), C, 0, 0, tiled=True)  15 us
  transfers between devices with their start and end apart: 51, of which 30 were waited for; matrix products, arithmetic and copies ran while one was open for 24% of the time, Pallas kernels for 15%

profile of v4, /device:TPU:8, one launch (start us, length us, event | category | flops | bytes accessed | tf_op | source)
XLA Modules:
  0.0 561.8 jit_solution(12263809859082262215)
XLA Ops:
  14.9 5.3 all-to-all-start
  26.3 7.2 %all-to-all-start.1 = ((bf16[64,8,256]{2,0,1:T(8,128)(2,1)}), bf16[64,8,256]{2,0,1:T(8,128)(2,1)S(1)}, u32[]{:S(2)}, u32[]{:S(2)}) async-start(bf16[64,8,256]{2,0,1:T(8,128)(2,1)} %bitcast.156), calls=%async_computation.1 | async-start | bytes 524288 | tf_op jit(solution)/shard_map/all_to_all | solution.py:138
  36.1 10.3 %all-to-all-done.1 = bf16[64,8,256]{2,0,1:T(8,128)(2,1)S(1)} async-done(((bf16[64,8,256]{2,0,1:T(8,128)(2,1)}), bf16[64,8,256]{2,0,1:T(8,128)(2,1)S(1)}, u32[]{:S(2)}, u32[]{:S(2)}) %all-to-all-start.1) | async-done | bytes 262176 | tf_op jit(solution)/shard_map/all_to_all | solution.py:138
  47.4 3.8 all-to-all-start.2
  51.2 12.4 %convert_reduce_fusion = f32[2048,128]{1,0:T(8,128)S(1)} fusion(s32[2048,8]{1,0:T(8,128)} %bitcast.188), kind=kLoop, calls=%fused_computation.1 | loop fusion | flops 6029312 | bytes 1114112 | tf_op jit(solution)/shard_map/reduce_sum | solution.py:623
  66.7 5.3 all-gather.6.cloned.1.call-done
  73.4 7.8 %all-to-all-start.3 = ((bf16[4,64,2048]{2,1,0:T(8,128)(2,1)}), bf16[4,64,2048]{2,1,0:T(8,128)(2,1)S(1)}, u32[]{:S(2)}, u32[]{:S(2)}) async-start(bf16[4,64,2048]{2,1,0:T(8,128)(2,1)} %bitcast.185), calls=%async_computation.3 | async-start | bytes 2097152 | tf_op jit(solution)/shard_map/all_to_all | solution.py:108
  81.2 4.5 fusion.59.raw_ref
  87.0 4.3 collective-permute-start
  93.2 45.9 %collective-permute-done = bf16[256,256]{1,0:T(8,128)(2,1)S(1)} collective-permute-done((bf16[256,256]{1,0:T(8,128)(2,1)S(1)}, bf16[256,256]{1,0:T(8,128)(2,1)S(1)}, u32[]{:S(2)}, u32[]{:S(2)}) %collective-permute-start) | collective-permute-done | bytes 131104 | tf_op jit(solution)/shard_map/ppermute | solution.py:664
  139.1 6.6 %collective-permute-done.1 = bf16[256,256]{1,0:T(8,128)(2,1)S(1)} collective-permute-done((bf16[256,256]{1,0:T(8,128)(2,1)S(1)}, bf16[256,256]{1,0:T(8,128)(2,1)S(1)}, u32[]{:S(2)}, u32[]{:S(2)}) %collective-permute-start.1) | collective-permute-done | bytes 131104 | tf_op jit(solution)/shard_map/ppermute | solution.py:664
  145.8 7.2 %shard_map.281 = (bf16[256,1024]{1,0:T(8,128)(2,1)S(1)}, bf16[256,1024]{1,0:T(8,128)(2,1)}) custom-call(f32[256,1280]{1,0:T(8,128)S(1)} %fusion.59.raw_ref, bf16[2,384,256]{2,1,0:T(8,128)(2,1)S(1)} %bitcast.160, f32[2,128,384]{2,1,0:T(8,128)S(1)} %and_select_fusion.bias_ref, f32[128,128]{1,0:T(8,128)S(1)} %slice.159.cos_ref, ...), custom_call_target="tpu_custom_call" | custom-call | flops 402653184 | bytes 2097152 | tf_op jit(solution)/shard_map/pallas_call | solution.py:360
  155.6 3.6 fusion.4
  162.9 7.0 %collective-permute-done.2 = bf16[64,2048]{1,0:T(8,128)(2,1)S(1)} collective-permute-done((bf16[64,2048]{1,0:T(8,128)(2,1)S(1)}, bf16[64,2048]{1,0:T(8,128)(2,1)S(1)}, u32[]{:S(2)}, u32[]{:S(2)}) %collective-permute-start.2) | collective-permute-done | bytes 262176 | tf_op jit(solution)/shard_map/ppermute | solution.py:96
  169.9 3.7 collective-permute-done.3
  173.6 5.4 collective-permute-done.4
  181.7 6.2 %all-to-all-start.4 = ((bf16[4,64,2048]{2,1,0:T(8,128)(2,1)}), bf16[4,64,2048]{2,1,0:T(8,128)(2,1)S(1)}, u32[]{:S(2)}, u32[]{:S(2)}) async-start(bf16[4,64,2048]{2,1,0:T(8,128)(2,1)} %bitcast.34), calls=%async_computation.4 | async-start | bytes 2097152 | tf_op jit(solution)/shard_map/all_to_all | solution.py:108
  190.2 15.0 %all-to-all-done.4 = bf16[4,64,2048]{2,1,0:T(8,128)(2,1)S(1)} async-done(((bf16[4,64,2048]{2,1,0:T(8,128)(2,1)}), bf16[4,64,2048]{2,1,0:T(8,128)(2,1)S(1)}, u32[]{:S(2)}, u32[]{:S(2)}) %all-to-all-start.4) | async-done | bytes 1048608 | tf_op jit(solution)/shard_map/all_to_all | solution.py:108
  209.5 17.7 %shard_map.282 = (bf16[2048,2048]{1,0:T(8,128)(2,1)}, bf16[2048,2048]{1,0:T(8,128)(2,1)}, bf16[2048,768]{1,0:T(8,128)(2,1)}, bf16[2048,768]{1,0:T(8,128)(2,1)}, ...) custom-call(s32[4]{0:T(128)} %pad_add_fusion.1.where_ref, ...), custom_call_target="tpu_custom_call" | custom-call | flops 1000 | bytes 1000 | tf_op jit(solution)/shard_map/pallas_call | solution.py:313
  227.2 9.0 %collective-permute-done.8.refs_0_ = bf16[256,2048]{1,0:T(8,128)(2,1)S(1)} collective-permute-done((bf16[256,2048]{1,0:T(8,128)(2,1)S(1)}, bf16[256,2048]{1,0:T(8,128)(2,1)S(1)}, u32[]{:S(2)}, u32[]{:S(2)}) %collective-permute-start.8) | collective-permute-done | bytes 1048608 | tf_op jit(solution)/shard_map/ppermute | solution.py:96
  240.2 10.6 %collective-permute-done.10 = bf16[128,2048]{1,0:T(8,128)(2,1)S(1)} collective-permute-done((bf16[128,2048]{1,0:T(8,128)(2,1)S(1)}, bf16[128,2048]{1,0:T(8,128)(2,1)S(1)}, u32[]{:S(2)}, u32[]{:S(2)}) %collective-permute-start.10) | collective-permute-done | bytes 524320 | tf_op jit(solution)/shard_map/ppermute | solution.py:96
  256.0 41.3 %shard_map.283 = (bf16[2048,2048]{1,0:T(8,128)(2,1)}, bf16[2048,2048]{1,0:T(8,128)(2,1)}, bf16[2048,768]{1,0:T(8,128)(2,1)}, bf16[2048,768]{1,0:T(8,128)(2,1)}, ...) custom-call(s32[12]{0:T(128)} %stack.76.where_ref, ...), custom_call_target="tpu_custom_call", output_to_operand_aliasing={{0}: (20, {}), {1}: (21, {}), {2}: (22, {}), {3}: (23, {}),... | custom-call | flops 1000 | bytes 1000 | tf_op jit(solution)/shard_map/pallas_call | solution.py:313
  298.0 5.6 %collective-permute-done.16 = bf16[1,256,2176]{2,1,0:T(8,128)(2,1)S(1)} collective-permute-done((bf16[1,256,2176]{2,1,0:T(8,128)(2,1)}, bf16[1,256,2176]{2,1,0:T(8,128)(2,1)S(1)}, u32[]{:S(2)}, u32[]{:S(2)}) %collective-permute-start.16) | collective-permute-done | bytes 1114144 | tf_op jit(solution)/shard_map/ppermute | solution.py:92
  310.6 11.4 %collective-permute-done.19 = bf16[128,2176]{1,0:T(8,128)(2,1)S(1)} collective-permute-done((bf16[128,2176]{1,0:T(8,128)(2,1)S(1)}, bf16[128,2176]{1,0:T(8,128)(2,1)S(1)}, u32[]{:S(2)}, u32[]{:S(2)}) %collective-permute-start.19) | collective-permute-done | bytes 557088 | tf_op jit(solution)/shard_map/ppermute | solution.py:96
  328.6 9.4 %shard_map.284 = (bf16[4,256,2048]{2,1,0:T(8,128)(2,1)S(1)}, bf16[4,256,2048]{2,1,0:T(8,128)(2,1)S(1)}) custom-call(s32[12]{0:T(128)S(1)} %concatenate.86.where_ref, bf16[2048,768]{1,0:T(8,128)(2,1)S(1)} %copy-done.1, bf16[768,2048]{1,0:T(8,128)(2,1)S(1)} %bitcast.159), custom_call_target="tpu_custom_call" | custom-call | flops 1000 | bytes 1000 | tf_op jit(solution)/shard_map/pallas_call | solution.py:529
  340.0 5.3 collective-permute-done.21
  349.3 5.1 all-to-all-start.5
  354.4 11.9 %fusion.60 = f32[768,2048]{1,0:T(8,128)} fusion(bf16[2048,768]{1,0:T(8,128)(2,1)} %get-tuple-element.136, bf16[2048,2048]{1,0:T(8,128)(2,1)} %get-tuple-element.137), kind=kOutput, calls=%fused_computation.181 | convolution fusion | flops 6442450944 | bytes 17825792 | tf_op jit(solution)/shard_map/dot_general | solution.py:19
  366.3 6.2 %add_convert_fusion = bf16[4,256,2048]{2,1,0:T(8,128)(2,1)} fusion(bf16[4,256,2048]{2,1,0:T(8,128)(2,1)} %collective-permute-done.24, bf16[4,256,2048]{2,1,0:T(8,128)(2,1)S(1)} %copy-done.7), kind=kLoop, calls=%fused_computation | loop fusion | flops 8388608 | bytes 12582912 | tf_op jit(solution)/shard_map/convert_element_type | solution.py:103
  372.5 6.4 %all-to-all-done.5.got_ref = bf16[4,64,2176]{2,1,0:T(8,128)(2,1)S(1)} async-done(((bf16[4,64,2176]{2,1,0:T(8,128)(2,1)}), bf16[4,64,2176]{2,1,0:T(8,128)(2,1)S(1)}, u32[]{:S(2)}, u32[]{:S(2)}) %all-to-all-start.5) | async-done | bytes 1114144 | tf_op jit(solution)/shard_map/all_to_all | solution.py:143
  381.9 3.5 all-to-all-start.6
  385.5 12.0 %fusion.61 = f32[768,2048]{1,0:T(8,128)} fusion(bf16[2048,768]{1,0:T(8,128)(2,1)} %get-tuple-element.145, bf16[2048,2048]{1,0:T(8,128)(2,1)} %get-tuple-element.137), kind=kOutput, calls=%fused_computation.182 | convolution fusion | flops 6442450944 | bytes 17825792 | tf_op jit(solution)/shard_map/dot_general | solution.py:19
  400.6 6.6 %all-to-all-start.7 = ((bf16[64,8,256]{2,0,1:T(8,128)(2,1)}), bf16[64,8,256]{2,0,1:T(8,128)(2,1)S(1)}, u32[]{:S(2)}, u32[]{:S(2)}) async-start(bf16[64,8,256]{2,0,1:T(8,128)(2,1)} %bitcast.155), calls=%async_computation.7 | async-start | bytes 524288 | tf_op jit(solution)/shard_map/all_to_all | solution.py:138
  407.2 4.7 fusion.11.dm_ref
  415.6 8.9 %shard_map.286 = (bf16[256,1024]{1,0:T(8,128)(2,1)S(1)}, bf16[2,384,256]{2,1,0:T(8,128)(2,1)S(1)}, f32[1,128]{1,0:T(1,128)S(1)}) custom-call(bf16[256,1024]{1,0:T(8,128)(2,1)S(1)} %copy-done.22, f32[256,1280]{1,0:T(8,128)S(1)} %copy-done.9, bf16[2,384,256]{2,1,0:T(8,128)(2,1)S(1)} %bitcast.161, f32[2,128,384]{2,1,0:T(8,128)S(1)} %copy-done.13, ...), custom_call_target="tpu_custom_call" | custom-call | flops 1006632960 | bytes 2621440 | tf_op jit(solution)/shard_map/pallas_call | solution.py:429
  424.6 5.0 collective-permute-start.25
  430.9 3.7 collective-permute-done.25
  440.9 4.1 fusion.53
  447.2 4.8 all-to-all-start.9
  453.1 6.7 %all-to-all-done.9 = bf16[32,2,1152]{2,1,0:T(2,128)(2,1)S(1)} async-done(((bf16[32,2,1152]{2,1,0:T(2,128)(2,1)}), bf16[32,2,1152]{2,1,0:T(2,128)(2,1)S(1)}, u32[]{:S(2)}, u32[]{:S(2)}) %all-to-all-start.9) | async-done | bytes 147488 | tf_op jit(solution)/shard_map/all_to_all | solution.py:767
  459.8 4.5 all-to-all-start.8
  468.0 16.9 %collective-permute-done.27 = bf16[64,2048]{1,0:T(8,128)(2,1)S(1)} collective-permute-done((bf16[64,2048]{1,0:T(8,128)(2,1)S(1)}, bf16[64,2048]{1,0:T(8,128)(2,1)S(1)}, u32[]{:S(2)}, u32[]{:S(2)}) %collective-permute-start.27) | collective-permute-done | bytes 262176 | tf_op jit(solution)/shard_map/ppermute | solution.py:96
  484.9 5.2 collective-permute-done.29
  501.2 4.4 all-to-all-start.11
  505.7 11.0 %fusion.65 = f32[768,2048]{1,0:T(8,128)} fusion(bf16[2048,768]{1,0:T(8,128)(2,1)S(1)} %copy-done.2, bf16[2048,2048]{1,0:T(8,128)(2,1)} %get-tuple-element.171), kind=kOutput, calls=%fused_computation.186 | convolution fusion | flops 6442450944 | bytes 17825792 | tf_op jit(solution)/shard_map/dot_general | solution.py:19
  518.9 9.3 %collective-permute-done.31 = bf16[64,2048]{1,0:T(8,128)(2,1)} collective-permute-done((bf16[64,2048]{1,0:T(8,128)(2,1)}, bf16[64,2048]{1,0:T(8,128)(2,1)}, u32[]{:S(2)}, u32[]{:S(2)}) %collective-permute-start.31) | collective-permute-done | bytes 262176 | tf_op jit(solution)/shard_map/ppermute | solution.py:157
  533.6 3.7 all-to-all-start.10
  545.5 4.0 fusion.63
  (364 shorter events, 125.4 us)
Async XLA Ops:
  7.2 64.7 %all-gather.6.cloned.1.call-start = ((), (), s32[]{:S(2)}) async-start(), calls=%async_computation.13 | async-start | bytes 5898240 | tf_op jit(solution)/shard_map/all_gather | solution.py:598
  14.9 11.3 %all-to-all-start = ((s32[8,16,256]{2,1,0:T(8,128)}), s32[8,16,256]{2,1,0:T(8,128)S(1)}, u32[]{:S(2)}, u32[]{:S(2)}) async-start(s32[8,16,256]{2,1,0:T(8,128)} %bitcast.3), calls=%async_computation | async-start | bytes 262144 | tf_op jit(solution)/shard_map/all_to_all | solution.py:605
  26.3 20.1 %all-to-all-start.1 = ((bf16[64,8,256]{2,0,1:T(8,128)(2,1)}), bf16[64,8,256]{2,0,1:T(8,128)(2,1)S(1)}, u32[]{:S(2)}, u32[]{:S(2)}) async-start(bf16[64,8,256]{2,0,1:T(8,128)(2,1)} %bitcast.156), calls=%async_computation.1 | async-start | bytes 524288 | tf_op jit(solution)/shard_map/all_to_all | solution.py:138
  47.4 18.2 %all-to-all-start.2 = ((bf16[4,512,256]{2,1,0:T(8,128)(2,1)}), bf16[4,512,256]{2,1,0:T(8,128)(2,1)S(1)}, u32[]{:S(2)}, u32[]{:S(2)}) async-start(bf16[4,512,256]{2,1,0:T(8,128)(2,1)} %bitcast.14), calls=%async_computation.2 | async-start | bytes 2097152 | tf_op jit(solution)/shard_map/all_to_all | solution.py:81
  51.2 103.4 %all-gather.8.cloned.1.call-start = ((), (), s32[]{:S(2)}) async-start(), calls=%async_computation.14 | async-start | bytes 5308416 | tf_op jit(solution)/shard_map/all_gather | solution.py:651
  73.4 81.2 %all-to-all-start.3 = ((bf16[4,64,2048]{2,1,0:T(8,128)(2,1)}), bf16[4,64,2048]{2,1,0:T(8,128)(2,1)S(1)}, u32[]{:S(2)}, u32[]{:S(2)}) async-start(bf16[4,64,2048]{2,1,0:T(8,128)(2,1)} %bitcast.185), calls=%async_computation.3 | async-start | bytes 2097152 | tf_op jit(solution)/shard_map/all_to_all | solution.py:108
  81.2 155.1 %all-gather.10.cloned.1.call-start = ((), (), s32[]{:S(2)}) async-start(), calls=%async_computation.15 | async-start | bytes 5242880 | tf_op jit(solution)/shard_map/all_gather | solution.py:681
  87.0 52.1 %collective-permute-start = (bf16[256,256]{1,0:T(8,128)(2,1)S(1)}, bf16[256,256]{1,0:T(8,128)(2,1)S(1)}, u32[]{:S(2)}, u32[]{:S(2)}) collective-permute-start(bf16[256,256]{1,0:T(8,128)(2,1)S(1)} %pad_maximum_fusion.12), channel_id=1, source_target_pairs={{0,8},{4,12},{1,9},{5,13},{2,10},{6,14},{3,11},{7,15},{16,24},{20,... | collective-permute-start | bytes 393224 | tf_op jit(solution)/shard_map/ppermute | solution.py:664
  91.3 54.5 %collective-permute-start.1 = (bf16[256,256]{1,0:T(8,128)(2,1)S(1)}, bf16[256,256]{1,0:T(8,128)(2,1)S(1)}, u32[]{:S(2)}, u32[]{:S(2)}) collective-permute-start(bf16[256,256]{1,0:T(8,128)(2,1)S(1)} %pad_maximum_fusion.12), channel_id=1, source_target_pairs={{0,4},{4,8},{8,12},{1,5},{5,9},{9,13},{2,6},{6,10},{10,14},{3,7},{... | collective-permute-start | bytes 393224 | tf_op jit(solution)/shard_map/ppermute | solution.py:664
  159.4 10.6 %collective-permute-start.2 = (bf16[64,2048]{1,0:T(8,128)(2,1)S(1)}, bf16[64,2048]{1,0:T(8,128)(2,1)S(1)}, u32[]{:S(2)}, u32[]{:S(2)}) collective-permute-start(bf16[64,2048]{1,0:T(8,128)(2,1)S(1)} %get-tuple-element.271), channel_id=1, source_target_pairs={{0,1},{1,0},{2,3},{3,2},{4,5},{5,4},{6,7},{7,6},{8,9},{9,8},{10,11... | collective-permute-start | bytes 786440 | tf_op jit(solution)/shard_map/ppermute | solution.py:96
  160.7 12.9 %collective-permute-start.3 = (bf16[64,2048]{1,0:T(8,128)(2,1)S(1)}, bf16[64,2048]{1,0:T(8,128)(2,1)S(1)}, u32[]{:S(2)}, u32[]{:S(2)}) collective-permute-start(bf16[64,2048]{1,0:T(8,128)(2,1)S(1)} %get-tuple-element.273), channel_id=1, source_target_pairs={{0,2},{1,3},{2,0},{3,1},{4,6},{5,7},{6,4},{7,5},{8,10},{9,11},{10,... | collective-permute-start | bytes 786440 | tf_op jit(solution)/shard_map/ppermute | solution.py:96
  162.2 16.8 %collective-permute-start.4 = (bf16[64,2048]{1,0:T(8,128)(2,1)S(1)}, bf16[64,2048]{1,0:T(8,128)(2,1)S(1)}, u32[]{:S(2)}, u32[]{:S(2)}) collective-permute-start(bf16[64,2048]{1,0:T(8,128)(2,1)S(1)} %get-tuple-element.272), channel_id=1, source_target_pairs={{0,3},{1,2},{2,1},{3,0},{4,7},{5,6},{6,5},{7,4},{8,11},{9,10},{10,... | collective-permute-start | bytes 786440 | tf_op jit(solution)/shard_map/ppermute | solution.py:96
  181.7 23.6 %all-to-all-start.4 = ((bf16[4,64,2048]{2,1,0:T(8,128)(2,1)}), bf16[4,64,2048]{2,1,0:T(8,128)(2,1)S(1)}, u32[]{:S(2)}, u32[]{:S(2)}) async-start(bf16[4,64,2048]{2,1,0:T(8,128)(2,1)} %bitcast.34), calls=%async_computation.4 | async-start | bytes 2097152 | tf_op jit(solution)/shard_map/all_to_all | solution.py:108
  187.9 161.1 %all-gather.12.cloned.1.call-start = ((), (), s32[]{:S(2)}) async-start(), calls=%async_computation.16 | async-start | bytes 4718592 | tf_op jit(solution)/shard_map/all_gather | solution.py:691
  190.2 19.2 %collective-permute-start.6 = (bf16[256,2048]{1,0:T(8,128)(2,1)S(1)}, bf16[256,2048]{1,0:T(8,128)(2,1)}, u32[]{:S(2)}, u32[]{:S(2)}) collective-permute-start(bf16[256,2048]{1,0:T(8,128)(2,1)S(1)} %bitcast.177), channel_id=1, source_target_pairs={{0,16},{16,0},{1,17},{17,1},{2,18},{18,2},{3,19},{19,3},{4,20},{20... | collective-permute-start | bytes 3145736 | tf_op jit(solution)/shard_map/ppermute | solution.py:92
  205.3 31.0 %collective-permute-start.8 = (bf16[256,2048]{1,0:T(8,128)(2,1)S(1)}, bf16[256,2048]{1,0:T(8,128)(2,1)S(1)}, u32[]{:S(2)}, u32[]{:S(2)}) collective-permute-start(bf16[256,2048]{1,0:T(8,128)(2,1)S(1)} %bitcast.182), channel_id=1, source_target_pairs={{0,1},{1,0},{2,3},{3,2},{4,5},{5,4},{6,7},{7,6},{8,9},{9,8},{10,11... | collective-permute-start | bytes 3145736 | tf_op jit(solution)/shard_map/ppermute | solution.py:96
  207.6 28.7 %collective-permute-start.9 = (bf16[256,2048]{1,0:T(8,128)(2,1)S(1)}, bf16[256,2048]{1,0:T(8,128)(2,1)}, u32[]{:S(2)}, u32[]{:S(2)}) collective-permute-start(bf16[256,2048]{1,0:T(8,128)(2,1)S(1)} %bitcast.183), channel_id=1, source_target_pairs={{0,2},{1,3},{2,0},{3,1},{4,6},{5,7},{6,4},{7,5},{8,10},{9,11},{10,... | collective-permute-start | bytes 3145736 | tf_op jit(solution)/shard_map/ppermute | solution.py:96
  236.3 19.7 %collective-permute-start.15 = (bf16[1024,2048]{1,0:T(8,128)(2,1)}, bf16[1024,2048]{1,0:T(8,128)(2,1)}, u32[]{:S(2)}, u32[]{:S(2)}) collective-permute-start(bf16[1024,2048]{1,0:T(8,128)(2,1)} %all-gather.10.cloned.1.call-done.refs_6_), channel_id=1, source_target_pairs={{0,16},{16,0},{1,17},{17,1},{2,18},{18,2},{3,19},{19,3},{4,20},{20... | collective-permute-start | bytes 12582920 | tf_op jit(solution)/shard_map/ppermute | solution.py:92
  236.5 14.3 %collective-permute-start.10 = (bf16[128,2048]{1,0:T(8,128)(2,1)S(1)}, bf16[128,2048]{1,0:T(8,128)(2,1)S(1)}, u32[]{:S(2)}, u32[]{:S(2)}) collective-permute-start(bf16[128,2048]{1,0:T(8,128)(2,1)S(1)} %slice.165), channel_id=1, source_target_pairs={{0,2},{1,3},{2,0},{3,1},{4,6},{5,7},{6,4},{7,5},{8,10},{9,11},{10,... | collective-permute-start | bytes 1572872 | tf_op jit(solution)/shard_map/ppermute | solution.py:96
  239.0 14.1 %collective-permute-start.11 = (bf16[128,2048]{1,0:T(8,128)(2,1)S(1)}, bf16[128,2048]{1,0:T(8,128)(2,1)S(1)}, u32[]{:S(2)}, u32[]{:S(2)}) collective-permute-start(bf16[128,2048]{1,0:T(8,128)(2,1)S(1)} %slice.166), channel_id=1, source_target_pairs={{0,1},{1,0},{2,3},{3,2},{4,5},{5,4},{6,7},{7,6},{8,9},{9,8},{10,11... | collective-permute-start | bytes 1572872 | tf_op jit(solution)/shard_map/ppermute | solution.py:96
  239.7 14.4 %collective-permute-start.12 = (bf16[256,2048]{1,0:T(8,128)(2,1)S(1)}, bf16[256,2048]{1,0:T(8,128)(2,1)S(1)}, u32[]{:S(2)}, u32[]{:S(2)}) collective-permute-start(bf16[256,2048]{1,0:T(8,128)(2,1)S(1)} %collective-permute-done.8.refs_0_), channel_id=1, source_target_pairs={{0,16},{16,0},{1,17},{17,1},{2,18},{18,2},{3,19},{19,3},{4,20},{20... | collective-permute-start | bytes 3145736 | tf_op jit(solution)/shard_map/ppermute | solution.py:92
  239.7 14.4 %collective-permute-start.13 = (bf16[256,2048]{1,0:T(8,128)(2,1)}, bf16[256,2048]{1,0:T(8,128)(2,1)}, u32[]{:S(2)}, u32[]{:S(2)}) collective-permute-start(bf16[256,2048]{1,0:T(8,128)(2,1)} %collective-permute-done.9.refs_1_), channel_id=1, source_target_pairs={{0,16},{16,0},{1,17},{17,1},{2,18},{18,2},{3,19},{19,3},{4,20},{20... | collective-permute-start | bytes 3145736 | tf_op jit(solution)/shard_map/ppermute | solution.py:92
  297.4 7.8 %collective-permute-start.17 = (bf16[2,256,2176]{2,1,0:T(8,128)(2,1)}, bf16[2,256,2176]{2,1,0:T(8,128)(2,1)S(1)}, u32[]{:S(2)}, u32[]{:S(2)}) collective-permute-start(bf16[2,256,2176]{2,1,0:T(8,128)(2,1)} %get-tuple-element.124), channel_id=1, source_target_pairs={{0,16},{16,0},{1,17},{17,1},{2,18},{18,2},{3,19},{19,3},{4,20},{20... | collective-permute-start | bytes 6684680 | tf_op jit(solution)/shard_map/ppermute | solution.py:92
  306.5 15.5 %collective-permute-start.19 = (bf16[128,2176]{1,0:T(8,128)(2,1)S(1)}, bf16[128,2176]{1,0:T(8,128)(2,1)S(1)}, u32[]{:S(2)}, u32[]{:S(2)}) collective-permute-start(bf16[128,2176]{1,0:T(8,128)(2,1)S(1)} %get-tuple-element.264), channel_id=1, source_target_pairs={{0,2},{1,3},{2,0},{3,1},{4,6},{5,7},{6,4},{7,5},{8,10},{9,11},{10,... | collective-permute-start | bytes 1671176 | tf_op jit(solution)/shard_map/ppermute | solution.py:96
  307.1 15.5 %collective-permute-start.20 = (bf16[128,2176]{1,0:T(8,128)(2,1)S(1)}, bf16[128,2176]{1,0:T(8,128)(2,1)S(1)}, u32[]{:S(2)}, u32[]{:S(2)}) collective-permute-start(bf16[128,2176]{1,0:T(8,128)(2,1)S(1)} %get-tuple-element.263), channel_id=1, source_target_pairs={{0,1},{1,0},{2,3},{3,2},{4,5},{5,4},{6,7},{7,6},{8,9},{9,8},{10,11... | collective-permute-start | bytes 1671176 | tf_op jit(solution)/shard_map/ppermute | solution.py:96
  308.5 31.5 %collective-permute-start.7 = (bf16[1,256,2176]{2,1,0:T(8,128)(2,1)}, bf16[1,256,2176]{2,1,0:T(8,128)(2,1)}, u32[]{:S(2)}, u32[]{:S(2)}) collective-permute-start(bf16[1,256,2176]{2,1,0:T(8,128)(2,1)} %get-tuple-element.107), channel_id=1, source_target_pairs={{0,16},{16,0},{1,17},{17,1},{2,18},{18,2},{3,19},{19,3},{4,20},{20... | collective-permute-start | bytes 3342344 | tf_op jit(solution)/shard_map/ppermute | solution.py:92
  308.5 31.5 %collective-permute-start.18 = (bf16[128,2176]{1,0:T(8,128)(2,1)}, bf16[128,2176]{1,0:T(8,128)(2,1)}, u32[]{:S(2)}, u32[]{:S(2)}) collective-permute-start(bf16[128,2176]{1,0:T(8,128)(2,1)} %get-tuple-element.125), channel_id=1, source_target_pairs={{0,1},{1,0},{2,3},{3,2},{4,5},{5,4},{6,7},{7,6},{8,9},{9,8},{10,11... | collective-permute-start | bytes 1671176 | tf_op jit(solution)/shard_map/ppermute | solution.py:96
  309.1 30.9 %collective-permute-start.23 = (bf16[128,2176]{1,0:T(8,128)(2,1)}, bf16[128,2176]{1,0:T(8,128)(2,1)}, u32[]{:S(2)}, u32[]{:S(2)}) collective-permute-start(bf16[128,2176]{1,0:T(8,128)(2,1)} %get-tuple-element.130), channel_id=1, source_target_pairs={{0,2},{1,3},{2,0},{3,1},{4,6},{5,7},{6,4},{7,5},{8,10},{9,11},{10,... | collective-permute-start | bytes 1671176 | tf_op jit(solution)/shard_map/ppermute | solution.py:96
  324.0 21.4 %collective-permute-start.21 = (bf16[128,2176]{1,0:T(8,128)(2,1)}, bf16[128,2176]{1,0:T(8,128)(2,1)}, u32[]{:S(2)}, u32[]{:S(2)}) collective-permute-start(bf16[128,2176]{1,0:T(8,128)(2,1)} %get-tuple-element.128), channel_id=1, source_target_pairs={{0,2},{1,3},{2,0},{3,1},{4,6},{5,7},{6,4},{7,5},{8,10},{9,11},{10,... | collective-permute-start | bytes 1671176 | tf_op jit(solution)/shard_map/ppermute | solution.py:96
  325.5 20.0 %collective-permute-start.22 = (bf16[128,2176]{1,0:T(8,128)(2,1)}, bf16[128,2176]{1,0:T(8,128)(2,1)}, u32[]{:S(2)}, u32[]{:S(2)}) collective-permute-start(bf16[128,2176]{1,0:T(8,128)(2,1)} %get-tuple-element.129), channel_id=1, source_target_pairs={{0,1},{1,0},{2,3},{3,2},{4,5},{5,4},{6,7},{7,6},{8,9},{9,8},{10,11... | collective-permute-start | bytes 1671176 | tf_op jit(solution)/shard_map/ppermute | solution.py:96
  349.0 17.3 %collective-permute-start.24 = (bf16[4,256,2048]{2,1,0:T(8,128)(2,1)}, bf16[4,256,2048]{2,1,0:T(8,128)(2,1)}, u32[]{:S(2)}, u32[]{:S(2)}) collective-permute-start(bf16[4,256,2048]{2,1,0:T(8,128)(2,1)} %copy-done.20), channel_id=1, source_target_pairs={{0,16},{16,0},{1,17},{17,1},{2,18},{18,2},{3,19},{19,3},{4,20},{20... | collective-permute-start | bytes 12582920 | tf_op jit(solution)/shard_map/ppermute | solution.py:92
  349.3 29.6 %all-to-all-start.5 = ((bf16[4,64,2176]{2,1,0:T(8,128)(2,1)}), bf16[4,64,2176]{2,1,0:T(8,128)(2,1)S(1)}, u32[]{:S(2)}, u32[]{:S(2)}) async-start(bf16[4,64,2176]{2,1,0:T(8,128)(2,1)} %bitcast.56), calls=%async_computation.5 | async-start | bytes 2228224 | tf_op jit(solution)/shard_map/all_to_all | solution.py:143
  381.9 17.0 %all-to-all-start.6 = ((bf16[4,64,2048]{2,1,0:T(8,128)(2,1)}), bf16[4,64,2048]{2,1,0:T(8,128)(2,1)S(1)}, u32[]{:S(2)}, u32[]{:S(2)}) async-start(bf16[4,64,2048]{2,1,0:T(8,128)(2,1)} %bitcast.59), calls=%async_computation.6 | async-start | bytes 2097152 | tf_op jit(solution)/shard_map/all_to_all | solution.py:81
  385.4 109.1 %reduce-scatter.2.cloned.1.call-start = ((), (), s32[]{:S(2)}) async-start(), calls=%async_computation.17 | async-start | bytes 5242880 | tf_op jit(solution)/shard_map/reduce_scatter | solution.py:739
  400.6 12.9 %all-to-all-start.7 = ((bf16[64,8,256]{2,0,1:T(8,128)(2,1)}), bf16[64,8,256]{2,0,1:T(8,128)(2,1)S(1)}, u32[]{:S(2)}, u32[]{:S(2)}) async-start(bf16[64,8,256]{2,0,1:T(8,128)(2,1)} %bitcast.155), calls=%async_computation.7 | async-start | bytes 524288 | tf_op jit(solution)/shard_map/all_to_all | solution.py:138
  407.2 138.3 %all-gather.14.cloned.1.call-start = ((), (), s32[]{:S(2)}) async-start(), calls=%async_computation.18 | async-start | bytes 5898240 | tf_op jit(solution)/shard_map/all_gather | solution.py:758
  424.6 10.1 %collective-permute-start.25 = (bf16[256,256]{1,0:T(8,128)(2,1)S(1)}, bf16[256,256]{1,0:T(8,128)(2,1)S(1)}, u32[]{:S(2)}, u32[]{:S(2)}) collective-permute-start(bf16[256,256]{1,0:T(8,128)(2,1)S(1)} %bitcast.206), channel_id=1, source_target_pairs={{4,0},{8,4},{12,8},{5,1},{9,5},{13,9},{6,2},{10,6},{14,10},{7,3},{... | collective-permute-start | bytes 393224 | tf_op jit(solution)/shard_map/ppermute | solution.py:754
  429.6 8.3 %collective-permute-start.26 = (bf16[256,256]{1,0:T(8,128)(2,1)S(1)}, bf16[256,256]{1,0:T(8,128)(2,1)S(1)}, u32[]{:S(2)}, u32[]{:S(2)}) collective-permute-start(bf16[256,256]{1,0:T(8,128)(2,1)S(1)} %bitcast.204), channel_id=1, source_target_pairs={{8,0},{12,4},{9,1},{13,5},{10,2},{14,6},{11,3},{15,7},{24,16},{28,... | collective-permute-start | bytes 393224 | tf_op jit(solution)/shard_map/ppermute | solution.py:754
  447.2 12.5 %all-to-all-start.9 = ((bf16[32,2,1152]{2,1,0:T(2,128)(2,1)}), bf16[32,2,1152]{2,1,0:T(2,128)(2,1)S(1)}, u32[]{:S(2)}, u32[]{:S(2)}) async-start(bf16[32,2,1152]{2,1,0:T(2,128)(2,1)} %reshape.501), calls=%async_computation.9 | async-start | bytes 294912 | tf_op jit(solution)/shard_map/all_to_all | solution.py:767
  459.8 31.9 %all-to-all-start.8 = ((bf16[4,512,256]{2,1,0:T(8,128)(2,1)}), bf16[4,512,256]{2,1,0:T(8,128)(2,1)}, u32[]{:S(2)}, u32[]{:S(2)}) async-start(bf16[4,512,256]{2,1,0:T(8,128)(2,1)} %bitcast.67), calls=%async_computation.8 | async-start | bytes 2097152 | tf_op jit(solution)/shard_map/all_to_all | solution.py:81
  464.4 20.5 %collective-permute-start.27 = (bf16[64,2048]{1,0:T(8,128)(2,1)S(1)}, bf16[64,2048]{1,0:T(8,128)(2,1)S(1)}, u32[]{:S(2)}, u32[]{:S(2)}) collective-permute-start(bf16[64,2048]{1,0:T(8,128)(2,1)S(1)} %get-tuple-element.268), channel_id=1, source_target_pairs={{0,1},{1,0},{2,3},{3,2},{4,5},{5,4},{6,7},{7,6},{8,9},{9,8},{10,11... | collective-permute-start | bytes 786440 | tf_op jit(solution)/shard_map/ppermute | solution.py:96
  466.5 18.5 %collective-permute-start.28 = (bf16[64,2048]{1,0:T(8,128)(2,1)S(1)}, bf16[64,2048]{1,0:T(8,128)(2,1)S(1)}, u32[]{:S(2)}, u32[]{:S(2)}) collective-permute-start(bf16[64,2048]{1,0:T(8,128)(2,1)S(1)} %get-tuple-element.270), channel_id=1, source_target_pairs={{0,2},{1,3},{2,0},{3,1},{4,6},{5,7},{6,4},{7,5},{8,10},{9,11},{10,... | collective-permute-start | bytes 786440 | tf_op jit(solution)/shard_map/ppermute | solution.py:96
  467.9 22.2 %collective-permute-start.29 = (bf16[64,2048]{1,0:T(8,128)(2,1)S(1)}, bf16[64,2048]{1,0:T(8,128)(2,1)S(1)}, u32[]{:S(2)}, u32[]{:S(2)}) collective-permute-start(bf16[64,2048]{1,0:T(8,128)(2,1)S(1)} %get-tuple-element.269), channel_id=1, source_target_pairs={{0,3},{1,2},{2,1},{3,0},{4,7},{5,6},{6,5},{7,4},{8,11},{9,10},{10,... | collective-permute-start | bytes 786440 | tf_op jit(solution)/shard_map/ppermute | solution.py:96
  496.5 22.4 %collective-permute-start.30 = (bf16[64,2048]{1,0:T(8,128)(2,1)}, bf16[64,2048]{1,0:T(8,128)(2,1)}, u32[]{:S(2)}, u32[]{:S(2)}) collective-permute-start(bf16[64,2048]{1,0:T(8,128)(2,1)} %get-tuple-element.265), channel_id=1, source_target_pairs={{0,4},{4,8},{8,12},{12,0},{1,5},{5,9},{9,13},{13,1},{2,6},{6,10},{... | collective-permute-start | bytes 786440 | tf_op jit(solution)/shard_map/ppermute | solution.py:157
  496.5 31.7 %collective-permute-start.31 = (bf16[64,2048]{1,0:T(8,128)(2,1)}, bf16[64,2048]{1,0:T(8,128)(2,1)}, u32[]{:S(2)}, u32[]{:S(2)}) collective-permute-start(bf16[64,2048]{1,0:T(8,128)(2,1)} %get-tuple-element.267), channel_id=1, source_target_pairs={{0,8},{4,12},{8,0},{12,4},{1,9},{5,13},{9,1},{13,5},{2,10},{6,14},... | collective-permute-start | bytes 786440 | tf_op jit(solution)/shard_map/ppermute | solution.py:157
  500.0 30.9 %collective-permute-start.32 = (bf16[64,2048]{1,0:T(8,128)(2,1)}, bf16[64,2048]{1,0:T(8,128)(2,1)}, u32[]{:S(2)}, u32[]{:S(2)}) collective-permute-start(bf16[64,2048]{1,0:T(8,128)(2,1)} %get-tuple-element.266), channel_id=1, source_target_pairs={{0,12},{4,0},{8,4},{12,8},{1,13},{5,1},{9,5},{13,9},{2,14},{6,2},{... | collective-permute-start | bytes 786440 | tf_op jit(solution)/shard_map/ppermute | solution.py:157
  501.2 32.3 %all-to-all-start.11 = ((bf16[4,80,2048]{2,1,0:T(8,128)(2,1)}), bf16[4,80,2048]{2,1,0:T(8,128)(2,1)}, u32[]{:S(2)}, u32[]{:S(2)}) async-start(bf16[4,80,2048]{2,1,0:T(8,128)(2,1)} %bitcast.180), calls=%async_computation.12 | async-start | bytes 2621440 | tf_op jit(solution)/shard_map/all_to_all | solution.py:81
  533.6 17.4 %all-to-all-start.10 = ((bf16[4,64,2048]{2,1,0:T(8,128)(2,1)}), bf16[4,64,2048]{2,1,0:T(8,128)(2,1)S(1)}, u32[]{:S(2)}, u32[]{:S(2)}) async-start(bf16[4,64,2048]{2,1,0:T(8,128)(2,1)} %bitcast.72), calls=%async_computation.11 | async-start | bytes 2097152 | tf_op jit(solution)/shard_map/all_to_all | solution.py:81
  (70 other events, 972.1 us)
Sparse Core Ops, SparseCore 0:
  10.2 61.6 all-gather.5
  74.1 76.6 all-gather.7
  155.7 63.3 all-gather.9
  253.4 48.6 all-gather.11
  399.0 53.5 reduce-scatter.1
  454.8 61.3 all-gather.13
